TPU v7x, 768 devices: a whole 4x8x12 slice. The times are simulated.
768 devices in a mesh: sec: 4 (over y_lo), dp: 48 (over y_hi, z, core), mp: 4 (over x).
Axes of the slice: x: 4, y: 8 (y_hi: 2, y_lo: 4; y = y_hi * 4 + y_lo), z: 12, core: 2. Of those that a mesh axis runs over, the one named last changes fastest.
Arguments:
- policy_query: bfloat16 [192, 128, 4096], P(('sec', 'dp'), None, 'mp'), may hold values from -6 to 6
- policy_memory: bfloat16 [2, 192, 128, 1024], P(None, ('sec', 'dp'), None, 'mp'), may hold values from -6 to 6
- chosen_output_rows: bfloat16 [192, 128, 4096], P(('sec', 'dp'), None, 'mp'), may hold values from -0.09375 to 0.09375
- adapter_rows: bfloat16 [192, 128, 8192], P(('sec', 'dp'), None, 'mp'), may hold values from -6 to 6
- adapter_down: bfloat16 [4096, 64], P('mp'), may hold values from -0.09375 to 0.09375
- adapter_up: bfloat16 [64, 8192], P(None, 'mp'), may hold values from -0.0078125 to 0.0078125
- scorer_query: bfloat16 [4, 4, 48, 128, 4096], P('sec', None, 'dp', None, 'mp'), may hold values from -6 to 6
- scorer_key_values: bfloat16 [4, 2, 4, 48, 128, 1024], P('sec', None, None, 'dp', None, 'mp'), may hold values from -6 to 6
- score_heads: float32 [2, 4096], P(None, 'mp'), may hold values from -0.1875 to 0.1875
- document_ids: int32 [4, 48, 128], P(None, 'dp'), may hold values from 0 to 3, never falling along the last dimension, each value on 1 to 64 neighbouring positions
- prompt_lengths: int32 [4, 48, 4], P(None, 'dp'), may hold values from 1 to 31
Outputs:
- advantages: float32 [192, 128], P(('sec', 'dp'))
- query_grad: bfloat16 [192, 128, 4096], P(('sec', 'dp'), None, 'mp')
- memory_grad: bfloat16 [2, 192, 128, 1024], P(None, ('sec', 'dp'), None, 'mp')
- down_grad: float32 [4096, 64], P('mp')
- up_grad: float32 [64, 8192], P(None, 'mp')
Inputs may be any that keep to these rules, and one draw needn't show every extreme that they name: `document_ids`: within each row the document numbers never fall; every document has 1 to 64 positions and one has exactly 64.
All inputs are finite; a program needn't handle non-finite values.
Results may differ from a plain program's by a relative error of at most 0.0081.
Values may be sent and summed in bfloat16 or wider, within the bound.
No kernel may reach another device: no remote copies, remote signals or barrier semaphores. Data moves between devices by JAX's collectives and lax.ppermute only.
A program may use at most 32 MiB of HBM per device.

v0:
```python
import jax
import jax.numpy as jnp
from jax import lax
from jax.sharding import PartitionSpec as P

HEAD_DIM = 128


kl_weight = 0.1
trace_decay = 0.95
epsilon = 1e-05
masked_score = -1e30


def span_masks(document_index, prompt):
    length = document_index.shape[-1]
    labels = jnp.arange(prompt.shape[-1], dtype=jnp.int32)
    member = (document_index[:, None] == labels[None, :]).astype(jnp.float32)
    counts = jnp.sum(member, axis=0)
    firsts = jnp.cumsum(counts) - counts
    position = jnp.arange(length).astype(jnp.float32)
    start_pos = jnp.sum(member * firsts[None, :], axis=1)
    prompt_pos = jnp.sum(member * prompt.astype(jnp.float32)[None, :], axis=1)
    ending = jnp.sum(member * (firsts + counts - 1.0)[None, :], axis=1)
    respond = (position - start_pos >= prompt_pos).astype(jnp.float32)
    closing = (position == ending).astype(jnp.float32)
    return (respond, closing)


def trace_matrix(document_index):
    length = document_index.shape[-1]
    position = jnp.arange(length, dtype=jnp.int32)
    later = position[None, :] - position[:, None]
    linked = (document_index[:, None] == document_index[None, :]) & (later >= 0)
    powers = jnp.power(jnp.float32(trace_decay), jnp.maximum(later, 0).astype(jnp.float32))
    return jnp.where(linked, powers, jnp.float32(0.0))


def attend_section(query, keys, values, document_index):
    length = query.shape[0]
    kv_heads = keys.shape[1] // HEAD_DIM
    groups = query.shape[1] // keys.shape[1]
    query_h = query.reshape(length, kv_heads, groups, HEAD_DIM)
    keys_h = keys.reshape(length, kv_heads, HEAD_DIM)
    values_h = values.reshape(length, kv_heads, HEAD_DIM)
    scores = jnp.einsum(
        "qcgd,kcd->cgqk", query_h, keys_h, preferred_element_type=jnp.float32
    ) * HEAD_DIM ** (-0.5)
    position = jnp.arange(length, dtype=jnp.int32)
    allowed = (document_index[:, None] == document_index[None, :]) & (
        position[:, None] >= position[None, :]
    )
    scores = jnp.where(allowed, scores, masked_score)
    top = jnp.max(scores, axis=-1, keepdims=True)
    raised = jnp.exp(scores - top)
    probs = raised / jnp.sum(raised, axis=-1, keepdims=True)
    probs_b = probs.astype(jnp.bfloat16)
    attended = jnp.einsum(
        "cgqk,kcd->qcgd", probs_b, values_h, preferred_element_type=jnp.float32
    ).reshape(length, -1)
    return (attended, probs, probs_b)


def attend_back(query, keys, values, probs, probs_b, grad_b):
    length = query.shape[0]
    kv_heads = keys.shape[1] // HEAD_DIM
    groups = query.shape[1] // keys.shape[1]
    query_h = query.reshape(length, kv_heads, groups, HEAD_DIM)
    keys_h = keys.reshape(length, kv_heads, HEAD_DIM)
    values_h = values.reshape(length, kv_heads, HEAD_DIM)
    grad_h = grad_b.reshape(length, kv_heads, groups, HEAD_DIM)
    dprobs = jnp.einsum("qcgd,kcd->cgqk", grad_h, values_h, preferred_element_type=jnp.float32)
    inner = jnp.sum(probs * dprobs, axis=-1, keepdims=True)
    dscores = (probs * (dprobs - inner)).astype(jnp.bfloat16)
    scale = HEAD_DIM ** (-0.5)
    query_grad = (
        (jnp.einsum("cgqk,kcd->qcgd", dscores, keys_h, preferred_element_type=jnp.float32) * scale)
        .astype(jnp.bfloat16)
        .reshape(length, -1)
    )
    keys_grad = (
        (jnp.einsum("cgqk,qcgd->kcd", dscores, query_h, preferred_element_type=jnp.float32) * scale)
        .astype(jnp.bfloat16)
        .reshape(length, -1)
    )
    values_grad = (
        jnp.einsum("cgqk,qcgd->kcd", probs_b, grad_h, preferred_element_type=jnp.float32)
        .astype(jnp.bfloat16)
        .reshape(length, -1)
    )
    return (query_grad, keys_grad, values_grad)


def on_device(
    policy_query,
    policy_memory,
    chosen_output_rows,
    adapter_rows,
    adapter_down,
    adapter_up,
    scorer_query,
    scorer_key_values,
    score_heads,
    document_ids,
    prompt_lengths,
):
    highest = lax.Precision.HIGHEST
    section_index = lax.axis_index("sec")
    docs_all = document_ids[:, 0, :]
    prompts_all = prompt_lengths[:, 0, :]
    own_doc = lax.dynamic_index_in_dim(docs_all, section_index, 0, keepdims=False)
    own_prompt = lax.dynamic_index_in_dim(prompts_all, section_index, 0, keepdims=False)
    query = policy_query[0]
    keys = policy_memory[0, 0]
    values = policy_memory[1, 0]
    chosen_float = chosen_output_rows[0].astype(jnp.float32)
    down_float = adapter_down.astype(jnp.float32)
    rows_all = lax.all_gather(chosen_output_rows, "sec", axis=0, tiled=True)
    head_pick = lax.dynamic_index_in_dim(
        score_heads, jnp.maximum(section_index - 2, 0), 0, keepdims=False
    )

    def score_row_values(item_list):
        scorer_query_rows, scorer_keys, scorer_values, document_index, chosen_token = item_list
        scorer_attended, scorer_probs, scorer_probs_batch = attend_section(
            scorer_query_rows, scorer_keys, scorer_values, document_index
        )
        by_rows = jnp.sum(scorer_attended * chosen_token.astype(jnp.float32), axis=1)
        by_head = jnp.dot(scorer_attended, head_pick, precision=highest)
        return jnp.where(section_index < 2, by_rows, by_head)

    partials = lax.map(
        score_row_values,
        (
            scorer_query[0, :, 0],
            scorer_key_values[0, 0, :, 0],
            scorer_key_values[0, 1, :, 0],
            docs_all,
            rows_all,
        ),
    )
    attended, probs, probs_b = attend_section(query, keys, values, own_doc)
    base_part = jnp.sum(attended * chosen_float, axis=1)
    in_part = jnp.dot(attended, down_float, precision=highest)
    out_part = jnp.einsum(
        "ld,rd->lr", adapter_rows[0], adapter_up, preferred_element_type=jnp.float32
    )
    raw_scores = lax.all_to_all(partials, "sec", split_axis=0, concat_axis=0, tiled=True)
    scores, base, lowrank_in, lowrank_out = lax.psum(
        (raw_scores, base_part, in_part, out_part), "mp"
    )
    policy_new = base + jnp.sum(lowrank_in * lowrank_out, axis=-1)
    policy_old = scores[0]
    policy_ref = scores[1]
    reward = scores[2]
    value = scores[3]
    respond, closing = span_masks(own_doc, own_prompt)
    next_value = jnp.concatenate([value[1:], jnp.zeros((1,), jnp.float32)]) * (1.0 - closing)
    delta = -kl_weight * (policy_old - policy_ref) + closing * reward + next_value - value
    advantage = jnp.dot(trace_matrix(own_doc), delta, precision=highest)
    count, total, square_total = lax.psum(
        (jnp.sum(respond), jnp.sum(respond * advantage), jnp.sum(respond * advantage * advantage)),
        ("sec", "dp"),
    )
    mean = total / count
    spread = square_total / count - mean * mean
    whitened = respond * (advantage - mean) * lax.rsqrt(spread + epsilon)
    ratio = jnp.exp(policy_new - policy_old)
    grad_score = -respond * ratio * whitened / count
    scaled_out = grad_score[:, None] * lowrank_out
    down_part = jnp.einsum("lh,lr->hr", attended, scaled_out, precision=highest)
    scaled_in = (grad_score[:, None] * lowrank_in).astype(jnp.bfloat16)
    up_part = jnp.einsum(
        "lr,ld->rd", scaled_in, adapter_rows[0], preferred_element_type=jnp.float32
    )
    down_grad, up_grad = lax.psum((down_part, up_part), ("sec", "dp"))
    grad_attended = (
        grad_score[:, None] * chosen_float + jnp.dot(scaled_out, down_float.T, precision=highest)
    ).astype(jnp.bfloat16)
    query_grad, keys_grad, values_grad = attend_back(
        query, keys, values, probs, probs_b, grad_attended
    )
    memory_grad = jnp.stack([keys_grad, values_grad])[:, None]
    return (whitened[None, :], query_grad[None], memory_grad, down_grad, up_grad)


def solution(mesh):
    return jax.shard_map(
        on_device,
        mesh=mesh,
        in_specs=(
            P(("sec", "dp"), None, "mp"),
            P(None, ("sec", "dp"), None, "mp"),
            P(("sec", "dp"), None, "mp"),
            P(("sec", "dp"), None, "mp"),
            P("mp", None),
            P(None, "mp"),
            P("sec", None, "dp", None, "mp"),
            P("sec", None, None, "dp", None, "mp"),
            P(None, "mp"),
            P(None, "dp", None),
            P(None, "dp", None),
        ),
        out_specs=(
            P(("sec", "dp"), None),
            P(("sec", "dp"), None, "mp"),
            P(None, ("sec", "dp"), None, "mp"),
            P("mp", None),
            P(None, "mp"),
        ),
        check_vma=False,
    )
```

profile of v0, /device:TPU:1, one launch (start us, length us, event | category | flops | bytes accessed | tf_op | source)
XLA Modules:
  0.0 965.1 jit_solution(1809258322218071161)
XLA Ops:
  7.2 0.7 all-gather.2.cloned.1.call-update
  7.9 1.1 fusion.76
  9.1 0.8 fusion.49
  10.0 0.9 copy.93
  11.1 0.8 copy.126
  11.9 0.7 copy.86
  12.6 0.7 copy.91
  13.9 0.3 copy-done.24
  14.3 0.5 add_add_fusion
  14.9 1.2 fusion.78
  16.1 2.1 fusion.28
  18.2 0.9 fusion.79
  19.4 0.9 fusion.26
  20.3 35.8 %all-gather.2.cloned.1.call-done = bf16[4,128,1024]{2,1,0:T(8,128)(2,1)} async-done(((bf16[1,128,1024]{2,1,0:T(8,128)(2,1)}), bf16[4,128,1024]{2,1,0:T(8,128)(2,1)}) %all-gather.2.cloned.1.call-update) | async-done | bytes 1048592 | tf_op jit(solution)/shard_map/all_gather | solution.py:118
  56.1 22.3 %while.12 = (s32[]{:T(128)}, f32[4,128]{1,0:T(4,128)}, pred[]{:T(512)}, bf16[4,128,256]{1,2,0:T(8,128)(2,1)S(1)}, s32[4,128]{1,0:T(4,128)}, /*index=5*/bf16[4,12...) while((s32[]{:T(128)}, f32[4,128]{1,0:T(4,128)}, ...), condition=%wide.region_8.9_spmd, body=%wide.region_4.8_spmd.sunk | while | flops 103859456 | bytes 7078082 | solution.py:132
  56.1 1.1 constant_dynamic-slice_fusion.11
  57.3 0.9 constant_dynamic-slice_fusion.12
  58.2 0.7 fusion.129
  59.0 0.4 fusion.131
  59.7 0.3 fusion.133
  60.0 0.4 fusion.134
  60.4 1.3 dynamic_update_slice.7
  61.6 1.1 constant_dynamic-slice_fusion.11
  62.9 0.9 constant_dynamic-slice_fusion.12
  63.8 0.7 fusion.129
  64.6 0.4 fusion.131
  65.2 0.3 fusion.133
  65.6 0.4 fusion.134
  65.9 1.3 dynamic_update_slice.7
  67.2 1.1 constant_dynamic-slice_fusion.11
  68.5 0.9 constant_dynamic-slice_fusion.12
  69.4 0.7 fusion.129
  70.2 0.4 fusion.131
  70.8 0.3 fusion.133
  71.1 0.4 fusion.134
  71.5 1.3 dynamic_update_slice.7
  72.8 1.1 constant_dynamic-slice_fusion.11
  74.1 0.9 constant_dynamic-slice_fusion.12
  75.0 0.7 fusion.129
  75.7 0.4 fusion.131
  76.7 0.4 fusion.134
  77.1 1.3 dynamic_update_slice.7
  78.4 3.2 all-to-all-start
  81.7 0.7 fusion.51
  82.3 3.7 all-to-all-done
  86.0 0.6 copy-done.23
  86.8 56.7 %all-reduce.8.cloned.1.call-done = (f32[4,128]{1,0:T(4,128)}, f32[128]{0:T(128)}, f32[128,64]{0,1:T(8,128)}, f32[128,64]{0,1:T(8,128)}) async-done(((f32[4,128]{1,0:T(4,128)}, f32[128]{0:T(128)}, f32[128,64]{0,1:T(8,128)}, f32[128,64]{0,1:T(8,128)}), (f32[4,128]{1,0:T(4,128)}, f32[128]{0:T(128)}, f32[128,64]{0,1:T(8,128)}, f32[128,64]{0,1:T(8,128)})) %all-reduce.8.cloned.1.call-update) | async-done | bytes 68112 | tf_op jit(solution)/shard_map/psum | solution.py:149
  143.5 0.7 slice_bitcast_fusion
  144.2 1.7 select_reduce_fusion.3
  145.9 424.0 %all-reduce = (f32[]{:T(128)}, f32[]{:T(128)}, f32[]{:T(128)}) all-reduce(f32[]{:T(128)} %get-tuple-element.150, f32[]{:T(128)} %get-tuple-element.151, f32[]{:T(128)} %get-tuple-element.149), channel_id=1, replica_groups=mesh['sec'=4,'dp'=48,'mp'=4] {'sec','dp'}, use_global_device_ids=true, to_apply=%region_16.17 | all-reduce | flops 3 | bytes 24 | tf_op jit(solution)/shard_map/psum | solution.py:161
  572.6 0.8 multiply_reduce_fusion.1
  573.4 1.9 fusion.60
  575.3 1.2 fusion.19
  576.6 1.4 fusion.42
  578.0 1.0 fusion.24
  579.2 0.9 copy-done.10
  580.4 0.7 copy-done.17
  581.4 0.9 copy-done.8
  582.4 1.2 fusion.23
  583.6 0.9 copy.103
  584.9 0.7 maximum_bitcast_fusion
  585.6 370.5 %all-reduce.6.cloned.1.call-done = (f32[1024,64]{0,1:T(8,128)}, f32[64,2048]{1,0:T(8,128)}) async-done(((f32[1024,64]{0,1:T(8,128)}, f32[64,2048]{1,0:T(8,128)}), (f32[1024,64]{0,1:T(8,128)}, f32[64,2048]{1,0:T(8,128)})) %all-reduce.6.cloned.1.call-update) | async-done | bytes 786448 | tf_op jit(solution)/shard_map/psum | solution.py:176
  956.0 1.7 copy.145
  957.8 0.8 copy.146
  (98 shorter events, 5.3 us)
Async XLA Ops:
  7.2 12.0 %copy-start = (bf16[1,128,2048]{2,1,0:T(8,128)(2,1)S(1)}, bf16[1,128,2048]{2,1,0:T(8,128)(2,1)}, u32[]{:S(2)}) copy-start(bf16[1,128,2048]{2,1,0:T(8,128)(2,1)} %param.16) | copy-start | bytes 1572868
  7.2 48.9 %all-gather.2.cloned.1.call-start = ((), (), s32[]{:S(2)}) async-start(), calls=%async_computation.1 | async-start | bytes 1310720 | tf_op jit(solution)/shard_map/all_gather | solution.py:118
  7.9 1.1 copy-start.20
  9.0 1.0 copy-start.1
  9.1 2.9 copy-start.6
  12.6 1.0 copy-start.18
  13.6 1.4 copy-start.16
  13.6 0.7 copy-start.24
  13.7 2.4 copy-start.7
  14.9 1.2 copy-start.22
  14.9 1.2 copy-start.9
  16.1 2.1 copy-start.12
  18.2 2.1 copy-start.2
  18.2 1.1 copy-start.15
  56.1 30.6 %copy-start.25 = (f32[4]{0:T(128)S(1)}, f32[4]{0:T(128)}, u32[]{:S(2)}) copy-start(f32[4]{0:T(128)} %get-tuple-element.194) | copy-start | bytes 52
  56.1 1.2 copy-start.4
  60.0 1.7 copy-start.5
  61.6 1.3 copy-start.4
  65.6 1.7 copy-start.5
  67.2 1.3 copy-start.4
  71.1 1.7 copy-start.5
  72.8 1.3 copy-start.4
  76.7 1.7 copy-start.5
  78.4 7.6 all-to-all-start
  81.6 61.8 %all-reduce.8.cloned.1.call-start = ((), (), s32[]{:S(2)}) async-start(), calls=%async_computation.3 | async-start | bytes 136192 | tf_op jit(solution)/shard_map/psum | solution.py:149
  86.0 0.6 copy-start.23
  86.6 488.7 %copy-start.13 = (bf16[1024,64]{0,1:T(8,128)(2,1)S(1)}, bf16[1024,64]{0,1:T(8,128)(2,1)}, u32[]{:S(2)}) copy-start(bf16[1024,64]{0,1:T(8,128)(2,1)} %param.17) | copy-start | bytes 393220
  86.6 490.0 %copy-start.3 = (f32[2,4,128,128]{2,3,1,0:T(8,128)S(1)}, f32[2,4,128,128]{2,3,1,0:T(8,128)}, u32[]{:S(2)}) copy-start(f32[2,4,128,128]{2,3,1,0:T(8,128)} %copy-done.2) | copy-start | bytes 1572868
  86.6 869.4 %all-reduce.6.cloned.1.call-start = ((), (), s32[]{:S(2)}) async-start(), calls=%async_computation.2 | async-start | bytes 1572864 | tf_op jit(solution)/shard_map/psum | solution.py:176
  575.3 1.3 copy-start.14
  576.6 1.4 copy-start.19
  578.0 1.2 copy-start.21
  579.0 1.0 copy-start.10
  580.3 0.8 copy-start.17
  581.4 1.0 copy-start.8
  956.0 1.7 copy-start.11
Sparse Core Ops, SparseCore 0:
  10.4 45.6 all-gather.1
  86.7 56.6 all-reduce.7
  581.6 374.4 all-reduce.5
where the time goes:
time: 966 us; the launch traced here: 965 us
  waiting for transfers between devices  467 us (48%)
  blocking collectives  424 us (44%)
  local copies, waits for them, and re-layouts  30.2 us (3%)
  matrix products  17.8 us (2%)
  between operations  16.8 us (2%)
    psum x1, blocking collectives, on_device(): lax.psum((jnp.sum(respond), jnp.sum(respond * advantage), jnp.sum(respond...  424 us
    psum x1, waiting for transfers between devices, on_device(): down_grad, up_grad = lax.psum((down_part, up_part), ('sec', 'dp'))  370 us
    psum x1, waiting for transfers between devices, on_device(): lax.psum((raw_scores, base_part, in_part, out_part), 'mp')  56.7 us
    all_gather x1, waiting for transfers between devices, on_device(): rows_all = lax.all_gather(chosen_output_rows, 'sec', axis=0, tiled=True)  35.8 us
  transfers between devices with their start and end apart: 4, of which 4 were waited for; matrix products, arithmetic and copies ran while one was open for 2% of the time, Pallas kernels for 0%

commit v1 on v0

v1 whole, which is shorter than its diff:
```python
import functools
import jax
import jax.numpy as jnp
import numpy as np
from jax import lax
from jax.experimental import pallas as pl
from jax.experimental.pallas import tpu as pltpu
from jax.sharding import Mesh, PartitionSpec as P

HEAD = 128
KL = 0.1
DECAY = 0.95
EPS = 1e-05
MASKED = -1e30
F32 = jnp.float32
BF16 = jnp.bfloat16
NT = (((1,), (1,)), ((), ()))
NN = (((1,), (0,)), ((), ()))
TN = (((0,), (0,)), ((), ()))


def dot(a, b, dims):
    return lax.dot_general(a, b, dims, preferred_element_type=F32)


def halves(x):
    high = x.astype(BF16)
    return high, (x - high.astype(F32)).astype(BF16)


def as_column(row):
    n = row.shape[1]
    return jnp.broadcast_to(row, (n, n)).T


def square(row):
    n = row.shape[1]
    return jnp.broadcast_to(row, (n, n))


def allowed_of(doc_row):
    n = doc_row.shape[1]
    doc = doc_row.astype(F32)
    rows = lax.broadcasted_iota(jnp.int32, (n, n), 0)
    lanes = lax.broadcasted_iota(jnp.int32, (n, n), 1)
    return (as_column(doc) == square(doc)) & (rows >= lanes)


def probs_of(query, keys, allowed):
    scores = dot(query, keys, NT) * HEAD ** (-0.5)
    scores = jnp.where(allowed, scores, MASKED)
    top = jnp.max(scores, axis=1, keepdims=True)
    raised = jnp.exp(scores - top)
    return raised / jnp.sum(raised, axis=1, keepdims=True)


def scorer_kernel(doc_ref, q_ref, k_ref, v_ref, out_ref):
    allowed = allowed_of(doc_ref[...])
    groups = q_ref.shape[1] // k_ref.shape[1]
    for head in range(q_ref.shape[1] // HEAD):
        at = slice(head * HEAD, (head + 1) * HEAD)
        kv = slice(head // groups * HEAD, (head // groups + 1) * HEAD)
        probs = probs_of(q_ref[:, at], k_ref[:, kv], allowed).astype(BF16)
        out_ref[:, at] = dot(probs, v_ref[:, kv], NN)


def score_kernel(sec_ref, att_ref, rows_ref, heads_ref, out_ref):
    n_heads = att_ref.shape[2] // HEAD
    by_rows = sec_ref[0] < 2
    first_head = sec_ref[0] == 2

    def put(weight):
        for row in range(att_ref.shape[0]):
            total = None
            for head in range(n_heads):
                at = slice(head * HEAD, (head + 1) * HEAD)
                term = att_ref[row, :, at] * weight(row, at)
                total = term if total is None else total + term
            out_ref[row:row + 1, :] = jnp.sum(total.T, axis=0, keepdims=True)

    @pl.when(by_rows)
    def _():
        put(lambda row, at: rows_ref[row, :, at].astype(F32))

    @pl.when(jnp.logical_not(by_rows))
    def _():
        put(lambda row, at: jnp.where(first_head, heads_ref[0:1, at], heads_ref[1:2, at]))


def policy_kernel(sec_ref, doc_ref, q_ref, k_ref, v_ref, rows_ref, adapter_ref, down_ref, up_ref,
                  att_ref, probs_ref, part_ref):
    allowed = allowed_of(doc_ref[sec_ref[0]])
    groups = q_ref.shape[1] // k_ref.shape[1]
    base = None
    low_in = None
    for head in range(q_ref.shape[1] // HEAD):
        at = slice(head * HEAD, (head + 1) * HEAD)
        kv = slice(head // groups * HEAD, (head // groups + 1) * HEAD)
        probs = probs_of(q_ref[:, at], k_ref[:, kv], allowed)
        probs_ref[head] = probs
        attended = dot(probs.astype(BF16), v_ref[:, kv], NN)
        att_ref[:, at] = attended
        term = attended * rows_ref[:, at].astype(F32)
        base = term if base is None else base + term
        high, low = halves(attended)
        down = down_ref[:, at]
        term = dot(down, high, NT) + dot(down, low, NT)
        low_in = term if low_in is None else low_in + term
    rank = down_ref.shape[0]
    part_ref[0:rank, :] = low_in
    part_ref[rank:2 * rank, :] = dot(up_ref[...], adapter_ref[...], NT)
    base_row = jnp.sum(base.T, axis=0, keepdims=True)
    part_ref[2 * rank:, :] = jnp.broadcast_to(base_row, (8, base_row.shape[1]))


def delta_kernel(sec_ref, prompt_ref, doc_ref, part_ref, keep_ref, sums_ref):
    sec = sec_ref[0]
    doc = doc_ref[sec].astype(F32)
    n = doc.shape[1]
    doc_col, doc_row = as_column(doc), square(doc)
    rows = lax.broadcasted_iota(jnp.int32, (n, n), 0)
    lanes = lax.broadcasted_iota(jnp.int32, (n, n), 1)
    position = lax.broadcasted_iota(jnp.int32, (1, n), 1).astype(F32)
    start = jnp.sum(jnp.where(doc_col < doc_row, 1.0, 0.0), axis=0, keepdims=True)
    ending = jnp.sum(jnp.where(doc_col <= doc_row, 1.0, 0.0), axis=0, keepdims=True) - 1.0
    prompt = jnp.zeros((1, n), F32)
    for label in range(prompt_ref.shape[1]):
        length = prompt_ref[sec, label].astype(F32)
        prompt = jnp.where(doc == float(label), length, prompt)
    respond = jnp.where(position - start >= prompt, 1.0, 0.0)
    closing = jnp.where(position == ending, 1.0, 0.0)

    def section(index):
        return jnp.sum(part_ref[index], axis=0, keepdims=True)

    old, ref, reward, value = section(0), section(1), section(2), section(3)
    next_value = jnp.where(position < n - 1.0, pltpu.roll(value, n - 1, 1), 0.0) * (1.0 - closing)
    delta = -KL * (old - ref) + closing * reward + next_value - value
    later = rows - lanes
    linked = (doc_col == doc_row) & (later >= 0)
    powers = jnp.exp(jnp.maximum(later, 0).astype(F32) * float(np.log(DECAY)))
    terms = jnp.where(linked, powers, 0.0) * as_column(delta)
    advantage = jnp.sum(terms, axis=0, keepdims=True)
    keep_ref[0:1, :] = respond
    keep_ref[1:2, :] = advantage
    keep_ref[2:3, :] = old
    keep_ref[3:8, :] = jnp.zeros((5, n), F32)
    lane = lax.broadcasted_iota(jnp.int32, (1, n), 1)
    count = jnp.sum(respond, axis=1, keepdims=True)
    total = jnp.sum(respond * advantage, axis=1, keepdims=True)
    squares = jnp.sum(respond * advantage * advantage, axis=1, keepdims=True)
    packed = jnp.where(lane == 0, count, jnp.where(lane == 1, total, jnp.where(lane == 2, squares, 0.0)))
    sums_ref[...] = jnp.broadcast_to(packed, sums_ref.shape)


def weights_kernel(moments_ref, keep_ref, part_ref, att_ref, adapter_ref,
                   white_ref, grad_ref, out_ref, down_ref, up_ref):
    rank = (part_ref.shape[1] - 8) // 2
    moments = jnp.sum(moments_ref[...], axis=0, keepdims=True)
    lane = lax.broadcasted_iota(jnp.int32, moments.shape, 1)

    def pick(index):
        return jnp.sum(jnp.where(lane == index, moments, 0.0), axis=1, keepdims=True)

    count, total, squares = pick(0), pick(1), pick(2)
    mean = total / count
    spread = squares / count - mean * mean
    respond, advantage, old = keep_ref[0:1, :], keep_ref[1:2, :], keep_ref[2:3, :]
    whitened = respond * (advantage - mean) * lax.rsqrt(spread + EPS)
    white_ref[...] = whitened
    part = part_ref[0].astype(F32)
    for index in range(1, part_ref.shape[0]):
        part = part + part_ref[index].astype(F32)
    low_in, low_out, base = part[0:rank], part[rank:2 * rank], part[2 * rank:2 * rank + 1]
    policy_new = base + jnp.sum(low_in * low_out, axis=0, keepdims=True)
    grad_score = -respond * jnp.exp(policy_new - old) * whitened / count
    grad_ref[...] = grad_score
    scaled_out = grad_score * low_out
    out_ref[...] = scaled_out
    high, low = halves(scaled_out)
    att_high, att_low = halves(att_ref[...])
    down_ref[...] = dot(high, att_high, NN) + (dot(low, att_high, NN) + dot(high, att_low, NN))
    up_ref[...] = dot((grad_score * low_in).astype(BF16), adapter_ref[...], NN)


def backward_kernel(grad_ref, out_ref, down_ref, rows_ref, probs_ref, q_ref, k_ref, v_ref,
                    query_ref, keys_ref, values_ref):
    grad_col = as_column(grad_ref[...])
    high, low = halves(out_ref[...])
    groups = q_ref.shape[1] // k_ref.shape[1]
    scale = HEAD ** (-0.5)
    for group in range(k_ref.shape[1] // HEAD):
        kv = slice(group * HEAD, (group + 1) * HEAD)
        keys, values = k_ref[:, kv], v_ref[:, kv]
        keys_grad, values_grad = None, None
        for head in range(group * groups, (group + 1) * groups):
            at = slice(head * HEAD, (head + 1) * HEAD)
            down = down_ref[:, at]
            grad = grad_col * rows_ref[:, at].astype(F32) + (dot(high, down, TN) + dot(low, down, TN))
            grad = grad.astype(BF16)
            probs = probs_ref[head]
            dprobs = dot(grad, values, NT)
            inner = jnp.sum(probs * dprobs, axis=1, keepdims=True)
            dscores = (probs * (dprobs - inner)).astype(BF16)
            query_ref[:, at] = (dot(dscores, keys, NN) * scale).astype(BF16)
            term = dot(dscores, q_ref[:, at], TN)
            keys_grad = term if keys_grad is None else keys_grad + term
            term = dot(probs.astype(BF16), grad, TN)
            values_grad = term if values_grad is None else values_grad + term
        keys_ref[:, kv] = (keys_grad * scale).astype(BF16)
        values_ref[:, kv] = values_grad.astype(BF16)


def gather_moments(sums, n_sec, sizes):
    n_yh, n_z, n_core = sizes
    first = share(sums[0:1], ("z", "core"), n_z * n_core).sum(axis=0)
    return share(first, ("sec", "yh"), n_sec * n_yh).reshape(-1, sums.shape[1])


def reduce_grads(down_part, up_part, n_sec, sizes):
    n_yh, n_z, n_core = sizes
    n_y = n_sec * n_yh
    tokens = 128
    flat = jnp.concatenate([down_part.reshape(-1, tokens), up_part.reshape(-1, tokens)], axis=0)
    total = flat.shape[0]
    x = flat.reshape(n_core, total // n_core, tokens)
    x = reduce_part(x, "core", n_core)
    x = reduce_part(x.reshape(n_z, -1, tokens), "z", n_z)
    x = reduce_part(x.reshape(n_y, -1, tokens), ("sec", "yh"), n_y)
    x = share(x, ("sec", "yh"), n_y).reshape(-1, tokens)
    x = share(x, "z", n_z).reshape(-1, tokens)
    x = share(x, "core", n_core).reshape(total, tokens)
    cut = down_part.size // tokens
    return x[:cut].reshape(down_part.shape), x[cut:].reshape(up_part.shape)


def whole(shape, space=pltpu.VMEM):
    return pl.BlockSpec(memory_space=space)


def call(kernel, outs, args, smem=(), **params):
    specs = [pl.BlockSpec(memory_space=pltpu.SMEM if i in smem else pltpu.VMEM) for i in range(len(args))]
    return pl.pallas_call(
        kernel,
        out_shape=outs,
        in_specs=specs,
        out_specs=jax.tree.map(lambda _: pl.BlockSpec(memory_space=pltpu.VMEM), outs),
        interpret=INTERPRET,
        **params,
    )(*args)


def sds(shape, dtype=F32):
    return jax.ShapeDtypeStruct(shape, dtype)


INTERPRET = False
SPLIT = (2, 12, 2)
AXES = ("sec", "yh", "z", "core", "mp")
DP = ("yh", "z", "core")


def share(x, axes, n):
    return lax.all_to_all(jnp.broadcast_to(x[None], (n,) + x.shape), axes, 0, 0, tiled=True)


def reduce_part(x, axes, n):
    got = lax.all_to_all(x, axes, 0, 0, tiled=True)
    return jnp.sum(got, axis=0)


def on_device(policy_query, policy_memory, chosen, adapter_rows, adapter_down, adapter_up,
              scorer_query, scorer_key_values, score_heads, document_ids, prompt_lengths):
    sec = lax.axis_index("sec").astype(jnp.int32).reshape(1)
    n_sec, n_mp = lax.axis_size("sec"), lax.axis_size("mp")
    sizes = [lax.axis_size(a) for a in DP]
    query, keys, values = policy_query[0], policy_memory[0, 0], policy_memory[1, 0]
    rows = chosen[0]
    tokens, features = query.shape
    kv_features = keys.shape[1]
    adapter = adapter_rows[0]
    down = adapter_down.T
    rank = down.shape[0]
    width = adapter.shape[1]
    heads = features // HEAD
    prompts = prompt_lengths[:, 0]

    rows_all = lax.all_gather(rows, "sec", axis=0, tiled=False)
    scorer_att = pl.pallas_call(
        scorer_kernel,
        grid=(n_sec,),
        out_shape=sds((n_sec, tokens, features)),
        in_specs=[
            pl.BlockSpec((None, 1, tokens), lambda j: (j, 0, 0)),
            pl.BlockSpec((None, None, None, tokens, features), lambda j: (0, j, 0, 0, 0)),
            pl.BlockSpec((None, None, None, None, tokens, kv_features), lambda j: (0, 0, j, 0, 0, 0)),
            pl.BlockSpec((None, None, None, None, tokens, kv_features), lambda j: (0, 1, j, 0, 0, 0)),
        ],
        out_specs=pl.BlockSpec((None, tokens, features), lambda j: (j, 0, 0)),
        interpret=INTERPRET,
        cost_estimate=pl.CostEstimate(flops=300_000_000, bytes_accessed=5_000_000, transcendentals=600_000),
    )(document_ids, scorer_query, scorer_key_values, scorer_key_values)
    attended, probs, part = call(
        policy_kernel,
        (sds((tokens, features)), sds((heads, tokens, tokens)), sds((2 * rank + 8, tokens))),
        (sec, document_ids, query, keys, values, rows, adapter, down, adapter_up),
        smem=(0,),
        cost_estimate=pl.CostEstimate(flops=150_000_000, bytes_accessed=3_000_000, transcendentals=150_000),
    )
    parts = share(part, "mp", n_mp)
    partials = call(score_kernel, sds((n_sec, tokens)), (sec, scorer_att, rows_all, score_heads), smem=(0,),
                    cost_estimate=pl.CostEstimate(flops=2_000_000, bytes_accessed=3_000_000, transcendentals=0))
    sent = jnp.broadcast_to(partials[:, None], (n_sec, n_mp, tokens)).reshape(n_sec * n_mp, 1, tokens)
    got = lax.all_to_all(sent, ("sec", "mp"), 0, 0, tiled=True).reshape(n_sec, n_mp, tokens)
    keep, sums = call(delta_kernel, (sds((8, tokens)), sds((8, tokens))),
                      (sec, prompts, document_ids, got), smem=(0, 1))
    moments = gather_moments(sums, n_sec, sizes)
    white, grad_score, scaled_out, down_part, up_part = call(
        weights_kernel,
        (sds((1, tokens)), sds((1, tokens)), sds((rank, tokens)), sds((rank, features)), sds((rank, width))),
        (moments, keep, parts, attended, adapter),
    )
    down_grad, up_grad = reduce_grads(down_part, up_part, n_sec, sizes)
    query_grad, keys_grad, values_grad = call(
        backward_kernel,
        (sds((tokens, features), BF16), sds((tokens, kv_features), BF16), sds((tokens, kv_features), BF16)),
        (grad_score, scaled_out, down, rows, probs, query, keys, values),
        cost_estimate=pl.CostEstimate(flops=300_000_000, bytes_accessed=4_000_000, transcendentals=0),
    )
    memory_grad = jnp.stack([keys_grad, values_grad])[:, None]
    return white, query_grad[None], memory_grad, down_grad.T, up_grad


def solution(mesh):
    devices = mesh.devices
    split = SPLIT if int(np.prod(SPLIT)) == devices.shape[1] else (1, devices.shape[1], 1)
    inner = Mesh(devices.reshape((devices.shape[0],) + split + (devices.shape[2],)), AXES)
    both = ("sec",) + DP
    return jax.shard_map(
        on_device,
        mesh=inner,
        in_specs=(
            P(both, None, "mp"),
            P(None, both, None, "mp"),
            P(both, None, "mp"),
            P(both, None, "mp"),
            P("mp", None),
            P(None, "mp"),
            P("sec", None, DP, None, "mp"),
            P("sec", None, None, DP, None, "mp"),
            P(None, "mp"),
            P(None, DP, None),
            P(None, DP, None),
        ),
        out_specs=(
            P(both, None),
            P(both, None, "mp"),
            P(None, both, None, "mp"),
            P("mp", None),
            P(None, "mp"),
        ),
        check_vma=False,
    )
```

time: 966 us -> 212 us (0.22)
  waiting for transfers between devices: 467 us -> 55.7 us
  blocking collectives: 424 us -> 81 us
  Pallas kernels: 0 us -> 28.8 us
  local copies, waits for them, and re-layouts: 30.2 us -> 8.9 us
  matrix products: 17.8 us -> 0 us
  starting transfers between devices: 3.35 us -> 21 us
    psum x2 -> x0, waiting for transfers between devices: 427 us -> none  [the longest x1 370 us: on_device(): down_grad, up_grad = lax.psum((down_part, up_part), ('sec', 'dp'))]
    psum x1 -> x0, blocking collectives: 424 us -> none  [on_device(): lax.psum((jnp.sum(respond), jnp.sum(respond * advantage), jnp.sum(respond...]
    all_to_all x0 -> x7, blocking collectives: none -> 81 us  [the longest x3 39.1 us: reduce_part(): got = lax.all_to_all(x, axes, 0, 0, tiled=True)]
    pallas_call x0 -> x6, Pallas kernels: none -> 28.8 us  [the longest x5 16.2 us: call(): pl.pallas_call(kernel, out_shape=outs, in_specs=specs, out_specs=jax.tree...]
    all_to_all x1 -> x3, starting transfers between devices: 3.23 us -> 20.9 us  [share(): lax.all_to_all(jnp.broadcast_to(x[None], (n,) + x.shape), axes, 0, 0, til...]
    all_to_all x1 -> x3, waiting for transfers between devices: 3.68 us -> 19.5 us  [share(): lax.all_to_all(jnp.broadcast_to(x[None], (n,) + x.shape), axes, 0, 0, til...]
    dot_general x23 -> x0, matrix products: 15.1 us -> none  [the longest x5 3.37 us: attend_section(): jnp.einsum('cgqk,kcd->qcgd', probs_b, values_h, preferred_element_type=jn...]
  transfers between devices with their start and end apart: 4 -> 4, of which waited for: 4 -> 4; matrix products, arithmetic and copies ran while one was open for 2% -> 1% of each run, Pallas kernels for 0% -> 10%
where the time goes in v1:
time: 212 us; the launch traced here: 211 us
  blocking collectives  81 us (38%)
  waiting for transfers between devices  55.7 us (26%)
  Pallas kernels  28.8 us (14%)
  starting transfers between devices  21 us (10%)
  between operations  14.1 us (7%)
  local copies, waits for them, and re-layouts  8.9 us (4%)
    all_to_all x3, blocking collectives, reduce_part(): got = lax.all_to_all(x, axes, 0, 0, tiled=True)  39.1 us
    all_gather x1, waiting for transfers between devices, on_device(): rows_all = lax.all_gather(rows, 'sec', axis=0, tiled=False)  35.6 us
    all_to_all x3, blocking collectives, share(): lax.all_to_all(jnp.broadcast_to(x[None], (n,) + x.shape), axes, 0, 0, til...  30.5 us
    all_to_all x3, starting transfers between devices, share(): lax.all_to_all(jnp.broadcast_to(x[None], (n,) + x.shape), axes, 0, 0, til...  20.9 us
    all_to_all x3, waiting for transfers between devices, share(): lax.all_to_all(jnp.broadcast_to(x[None], (n,) + x.shape), axes, 0, 0, til...  19.5 us
    pallas_call x5, Pallas kernels, call(): pl.pallas_call(kernel, out_shape=outs, in_specs=specs, out_specs=jax.tree...  16.2 us
    pallas_call x1, Pallas kernels, on_device(): pl.pallas_call(scorer_kernel, grid=(n_sec,), out_shape=sds((n_sec, tokens...  12.6 us
    all_to_all x1, blocking collectives, on_device(): lax.all_to_all(sent, ('sec', 'mp'), 0, 0, tiled=True)  11.4 us
  transfers between devices with their start and end apart: 4, of which 4 were waited for; matrix products, arithmetic and copies ran while one was open for 1% of the time, Pallas kernels for 10%

profile of v1, /device:TPU:1, one launch (start us, length us, event | category | flops | bytes accessed | tf_op | source)
XLA Modules:
  0.0 211.1 jit_solution(8105090599300527110)
XLA Ops:
  7.2 0.0 all-gather.2.cloned.1.call-start
  7.2 0.7 all-gather.2.cloned.1.call-update
  7.9 12.6 %shard_map.146.att_ref = f32[4,128,1024]{2,1,0:T(8,128)} custom-call(s32[4,1,128]{2,1,0:T(1,128)} %doc_ref.5, bf16[1,4,1,128,1024]{4,3,2,1,0:T(8,128)(2,1)} %q_ref.1, bf16[1,2,4,1,128,256]{5,4,3,2,1,0:T(8,128)(2,1)} %v_ref.1, bf16[1,2,4,1,128,256]{5,4,3,2,1,0:T(8,128)(2,1)} %v_ref.1), custom_call_target="tpu_custom_call" | custom-call | flops 300000000 | bytes 5000000 | tf_op jit(solution)/shard_map/pallas_call | solution.py:289
  20.5 0.0 copy-start.1
  20.5 35.6 %all-gather.2.cloned.1.call-done.rows_ref = bf16[4,128,1024]{2,1,0:T(8,128)(2,1)} async-done(((bf16[1,128,1024]{2,1,0:T(8,128)(2,1)}), bf16[4,128,1024]{2,1,0:T(8,128)(2,1)}) %all-gather.2.cloned.1.call-update) | async-done | bytes 1048592 | tf_op jit(solution)/shard_map/all_gather | solution.py:288
  56.1 2.8 %shard_map.147 = f32[4,128]{1,0:T(4,128)} custom-call(s32[1]{0:T(128)} %bitcast.sec_ref, f32[4,128,1024]{2,1,0:T(8,128)} %shard_map.146.att_ref, bf16[4,128,1024]{2,1,0:T(8,128)(2,1)} %all-gather.2.cloned.1.call-done.rows_ref, f32[2,1024]{1,0:T(2,128)} %heads_ref.1), custom_call_target="tpu_custom_call" | custom-call | flops 2000000 | bytes 3000000 | tf_op jit(solution)/shard_map/pallas_call | solution.py:243
  58.8 0.7 broadcast_in_dim.24
  59.5 11.4 %all_to_all.50 = f32[16,1,128]{2,1,0:T(1,128)} all-to-all(f32[16,1,128]{2,1,0:T(1,128)S(1)} %bitcast.49), channel_id=1, replica_groups=mesh['sec'=4,'yh'=2,'z'=12,'core'=2,'mp'=4] {'sec','mp'}, dimensions={0} | all-to-all | bytes 16384 | tf_op jit(solution)/shard_map/all_to_all | solution.py:314
  70.9 1.6 shard_map.148
  72.5 0.7 slice_bitcast_fusion.2
  73.2 0.6 broadcast_in_dim.26
  73.8 12.6 %all-to-all-start.1 = ((f32[24,1,128]{2,1,0:T(1,128)}), f32[24,1,128]{2,1,0:T(1,128)S(1)}, u32[]{:S(2)}, u32[]{:S(2)}) async-start(f32[24,1,128]{2,1,0:T(1,128)} %broadcast_in_dim.26), calls=%async_computation.1 | async-start | bytes 24576 | tf_op jit(solution)/shard_map/all_to_all | solution.py:264
  86.5 0.0 copy-done.1
  86.5 0.7 slice_bitcast_fusion
  87.1 4.4 %shard_map.149 = (f32[128,1024]{1,0:T(8,128)}, f32[8,128,128]{2,1,0:T(8,128)}, f32[136,128]{1,0:T(8,128)}) custom-call(s32[1]{0:T(128)} %bitcast.sec_ref, s32[4,1,128]{2,1,0:T(1,128)} %doc_ref.5, bf16[128,1024]{1,0:T(8,128)(2,1)} %bitcast.39, bf16[128,256]{1,0:T(8,128)(2,1)} %get-tuple-element.52.k_ref, bf16[128,256]{1,0:T(8,128)(2,1)} %get-tuple-element.51.v_ref, ...), custom_call_target="tpu_custom_call" | custom-call | flops 150000000 | bytes 3000000 | tf_op jit(solution)/shard_map/pallas_call | solution.py:243
  91.5 4.3 %all-to-all-done.1 = f32[24,1,128]{2,1,0:T(1,128)S(1)} async-done(((f32[24,1,128]{2,1,0:T(1,128)}), f32[24,1,128]{2,1,0:T(1,128)S(1)}, u32[]{:S(2)}, u32[]{:S(2)}) %all-to-all-start.1) | async-done | bytes 12320 | tf_op jit(solution)/shard_map/all_to_all | solution.py:264
  95.8 1.6 broadcast_in_dim.56
  97.5 3.4 %all-to-all-start.3 = ((f32[4,136,128]{2,1,0:T(8,128)}), f32[4,136,128]{2,1,0:T(8,128)S(1)}, u32[]{:S(2)}, u32[]{:S(2)}) async-start(f32[4,136,128]{2,1,0:T(8,128)} %broadcast_in_dim.56), calls=%async_computation.3 | async-start | bytes 557056 | tf_op jit(solution)/shard_map/all_to_all | solution.py:264
  100.9 5.9 %all-to-all-done.3.part_ref = f32[4,136,128]{2,1,0:T(8,128)S(1)} async-done(((f32[4,136,128]{2,1,0:T(8,128)}), f32[4,136,128]{2,1,0:T(8,128)S(1)}, u32[]{:S(2)}, u32[]{:S(2)}) %all-to-all-start.3) | async-done | bytes 278560 | tf_op jit(solution)/shard_map/all_to_all | solution.py:264
  106.9 0.0 copy-start
  106.9 12.7 %all_to_all.51 = f32[8,1,128]{2,1,0:T(1,128)} all-to-all(f32[8,1,128]{2,1,0:T(1,128)S(1)} %broadcast_in_dim.27), channel_id=1, replica_groups=mesh['sec'=4,'yh'=2,'z'=12,'core'=2,'mp'=4] {'sec','yh'}, dimensions={0} | all-to-all | bytes 8192 | tf_op jit(solution)/shard_map/all_to_all | solution.py:264
  119.5 0.0 copy-done
  119.5 2.5 %shard_map.150 = (f32[1,128]{1,0:T(1,128)}, f32[1,128]{1,0:T(1,128)}, f32[64,128]{1,0:T(8,128)}, f32[64,1024]{1,0:T(8,128)}, f32[64,2048]{1,0:T(8,128)}) custom-call(f32[8,128]{1,0:T(8,128)} %bitcast.51, f32[8,128]{1,0:T(8,128)} %get-tuple-element.19.keep_ref, f32[4,136,128]{2,1,0:T(8,128)} %copy-done, f32[128,1024]{1,0:T(8,128)} %get-tuple-element.21.att_ref, ...), custom_call_target="tpu_custom_call" | custom-call | tf_op jit(solution)/shard_map/pallas_call | solution.py:243
  122.1 1.1 reshape.64
  123.2 1.0 reshape.63
  124.2 0.1 pad_maximum_fusion
  124.2 7.4 %all_to_all.52 = f32[2,768,128]{2,1,0:T(8,128)S(1)} all-to-all(f32[2,768,128]{2,1,0:T(8,128)S(1)} %bitcast.30), channel_id=1, replica_groups=mesh['sec'=4,'yh'=2,'z'=12,'core'=2,'mp'=4] {'core'}, dimensions={0} | all-to-all | bytes 1572864 | tf_op jit(solution)/shard_map/all_to_all | solution.py:268
  131.6 0.1 reduce_sum.37
  131.7 22.8 %all_to_all.53 = f32[12,64,128]{2,1,0:T(8,128)S(1)} all-to-all(f32[12,64,128]{2,1,0:T(8,128)S(1)} %bitcast.38), channel_id=1, replica_groups=mesh['sec'=4,'yh'=2,'z'=12,'core'=2,'mp'=4] {'z'}, dimensions={0} | all-to-all | bytes 786432 | tf_op jit(solution)/shard_map/all_to_all | solution.py:268
  154.5 8.9 %all_to_all.54 = f32[8,8,128]{2,1,0:T(8,128)S(1)} all-to-all(f32[8,8,128]{2,1,0:T(8,128)S(1)} %bitcast.44), channel_id=1, replica_groups=mesh['sec'=4,'yh'=2,'z'=12,'core'=2,'mp'=4] {'sec','yh'}, dimensions={0} | all-to-all | bytes 65536 | tf_op jit(solution)/shard_map/all_to_all | solution.py:268
  163.5 8.9 %all_to_all.55 = f32[8,8,128]{2,1,0:T(8,128)S(1)} all-to-all(f32[8,8,128]{2,1,0:T(8,128)S(1)} %broadcast_in_dim.59), channel_id=1, replica_groups=mesh['sec'=4,'yh'=2,'z'=12,'core'=2,'mp'=4] {'sec','yh'}, dimensions={0} | all-to-all | bytes 65536 | tf_op jit(solution)/shard_map/all_to_all | solution.py:264
  172.4 0.8 broadcast_in_dim.61
  173.2 4.8 %all-to-all-start.8 = ((f32[12,64,128]{2,1,0:T(8,128)}), f32[12,64,128]{2,1,0:T(8,128)S(1)}, u32[]{:S(2)}, u32[]{:S(2)}) async-start(f32[12,64,128]{2,1,0:T(8,128)} %broadcast_in_dim.61), calls=%async_computation.8 | async-start | bytes 786432 | tf_op jit(solution)/shard_map/all_to_all | solution.py:264
  178.0 4.9 %shard_map.151 = (bf16[128,1024]{1,0:T(8,128)(2,1)}, bf16[128,256]{1,0:T(8,128)(2,1)}, bf16[128,256]{1,0:T(8,128)(2,1)}) custom-call(f32[1,128]{1,0:T(1,128)} %get-tuple-element.23.grad_ref, f32[64,128]{1,0:T(8,128)} %get-tuple-element.24.out_ref, bf16[64,1024]{1,0:T(8,128)(2,1)} %bitcast.42, bf16[128,1024]{1,0:T(8,128)(2,1)} %bitcast.34, ...), custom_call_target="tpu_custom_call" | custom-call | flops 300000000 | bytes 4000000 | tf_op jit(solution)/shard_map/pallas_call | solution.py:243
  182.9 1.5 maximum_bitcast_fusion
  184.4 9.2 %all-to-all-done.8 = f32[12,64,128]{2,1,0:T(8,128)S(1)} async-done(((f32[12,64,128]{2,1,0:T(8,128)}), f32[12,64,128]{2,1,0:T(8,128)S(1)}, u32[]{:S(2)}, u32[]{:S(2)}) %all-to-all-start.8) | async-done | bytes 393248 | tf_op jit(solution)/shard_map/all_to_all | solution.py:264
  193.7 0.1 broadcast_in_dim.63
  193.7 8.9 %all_to_all.56 = f32[2,768,128]{2,1,0:T(8,128)S(1)} all-to-all(f32[2,768,128]{2,1,0:T(8,128)S(1)} %broadcast_in_dim.63), channel_id=1, replica_groups=mesh['sec'=4,'yh'=2,'z'=12,'core'=2,'mp'=4] {'core'}, dimensions={0} | all-to-all | bytes 1572864 | tf_op jit(solution)/shard_map/all_to_all | solution.py:264
  202.7 0.7 reshape.69
  203.4 0.9 reshape.70
  (7 shorter events, 0.1 us)
Async XLA Ops:
  7.2 48.9 %all-gather.2.cloned.1.call-start = ((), (), s32[]{:S(2)}) async-start(), calls=%async_computation.10 | async-start | bytes 1310720 | tf_op jit(solution)/shard_map/all_gather | solution.py:288
  20.5 66.0 %copy-start.1 = (bf16[2,1,128,256]{3,2,1,0:T(8,128)(2,1)S(1)}, bf16[2,1,128,256]{3,2,1,0:T(8,128)(2,1)}, u32[]{:S(2)}) copy-start(bf16[2,1,128,256]{3,2,1,0:T(8,128)(2,1)} %param.12) | copy-start | bytes 393220
  73.8 22.0 %all-to-all-start.1 = ((f32[24,1,128]{2,1,0:T(1,128)}), f32[24,1,128]{2,1,0:T(1,128)S(1)}, u32[]{:S(2)}, u32[]{:S(2)}) async-start(f32[24,1,128]{2,1,0:T(1,128)} %broadcast_in_dim.26), calls=%async_computation.1 | async-start | bytes 24576 | tf_op jit(solution)/shard_map/all_to_all | solution.py:264
  97.5 9.4 %all-to-all-start.3 = ((f32[4,136,128]{2,1,0:T(8,128)}), f32[4,136,128]{2,1,0:T(8,128)S(1)}, u32[]{:S(2)}, u32[]{:S(2)}) async-start(f32[4,136,128]{2,1,0:T(8,128)} %broadcast_in_dim.56), calls=%async_computation.3 | async-start | bytes 557056 | tf_op jit(solution)/shard_map/all_to_all | solution.py:264
  106.9 12.7 %copy-start = (f32[4,136,128]{2,1,0:T(8,128)}, f32[4,136,128]{2,1,0:T(8,128)S(1)}, u32[]{:S(2)}) copy-start(f32[4,136,128]{2,1,0:T(8,128)S(1)} %all-to-all-done.3.part_ref) | copy-start | bytes 835588
  173.2 20.5 %all-to-all-start.8 = ((f32[12,64,128]{2,1,0:T(8,128)}), f32[12,64,128]{2,1,0:T(8,128)S(1)}, u32[]{:S(2)}, u32[]{:S(2)}) async-start(f32[12,64,128]{2,1,0:T(8,128)} %broadcast_in_dim.61), calls=%async_computation.8 | async-start | bytes 786432 | tf_op jit(solution)/shard_map/all_to_all | solution.py:264
Sparse Core Ops, SparseCore 0:
  10.4 45.6 all-gather.1

commit v2 on v1

--- a/solution.py
+++ b/solution.py
@@ -1,4 +1,3 @@
-import functools
 import jax
 import jax.numpy as jnp
 import numpy as np
@@ -54,7 +53,8 @@
     return raised / jnp.sum(raised, axis=1, keepdims=True)
 
 
-def scorer_kernel(doc_ref, q_ref, k_ref, v_ref, out_ref):
+def scorer_kernel(doc_ref, q_ref, k_ref, v_ref, after_ref, out_ref):
+    del after_ref
     allowed = allowed_of(doc_ref[...])
     groups = q_ref.shape[1] // k_ref.shape[1]
     for head in range(q_ref.shape[1] // HEAD):
@@ -64,31 +64,37 @@
         out_ref[:, at] = dot(probs, v_ref[:, kv], NN)
 
 
-def score_kernel(sec_ref, att_ref, rows_ref, heads_ref, out_ref):
+def score_kernel(sec_ref, att_ref, own_ref, next_ref, after_ref, last_ref, heads_ref, out_ref):
+    sec = sec_ref[0]
+    n_sec = att_ref.shape[0]
+    copies = out_ref.shape[0] // n_sec
     n_heads = att_ref.shape[2] // HEAD
-    by_rows = sec_ref[0] < 2
-    first_head = sec_ref[0] == 2
+    held = (own_ref, next_ref, after_ref, last_ref)
 
     def put(weight):
-        for row in range(att_ref.shape[0]):
+        for step in range(n_sec):
+            row = lax.rem(sec + step, n_sec)
             total = None
             for head in range(n_heads):
                 at = slice(head * HEAD, (head + 1) * HEAD)
-                term = att_ref[row, :, at] * weight(row, at)
+                term = att_ref[row, :, at] * weight(step, at)
                 total = term if total is None else total + term
-            out_ref[row:row + 1, :] = jnp.sum(total.T, axis=0, keepdims=True)
-
-    @pl.when(by_rows)
+            score = jnp.sum(total.T, axis=0, keepdims=True)
+            for copy in range(copies):
+                out_ref[row * copies + copy] = score
+
+    @pl.when(sec < 2)
     def _():
-        put(lambda row, at: rows_ref[row, :, at].astype(F32))
-
-    @pl.when(jnp.logical_not(by_rows))
+        put(lambda step, at: held[step][:, at].astype(F32))
+
+    @pl.when(sec >= 2)
     def _():
-        put(lambda row, at: jnp.where(first_head, heads_ref[0:1, at], heads_ref[1:2, at]))
-
-
-def policy_kernel(sec_ref, doc_ref, q_ref, k_ref, v_ref, rows_ref, adapter_ref, down_ref, up_ref,
+        put(lambda step, at: jnp.where(sec == 2, heads_ref[0:1, at], heads_ref[1:2, at]))
+
+
+def policy_kernel(sec_ref, doc_ref, q_ref, memory_ref, rows_ref, adapter_ref, down_ref, up_ref,
                   att_ref, probs_ref, part_ref):
+    k_ref, v_ref = memory_ref.at[0, 0], memory_ref.at[1, 0]
     allowed = allowed_of(doc_ref[sec_ref[0]])
     groups = q_ref.shape[1] // k_ref.shape[1]
     base = None
@@ -150,12 +156,13 @@
     total = jnp.sum(respond * advantage, axis=1, keepdims=True)
     squares = jnp.sum(respond * advantage * advantage, axis=1, keepdims=True)
     packed = jnp.where(lane == 0, count, jnp.where(lane == 1, total, jnp.where(lane == 2, squares, 0.0)))
-    sums_ref[...] = jnp.broadcast_to(packed, sums_ref.shape)
-
-
-def weights_kernel(moments_ref, keep_ref, part_ref, att_ref, adapter_ref,
-                   white_ref, grad_ref, out_ref, down_ref, up_ref):
-    rank = (part_ref.shape[1] - 8) // 2
+    for copy in range(sums_ref.shape[0]):
+        sums_ref[copy] = packed
+
+
+def weights_kernel(core_ref, moments_ref, keep_ref, att_ref, adapter_ref, part0, part1, part2, part3,
+                   white_ref, grad_ref, out_ref, own_ref, send_ref, both_ref):
+    rank = (part0.shape[0] - 8) // 2
     moments = jnp.sum(moments_ref[...], axis=0, keepdims=True)
     lane = lax.broadcasted_iota(jnp.int32, moments.shape, 1)
 
@@ -168,9 +175,7 @@
     respond, advantage, old = keep_ref[0:1, :], keep_ref[1:2, :], keep_ref[2:3, :]
     whitened = respond * (advantage - mean) * lax.rsqrt(spread + EPS)
     white_ref[...] = whitened
-    part = part_ref[0].astype(F32)
-    for index in range(1, part_ref.shape[0]):
-        part = part + part_ref[index].astype(F32)
+    part = (part0[...] + part1[...]) + (part2[...] + part3[...])
     low_in, low_out, base = part[0:rank], part[rank:2 * rank], part[2 * rank:2 * rank + 1]
     policy_new = base + jnp.sum(low_in * low_out, axis=0, keepdims=True)
     grad_score = -respond * jnp.exp(policy_new - old) * whitened / count
@@ -178,13 +183,52 @@
     scaled_out = grad_score * low_out
     out_ref[...] = scaled_out
     high, low = halves(scaled_out)
-    att_high, att_low = halves(att_ref[...])
-    down_ref[...] = dot(high, att_high, NN) + (dot(low, att_high, NN) + dot(high, att_low, NN))
-    up_ref[...] = dot((grad_score * low_in).astype(BF16), adapter_ref[...], NN)
-
-
-def backward_kernel(grad_ref, out_ref, down_ref, rows_ref, probs_ref, q_ref, k_ref, v_ref,
-                    query_ref, keys_ref, values_ref):
+    scaled_in = (grad_score * low_in).astype(BF16)
+    n_down = att_ref.shape[1] // HEAD
+    for block in range(both_ref.shape[0]):
+        if block < n_down:
+            att_high, att_low = halves(att_ref[:, block * HEAD:(block + 1) * HEAD])
+            value = dot(high, att_high, NN) + (dot(low, att_high, NN) + dot(high, att_low, NN))
+        else:
+            at = (block - n_down) * HEAD
+            value = dot(scaled_in, adapter_ref[:, at:at + HEAD], NN)
+        both_ref[block] = value
+    core = core_ref[0]
+    cores = both_ref.shape[0] // own_ref.shape[0]
+    for slot in range(own_ref.shape[0]):
+        own_ref[slot] = both_ref[core * own_ref.shape[0] + slot]
+        send_ref[slot] = both_ref[(cores - 1 - core) * own_ref.shape[0] + slot]
+
+
+def spread_kernel(got_ref, out_ref):
+    total = got_ref[0].astype(F32)
+    for index in range(1, got_ref.shape[0]):
+        total = total + got_ref[index].astype(F32)
+    total = total.astype(BF16)
+    for index in range(out_ref.shape[0]):
+        out_ref[index] = total
+
+
+def place_kernel(core_ref, own_ref, other_ref, down_ref, up_ref, both_ref):
+    core = core_ref[0]
+    slots = own_ref.shape[0]
+    cores = both_ref.shape[0] // slots
+    for slot in range(slots):
+        both_ref[(cores - 1 - core) * slots + slot] = other_ref[slot]
+        both_ref[core * slots + slot] = own_ref[slot]
+    n_down = down_ref.shape[1] // HEAD
+    for block in range(both_ref.shape[0]):
+        value = both_ref[block].astype(F32)
+        if block < n_down:
+            down_ref[:, block * HEAD:(block + 1) * HEAD] = value
+        else:
+            at = (block - n_down) * HEAD
+            up_ref[:, at:at + HEAD] = value
+
+
+def backward_kernel(grad_ref, out_ref, down_ref, rows_ref, probs_ref, q_ref, memory_ref,
+                    query_ref, memory_grad_ref):
+    k_ref, v_ref = memory_ref.at[0, 0], memory_ref.at[1, 0]
     grad_col = as_column(grad_ref[...])
     high, low = halves(out_ref[...])
     groups = q_ref.shape[1] // k_ref.shape[1]
@@ -207,44 +251,18 @@
             keys_grad = term if keys_grad is None else keys_grad + term
             term = dot(probs.astype(BF16), grad, TN)
             values_grad = term if values_grad is None else values_grad + term
-        keys_ref[:, kv] = (keys_grad * scale).astype(BF16)
-        values_ref[:, kv] = values_grad.astype(BF16)
-
-
-def gather_moments(sums, n_sec, sizes):
-    n_yh, n_z, n_core = sizes
-    first = share(sums[0:1], ("z", "core"), n_z * n_core).sum(axis=0)
-    return share(first, ("sec", "yh"), n_sec * n_yh).reshape(-1, sums.shape[1])
-
-
-def reduce_grads(down_part, up_part, n_sec, sizes):
-    n_yh, n_z, n_core = sizes
-    n_y = n_sec * n_yh
-    tokens = 128
-    flat = jnp.concatenate([down_part.reshape(-1, tokens), up_part.reshape(-1, tokens)], axis=0)
-    total = flat.shape[0]
-    x = flat.reshape(n_core, total // n_core, tokens)
-    x = reduce_part(x, "core", n_core)
-    x = reduce_part(x.reshape(n_z, -1, tokens), "z", n_z)
-    x = reduce_part(x.reshape(n_y, -1, tokens), ("sec", "yh"), n_y)
-    x = share(x, ("sec", "yh"), n_y).reshape(-1, tokens)
-    x = share(x, "z", n_z).reshape(-1, tokens)
-    x = share(x, "core", n_core).reshape(total, tokens)
-    cut = down_part.size // tokens
-    return x[:cut].reshape(down_part.shape), x[cut:].reshape(up_part.shape)
-
-
-def whole(shape, space=pltpu.VMEM):
-    return pl.BlockSpec(memory_space=space)
-
-
-def call(kernel, outs, args, smem=(), **params):
+        memory_grad_ref[0, 0, :, kv] = (keys_grad * scale).astype(BF16)
+        memory_grad_ref[1, 0, :, kv] = values_grad.astype(BF16)
+
+
+def call(kernel, outs, args, smem=(), scratch=(), **params):
     specs = [pl.BlockSpec(memory_space=pltpu.SMEM if i in smem else pltpu.VMEM) for i in range(len(args))]
     return pl.pallas_call(
         kernel,
         out_shape=outs,
         in_specs=specs,
         out_specs=jax.tree.map(lambda _: pl.BlockSpec(memory_space=pltpu.VMEM), outs),
+        scratch_shapes=scratch,
         interpret=INTERPRET,
         **params,
     )(*args)
@@ -258,35 +276,58 @@
 SPLIT = (2, 12, 2)
 AXES = ("sec", "yh", "z", "core", "mp")
 DP = ("yh", "z", "core")
+Y = ("sec", "yh")
 
 
 def share(x, axes, n):
-    return lax.all_to_all(jnp.broadcast_to(x[None], (n,) + x.shape), axes, 0, 0, tiled=True)
-
-
-def reduce_part(x, axes, n):
-    got = lax.all_to_all(x, axes, 0, 0, tiled=True)
-    return jnp.sum(got, axis=0)
+    return exchange(jnp.broadcast_to(x[None], (n,) + x.shape), axes)
+
+
+def exchange(x, axes):
+    return lax.all_to_all(x, axes, 0, 0, tiled=True)
+
+
+def swap(x, n):
+    return lax.ppermute(x, "core", [(i, n - 1 - i) for i in range(n)])
 
 
 def on_device(policy_query, policy_memory, chosen, adapter_rows, adapter_down, adapter_up,
               scorer_query, scorer_key_values, score_heads, document_ids, prompt_lengths):
     sec = lax.axis_index("sec").astype(jnp.int32).reshape(1)
+    core = lax.axis_index("core").astype(jnp.int32).reshape(1)
     n_sec, n_mp = lax.axis_size("sec"), lax.axis_size("mp")
-    sizes = [lax.axis_size(a) for a in DP]
-    query, keys, values = policy_query[0], policy_memory[0, 0], policy_memory[1, 0]
+    n_yh, n_z, n_core = (lax.axis_size(a) for a in DP)
+    n_y = n_sec * n_yh
+    query = policy_query[0]
     rows = chosen[0]
     tokens, features = query.shape
-    kv_features = keys.shape[1]
+    kv_features = policy_memory.shape[3]
     adapter = adapter_rows[0]
     down = adapter_down.T
     rank = down.shape[0]
     width = adapter.shape[1]
     heads = features // HEAD
     prompts = prompt_lengths[:, 0]
-
-    rows_all = lax.all_gather(rows, "sec", axis=0, tiled=False)
-    scorer_att = pl.pallas_call(
+    blocks = (features + width) // HEAD
+    half = sds((blocks // n_core, rank, HEAD))
+
+    held = (
+        rows,
+        lax.ppermute(rows, "sec", [(1, 0), (2, 1)]),
+        lax.ppermute(rows, "sec", [(2, 0), (3, 1)]),
+        lax.ppermute(rows, "sec", [(3, 0), (0, 1)]),
+    )
+    attended, probs, part = call(
+        policy_kernel,
+        (sds((tokens, features)), sds((heads, tokens, tokens)), sds((2 * rank + 8, tokens))),
+        (sec, document_ids, query, policy_memory, rows, adapter, down, adapter_up),
+        smem=(0,),
+        cost_estimate=pl.CostEstimate(flops=150_000_000, bytes_accessed=3_000_000, transcendentals=150_000),
+    )
+    parts = (part,) + tuple(
+        lax.ppermute(part, "mp", [(i, (i + k) % n_mp) for i in range(n_mp)]) for k in range(1, n_mp)
+    )
+    scorer = pl.pallas_call(
         scorer_kernel,
         grid=(n_sec,),
         out_shape=sds((n_sec, tokens, features)),
@@ -295,39 +336,43 @@
             pl.BlockSpec((None, None, None, tokens, features), lambda j: (0, j, 0, 0, 0)),
             pl.BlockSpec((None, None, None, None, tokens, kv_features), lambda j: (0, 0, j, 0, 0, 0)),
             pl.BlockSpec((None, None, None, None, tokens, kv_features), lambda j: (0, 1, j, 0, 0, 0)),
+            pl.BlockSpec(memory_space=pl.ANY),
         ],
         out_specs=pl.BlockSpec((None, tokens, features), lambda j: (j, 0, 0)),
         interpret=INTERPRET,
-        cost_estimate=pl.CostEstimate(flops=300_000_000, bytes_accessed=5_000_000, transcendentals=600_000),
-    )(document_ids, scorer_query, scorer_key_values, scorer_key_values)
-    attended, probs, part = call(
-        policy_kernel,
-        (sds((tokens, features)), sds((heads, tokens, tokens)), sds((2 * rank + 8, tokens))),
-        (sec, document_ids, query, keys, values, rows, adapter, down, adapter_up),
+        cost_estimate=pl.CostEstimate(flops=300_000_000, bytes_accessed=30_000_000, transcendentals=600_000),
+    )
+    scorer_att = scorer(document_ids, scorer_query, scorer_key_values, scorer_key_values, part)
+    partials = call(score_kernel, sds((n_sec * n_mp, 1, tokens)), (sec, scorer_att) + held + (score_heads,),
+                    smem=(0,),
+                    cost_estimate=pl.CostEstimate(flops=2_000_000, bytes_accessed=3_000_000, transcendentals=0))
+    got = exchange(partials, ("sec", "mp")).reshape(n_sec, n_mp, tokens)
+    keep, sums = call(delta_kernel, (sds((8, tokens)), sds((n_z * n_core, 1, tokens))),
+                      (sec, prompts, document_ids, got), smem=(0, 1))
+    sums = exchange(sums, ("z", "core")).sum(axis=0)
+    moments = share(sums, Y, n_y).reshape(n_y, tokens)
+    white, grad_score, scaled_out, own, send = call(
+        weights_kernel,
+        (sds((1, tokens)), sds((1, tokens)), sds((rank, tokens)), half, half),
+        (core, moments, keep, attended, adapter) + parts,
         smem=(0,),
-        cost_estimate=pl.CostEstimate(flops=150_000_000, bytes_accessed=3_000_000, transcendentals=150_000),
-    )
-    parts = share(part, "mp", n_mp)
-    partials = call(score_kernel, sds((n_sec, tokens)), (sec, scorer_att, rows_all, score_heads), smem=(0,),
-                    cost_estimate=pl.CostEstimate(flops=2_000_000, bytes_accessed=3_000_000, transcendentals=0))
-    sent = jnp.broadcast_to(partials[:, None], (n_sec, n_mp, tokens)).reshape(n_sec * n_mp, 1, tokens)
-    got = lax.all_to_all(sent, ("sec", "mp"), 0, 0, tiled=True).reshape(n_sec, n_mp, tokens)
-    keep, sums = call(delta_kernel, (sds((8, tokens)), sds((8, tokens))),
-                      (sec, prompts, document_ids, got), smem=(0, 1))
-    moments = gather_moments(sums, n_sec, sizes)
-    white, grad_score, scaled_out, down_part, up_part = call(
-        weights_kernel,
-        (sds((1, tokens)), sds((1, tokens)), sds((rank, tokens)), sds((rank, features)), sds((rank, width))),
-        (moments, keep, parts, attended, adapter),
-    )
-    down_grad, up_grad = reduce_grads(down_part, up_part, n_sec, sizes)
-    query_grad, keys_grad, values_grad = call(
+        scratch=(pltpu.VMEM((blocks, rank, HEAD), F32),),
+    )
+    summed = own + swap(send, n_core) if n_core > 1 else own
+    got = exchange(summed.astype(BF16).reshape(n_z, -1, HEAD), "z")
+    per = got.shape[1]
+    got = exchange(call(spread_kernel, sds((n_y, per, HEAD), BF16), (got,)), Y)
+    got = exchange(call(spread_kernel, sds((n_z, per, HEAD), BF16), (got,)), "z")
+    got = got.reshape(half.shape)
+    down_grad, up_grad = call(place_kernel, (sds((rank, features)), sds((rank, width))),
+                              (core, got, swap(got, n_core)), smem=(0,),
+                              scratch=(pltpu.VMEM((blocks, rank, HEAD), BF16),))
+    query_grad, memory_grad = call(
         backward_kernel,
-        (sds((tokens, features), BF16), sds((tokens, kv_features), BF16), sds((tokens, kv_features), BF16)),
-        (grad_score, scaled_out, down, rows, probs, query, keys, values),
-        cost_estimate=pl.CostEstimate(flops=300_000_000, bytes_accessed=4_000_000, transcendentals=0),
-    )
-    memory_grad = jnp.stack([keys_grad, values_grad])[:, None]
+        (sds((tokens, features), BF16), sds(policy_memory.shape, BF16)),
+        (grad_score, scaled_out, down, rows, probs, query, policy_memory),
+        cost_estimate=pl.CostEstimate(flops=300_000_000, bytes_accessed=20_000_000, transcendentals=0),
+    )
     return white, query_grad[None], memory_grad, down_grad.T, up_grad
 
 
@@ -336,6 +381,7 @@
     split = SPLIT if int(np.prod(SPLIT)) == devices.shape[1] else (1, devices.shape[1], 1)
     inner = Mesh(devices.reshape((devices.shape[0],) + split + (devices.shape[2],)), AXES)
     both = ("sec",) + DP
+
     return jax.shard_map(
         on_device,
         mesh=inner,

time: 212 us -> 166 us (0.78)
  waiting for transfers between devices: 55.7 us -> 7.87 us
  between operations: 14.1 us -> 0.81 us
  starting transfers between devices: 21 us -> 34.2 us
  local copies, waits for them, and re-layouts: 8.9 us -> 3.26 us
  Pallas kernels: 28.8 us -> 34.1 us
  blocking collectives: 81 us -> 83.9 us
    all_gather x1 -> x0, waiting for transfers between devices: 35.6 us -> none  [on_device(): rows_all = lax.all_gather(rows, 'sec', axis=0, tiled=False)]
    ppermute x0 -> x8, starting transfers between devices: none -> 28.3 us  [the longest x3 10.7 us: on_device(): lax.ppermute(part, 'mp', [(i, (i + k) % n_mp) for i in range(n_mp)])]
    all_to_all x3 -> x1, starting transfers between devices: 20.9 us -> 5.92 us  [exchange(): return lax.all_to_all(x, axes, 0, 0, tiled=True)]
    all_to_all x3 -> x1, waiting for transfers between devices: 19.5 us -> 6.32 us  [exchange(): return lax.all_to_all(x, axes, 0, 0, tiled=True)]
    pallas_call x5 -> x8, Pallas kernels: 16.2 us -> 21.5 us  [call(): pl.pallas_call(kernel, out_shape=outs, in_specs=specs, out_specs=jax.tree...]
    broadcast_in_dim x8 -> x1, local copies, waits for them, and re-layouts: 4.43 us -> 0.6 us  [share(): return exchange(jnp.broadcast_to(x[None], (n,) + x.shape), axes)]
    reshape x4 -> x0, local copies, waits for them, and re-layouts: 3.75 us -> none  [the longest x2 1.62 us: reduce_grads(): return (x[:cut].reshape(down_part.shape), x[cut:].reshape(up_part.shape))]
    all_to_all x7 -> x5, blocking collectives: 81 us -> 83.9 us  [exchange(): return lax.all_to_all(x, axes, 0, 0, tiled=True)]
  transfers between devices with their start and end apart: 4 -> 9, of which waited for: 4 -> 2; matrix products, arithmetic and copies ran while one was open for 1% -> 0% of each run, Pallas kernels for 10% -> 16%
where the time goes in v2:
time: 166 us; the launch traced here: 165 us
  blocking collectives  83.9 us (51%)
  starting transfers between devices  34.2 us (21%)
  Pallas kernels  34.1 us (21%)
  waiting for transfers between devices  7.87 us (5%)
  local copies, waits for them, and re-layouts  3.26 us (2%)
    all_to_all x5, blocking collectives, exchange(): return lax.all_to_all(x, axes, 0, 0, tiled=True)  83.9 us
    pallas_call x8, Pallas kernels, call(): pl.pallas_call(kernel, out_shape=outs, in_specs=specs, out_specs=jax.tree...  21.5 us
    pallas_call x1, Pallas kernels, on_device(): scorer(document_ids, scorer_query, scorer_key_values, scorer_key_values,...  12.6 us
    ppermute x3, starting transfers between devices, on_device(): lax.ppermute(part, 'mp', [(i, (i + k) % n_mp) for i in range(n_mp)])  10.7 us
    ppermute x2, starting transfers between devices, swap(): return lax.ppermute(x, 'core', [(i, n - 1 - i) for i in range(n)])  10.3 us
    all_to_all x1, waiting for transfers between devices, exchange(): return lax.all_to_all(x, axes, 0, 0, tiled=True)  6.32 us
    all_to_all x1, starting transfers between devices, exchange(): return lax.all_to_all(x, axes, 0, 0, tiled=True)  5.92 us
    ppermute x1, starting transfers between devices, on_device(): lax.ppermute(rows, 'sec', [(3, 0), (0, 1)])  4.66 us
  transfers between devices with their start and end apart: 9, of which 2 were waited for; matrix products, arithmetic and copies ran while one was open for 0% of the time, Pallas kernels for 16%

profile of v2, /device:TPU:1, one launch (start us, length us, event | category | flops | bytes accessed | tf_op | source)
XLA Modules:
  0.0 165.3 jit_solution(988868934826341603)
XLA Ops:
  0.6 1.3 collective-permute-start
  1.9 1.3 collective-permute-start.1
  3.2 4.7 %collective-permute-start.2 = (bf16[128,1024]{1,0:T(8,128)(2,1)}, bf16[128,1024]{1,0:T(8,128)(2,1)S(1)}, u32[]{:S(2)}, u32[]{:S(2)}) collective-permute-start(bf16[128,1024]{1,0:T(8,128)(2,1)} %bitcast.13), channel_id=1, source_target_pairs={{576,0},{0,192},{577,1},{1,193},{578,2},{2,194},{579,3},{3,195},{5... | collective-permute-start | bytes 786440 | tf_op jit(solution)/shard_map/ppermute | solution.py:318
  7.9 4.4 %shard_map.146 = (f32[128,1024]{1,0:T(8,128)}, f32[8,128,128]{2,1,0:T(8,128)}, f32[136,128]{1,0:T(8,128)}) custom-call(s32[1]{0:T(128)} %bitcast.1.sec_ref, s32[4,1,128]{2,1,0:T(1,128)} %doc_ref.5, bf16[128,1024]{1,0:T(8,128)(2,1)} %bitcast.19, bf16[2,1,128,256]{3,2,1,0:T(8,128)(2,1)} %memory_ref.3, bf16[128,1024]{1,0:T(8,128)(2,1)} %bitcast.14, ...), custom_call_target="tpu_custom_call" | custom-call | flops 150000000 | bytes 3000000 | tf_op jit(solution)/shard_map/pallas_call | solution.py:260
  12.3 3.3 %collective-permute-start.3 = (f32[136,128]{1,0:T(8,128)}, f32[136,128]{1,0:T(8,128)S(1)}, u32[]{:S(2)}, u32[]{:S(2)}) collective-permute-start(f32[136,128]{1,0:T(8,128)} %get-tuple-element.19.after_ref.part0), channel_id=1, source_target_pairs={{0,1},{1,2},{2,3},{3,0},{4,5},{5,6},{6,7},{7,4},{8,9},{9,10},{10,1... | collective-permute-start | bytes 208904 | tf_op jit(solution)/shard_map/ppermute | solution.py:328
  15.5 4.4 %collective-permute-start.4 = (f32[136,128]{1,0:T(8,128)}, f32[136,128]{1,0:T(8,128)S(1)}, u32[]{:S(2)}, u32[]{:S(2)}) collective-permute-start(f32[136,128]{1,0:T(8,128)} %get-tuple-element.19.after_ref.part0), channel_id=1, source_target_pairs={{0,2},{1,3},{2,0},{3,1},{4,6},{5,7},{6,4},{7,5},{8,10},{9,11},{10,... | collective-permute-start | bytes 208904 | tf_op jit(solution)/shard_map/ppermute | solution.py:328
  19.9 0.0 collective-permute-done.next_ref
  19.9 0.0 copy-start.1
  19.9 3.1 %collective-permute-start.5 = (f32[136,128]{1,0:T(8,128)}, f32[136,128]{1,0:T(8,128)S(1)}, u32[]{:S(2)}, u32[]{:S(2)}) collective-permute-start(f32[136,128]{1,0:T(8,128)} %get-tuple-element.19.after_ref.part0), channel_id=1, source_target_pairs={{0,3},{1,0},{2,1},{3,2},{4,7},{5,4},{6,5},{7,6},{8,11},{9,8},{10,9... | collective-permute-start | bytes 208904 | tf_op jit(solution)/shard_map/ppermute | solution.py:328
  23.0 12.6 %shard_map.147.att_ref = f32[4,128,1024]{2,1,0:T(8,128)} custom-call(s32[4,1,128]{2,1,0:T(1,128)} %doc_ref.5, bf16[1,4,1,128,1024]{4,3,2,1,0:T(8,128)(2,1)} %q_ref.1, bf16[1,2,4,1,128,256]{5,4,3,2,1,0:T(8,128)(2,1)} %v_ref.1, bf16[1,2,4,1,128,256]{5,4,3,2,1,0:T(8,128)(2,1)} %v_ref.1, f32[136,128]{1,0:T(8,128)} %get-tuple-element.19.after_ref.part0), custom_call_target="tpu_custom_call" | custom-call | flops 300000000 | bytes 30000000 | tf_op jit(solution)/shard_map/pallas_call | solution.py:345
  35.6 0.0 copy-done.1
  35.6 0.0 collective-permute-done.1.after_ref
  35.6 0.0 copy-start.2
  35.6 0.0 collective-permute-done.2.last_ref
  35.6 0.7 copy-done.2
  36.3 0.0 copy-start.3
  36.3 0.7 copy-done.3
  37.0 2.7 %shard_map.148 = f32[16,1,128]{2,1,0:T(1,128)} custom-call(s32[1]{0:T(128)} %bitcast.1.sec_ref, f32[4,128,1024]{2,1,0:T(8,128)} %shard_map.147.att_ref, bf16[128,1024]{1,0:T(8,128)(2,1)} %bitcast.15, bf16[128,1024]{1,0:T(8,128)(2,1)} %copy-done.1, bf16[128,1024]{1,0:T(8,128)(2,1)} %copy-done.2, bf16[128,1024]{1,0:T(8,128)(2,1)} %copy-done.3, f32[2,1024]{1,0:T(2,128)} %heads_ref.1), custom_call_target="tpu_custom_call" | custom-call | flops 2000000 | bytes 3000000 | tf_op jit(solution)/shard_map/pallas_call | solution.py:260
  39.7 13.0 %all_to_all.30 = f32[16,1,128]{2,1,0:T(1,128)} all-to-all(f32[16,1,128]{2,1,0:T(1,128)} %shard_map.148), channel_id=1, replica_groups=mesh['sec'=4,'yh'=2,'z'=12,'core'=2,'mp'=4] {'sec','mp'}, dimensions={0} | all-to-all | bytes 16384 | tf_op jit(solution)/shard_map/all_to_all | solution.py:287
  52.8 1.6 shard_map.149
  54.4 29.1 %all_to_all.31 = f32[24,1,128]{2,1,0:T(1,128)S(1)} all-to-all(f32[24,1,128]{2,1,0:T(1,128)} %get-tuple-element.20), channel_id=1, replica_groups=mesh['sec'=4,'yh'=2,'z'=12,'core'=2,'mp'=4] {'z','core'}, dimensions={0} | all-to-all | bytes 24576 | tf_op jit(solution)/shard_map/all_to_all | solution.py:287
  83.5 0.6 broadcast_in_dim.4
  84.1 5.9 %all-to-all-start.2 = ((f32[8,1,128]{2,1,0:T(1,128)}), f32[8,1,128]{2,1,0:T(1,128)S(1)}, u32[]{:S(2)}, u32[]{:S(2)}) async-start(f32[8,1,128]{2,1,0:T(1,128)} %broadcast_in_dim.4), calls=%async_computation.2 | async-start | bytes 8192 | tf_op jit(solution)/shard_map/all_to_all | solution.py:287
  90.0 0.0 collective-permute-done.3.part1
  90.0 0.0 copy-start.5
  90.1 0.0 collective-permute-done.4.part2
  90.1 0.0 copy-start.6
  90.1 0.0 collective-permute-done.5.part3
  90.1 0.0 copy-start.7
  90.1 6.3 %all-to-all-done.2 = f32[8,1,128]{2,1,0:T(1,128)S(1)} async-done(((f32[8,1,128]{2,1,0:T(1,128)}), f32[8,1,128]{2,1,0:T(1,128)S(1)}, u32[]{:S(2)}, u32[]{:S(2)}) %all-to-all-start.2) | async-done | bytes 4128 | tf_op jit(solution)/shard_map/all_to_all | solution.py:287
  96.4 0.0 copy-start.8
  96.4 0.0 copy-done.5
  96.4 0.0 copy-done.6
  96.4 0.0 copy-done.7
  96.4 0.6 copy-done.8
  97.0 2.7 %shard_map.150 = (f32[1,128]{1,0:T(1,128)}, f32[1,128]{1,0:T(1,128)}, f32[64,128]{1,0:T(8,128)}, f32[12,64,128]{2,1,0:T(8,128)}, f32[12,64,128]{2,1,0:T(8,128)}) custom-call(s32[1]{0:T(128)} %bitcast.core_ref, f32[8,128]{1,0:T(8,128)} %bitcast.24, f32[8,128]{1,0:T(8,128)} %get-tuple-element.21.keep_ref, f32[128,1024]{1,0:T(8,128)} %get-tuple-element.22.att_ref, ...), custom_call_target="tpu_custom_call" | custom-call | tf_op jit(solution)/shard_map/pallas_call | solution.py:260
  99.7 4.1 %collective-permute-start.6 = (f32[12,64,128]{2,1,0:T(8,128)}, f32[12,64,128]{2,1,0:T(8,128)S(1)}, u32[]{:S(2)}, u32[]{:S(2)}) collective-permute-start(f32[12,64,128]{2,1,0:T(8,128)} %get-tuple-element.30), channel_id=1, source_target_pairs={{0,4},{4,0},{1,5},{5,1},{2,6},{6,2},{3,7},{7,3},{8,12},{12,8},{9,1... | collective-permute-start | bytes 1179656 | tf_op jit(solution)/shard_map/ppermute | solution.py:291
  103.9 1.5 collective-permute-done.6
  105.4 1.1 add_convert_fusion
  106.5 16.6 %all_to_all.32.got_ref = bf16[12,64,128]{2,1,0:T(8,128)(2,1)} all-to-all(bf16[12,64,128]{2,1,0:T(8,128)(2,1)S(1)} %add_convert_fusion), channel_id=1, replica_groups=mesh['sec'=4,'yh'=2,'z'=12,'core'=2,'mp'=4] {'z'}, dimensions={0} | all-to-all | bytes 393216 | tf_op jit(solution)/shard_map/all_to_all | solution.py:287
  123.0 1.6 shard_map.152
  124.6 10.8 %all_to_all.33.got_ref = bf16[8,64,128]{2,1,0:T(8,128)(2,1)} all-to-all(bf16[8,64,128]{2,1,0:T(8,128)(2,1)} %shard_map.152), channel_id=1, replica_groups=mesh['sec'=4,'yh'=2,'z'=12,'core'=2,'mp'=4] {'sec','yh'}, dimensions={0} | all-to-all | bytes 262144 | tf_op jit(solution)/shard_map/all_to_all | solution.py:287
  135.4 1.6 shard_map.153
  137.0 14.5 %all_to_all.34.own_ref = bf16[12,64,128]{2,1,0:T(8,128)(2,1)S(1)} all-to-all(bf16[12,64,128]{2,1,0:T(8,128)(2,1)} %shard_map.153), channel_id=1, replica_groups=mesh['sec'=4,'yh'=2,'z'=12,'core'=2,'mp'=4] {'z'}, dimensions={0} | all-to-all | bytes 393216 | tf_op jit(solution)/shard_map/all_to_all | solution.py:287
  151.5 0.0 copy-start
  151.5 6.2 %collective-permute-start.7 = (bf16[12,64,128]{2,1,0:T(8,128)(2,1)S(1)}, bf16[12,64,128]{2,1,0:T(8,128)(2,1)S(1)}, u32[]{:S(2)}, u32[]{:S(2)}) collective-permute-start(bf16[12,64,128]{2,1,0:T(8,128)(2,1)S(1)} %all_to_all.34.own_ref), channel_id=1, source_target_pairs={{0,4},{4,0},{1,5},{5,1},{2,6},{6,2},{3,7},{7,3},{8,12},{12,8},{9,1... | collective-permute-start | bytes 589832 | tf_op jit(solution)/shard_map/ppermute | solution.py:291
  157.7 4.9 %shard_map.151 = (bf16[128,1024]{1,0:T(8,128)(2,1)}, bf16[2,1,128,256]{3,2,1,0:T(8,128)(2,1)}) custom-call(f32[1,128]{1,0:T(1,128)} %get-tuple-element.24.grad_ref, f32[64,128]{1,0:T(8,128)} %get-tuple-element.25.out_ref, bf16[64,1024]{1,0:T(8,128)(2,1)} %bitcast.22, bf16[128,1024]{1,0:T(8,128)(2,1)} %bitcast.16, ...), custom_call_target="tpu_custom_call" | custom-call | flops 300000000 | bytes 20000000 | tf_op jit(solution)/shard_map/pallas_call | solution.py:260
  162.6 0.0 collective-permute-done.7.other_ref
  162.6 0.0 copy-done
  162.6 0.0 copy-start.4
  162.6 0.7 copy-done.4
  163.3 1.9 %shard_map.154 = (f32[64,1024]{1,0:T(8,128)}, f32[64,2048]{1,0:T(8,128)}) custom-call(s32[1]{0:T(128)} %bitcast.core_ref, bf16[12,64,128]{2,1,0:T(8,128)(2,1)} %copy-done, bf16[12,64,128]{2,1,0:T(8,128)(2,1)} %copy-done.4), custom_call_target="tpu_custom_call" | custom-call | tf_op jit(solution)/shard_map/pallas_call | solution.py:260
  (1 shorter events, 0.0 us)
Async XLA Ops:
  0.6 19.3 %collective-permute-start = (bf16[128,1024]{1,0:T(8,128)(2,1)}, bf16[128,1024]{1,0:T(8,128)(2,1)S(1)}, u32[]{:S(2)}, u32[]{:S(2)}) collective-permute-start(bf16[128,1024]{1,0:T(8,128)(2,1)} %bitcast.11), channel_id=1, source_target_pairs={{192,0},{384,192},{193,1},{385,193},{194,2},{386,194},{195,3},{387... | collective-permute-start | bytes 786440 | tf_op jit(solution)/shard_map/ppermute | solution.py:316
  1.9 33.7 %collective-permute-start.1 = (bf16[128,1024]{1,0:T(8,128)(2,1)}, bf16[128,1024]{1,0:T(8,128)(2,1)S(1)}, u32[]{:S(2)}, u32[]{:S(2)}) collective-permute-start(bf16[128,1024]{1,0:T(8,128)(2,1)} %bitcast.12), channel_id=1, source_target_pairs={{384,0},{576,192},{385,1},{577,193},{386,2},{578,194},{387,3},{579... | collective-permute-start | bytes 786440 | tf_op jit(solution)/shard_map/ppermute | solution.py:317
  3.2 32.4 %collective-permute-start.2 = (bf16[128,1024]{1,0:T(8,128)(2,1)}, bf16[128,1024]{1,0:T(8,128)(2,1)S(1)}, u32[]{:S(2)}, u32[]{:S(2)}) collective-permute-start(bf16[128,1024]{1,0:T(8,128)(2,1)} %bitcast.13), channel_id=1, source_target_pairs={{576,0},{0,192},{577,1},{1,193},{578,2},{2,194},{579,3},{3,195},{5... | collective-permute-start | bytes 786440 | tf_op jit(solution)/shard_map/ppermute | solution.py:318
  12.3 77.8 %collective-permute-start.3 = (f32[136,128]{1,0:T(8,128)}, f32[136,128]{1,0:T(8,128)S(1)}, u32[]{:S(2)}, u32[]{:S(2)}) collective-permute-start(f32[136,128]{1,0:T(8,128)} %get-tuple-element.19.after_ref.part0), channel_id=1, source_target_pairs={{0,1},{1,2},{2,3},{3,0},{4,5},{5,6},{6,7},{7,4},{8,9},{9,10},{10,1... | collective-permute-start | bytes 208904 | tf_op jit(solution)/shard_map/ppermute | solution.py:328
  15.5 74.5 %collective-permute-start.4 = (f32[136,128]{1,0:T(8,128)}, f32[136,128]{1,0:T(8,128)S(1)}, u32[]{:S(2)}, u32[]{:S(2)}) collective-permute-start(f32[136,128]{1,0:T(8,128)} %get-tuple-element.19.after_ref.part0), channel_id=1, source_target_pairs={{0,2},{1,3},{2,0},{3,1},{4,6},{5,7},{6,4},{7,5},{8,10},{9,11},{10,... | collective-permute-start | bytes 208904 | tf_op jit(solution)/shard_map/ppermute | solution.py:328
  19.9 15.7 %copy-start.1 = (bf16[128,1024]{1,0:T(8,128)(2,1)}, bf16[128,1024]{1,0:T(8,128)(2,1)S(1)}, u32[]{:S(2)}) copy-start(bf16[128,1024]{1,0:T(8,128)(2,1)S(1)} %collective-permute-done.next_ref) | copy-start | bytes 786436
  19.9 70.1 %collective-permute-start.5 = (f32[136,128]{1,0:T(8,128)}, f32[136,128]{1,0:T(8,128)S(1)}, u32[]{:S(2)}, u32[]{:S(2)}) collective-permute-start(f32[136,128]{1,0:T(8,128)} %get-tuple-element.19.after_ref.part0), channel_id=1, source_target_pairs={{0,3},{1,0},{2,1},{3,2},{4,7},{5,4},{6,5},{7,6},{8,11},{9,8},{10,9... | collective-permute-start | bytes 208904 | tf_op jit(solution)/shard_map/ppermute | solution.py:328
  35.6 0.7 copy-start.2
  36.3 0.7 copy-start.3
  84.1 12.3 %all-to-all-start.2 = ((f32[8,1,128]{2,1,0:T(1,128)}), f32[8,1,128]{2,1,0:T(1,128)S(1)}, u32[]{:S(2)}, u32[]{:S(2)}) async-start(f32[8,1,128]{2,1,0:T(1,128)} %broadcast_in_dim.4), calls=%async_computation.2 | async-start | bytes 8192 | tf_op jit(solution)/shard_map/all_to_all | solution.py:287
  90.0 6.4 %copy-start.5 = (f32[136,128]{1,0:T(8,128)}, f32[136,128]{1,0:T(8,128)S(1)}, u32[]{:S(2)}) copy-start(f32[136,128]{1,0:T(8,128)S(1)} %collective-permute-done.3.part1) | copy-start | bytes 208900
  90.1 6.4 %copy-start.6 = (f32[136,128]{1,0:T(8,128)}, f32[136,128]{1,0:T(8,128)S(1)}, u32[]{:S(2)}) copy-start(f32[136,128]{1,0:T(8,128)S(1)} %collective-permute-done.4.part2) | copy-start | bytes 208900
  90.1 6.3 %copy-start.7 = (f32[136,128]{1,0:T(8,128)}, f32[136,128]{1,0:T(8,128)S(1)}, u32[]{:S(2)}) copy-start(f32[136,128]{1,0:T(8,128)S(1)} %collective-permute-done.5.part3) | copy-start | bytes 208900
  96.4 0.6 copy-start.8
  99.7 5.7 %collective-permute-start.6 = (f32[12,64,128]{2,1,0:T(8,128)}, f32[12,64,128]{2,1,0:T(8,128)S(1)}, u32[]{:S(2)}, u32[]{:S(2)}) collective-permute-start(f32[12,64,128]{2,1,0:T(8,128)} %get-tuple-element.30), channel_id=1, source_target_pairs={{0,4},{4,0},{1,5},{5,1},{2,6},{6,2},{3,7},{7,3},{8,12},{12,8},{9,1... | collective-permute-start | bytes 1179656 | tf_op jit(solution)/shard_map/ppermute | solution.py:291
  151.5 11.1 %copy-start = (bf16[12,64,128]{2,1,0:T(8,128)(2,1)}, bf16[12,64,128]{2,1,0:T(8,128)(2,1)S(1)}, u32[]{:S(2)}) copy-start(bf16[12,64,128]{2,1,0:T(8,128)(2,1)S(1)} %all_to_all.34.own_ref) | copy-start | bytes 589828
  151.5 11.1 %collective-permute-start.7 = (bf16[12,64,128]{2,1,0:T(8,128)(2,1)S(1)}, bf16[12,64,128]{2,1,0:T(8,128)(2,1)S(1)}, u32[]{:S(2)}, u32[]{:S(2)}) collective-permute-start(bf16[12,64,128]{2,1,0:T(8,128)(2,1)S(1)} %all_to_all.34.own_ref), channel_id=1, source_target_pairs={{0,4},{4,0},{1,5},{5,1},{2,6},{6,2},{3,7},{7,3},{8,12},{12,8},{9,1... | collective-permute-start | bytes 589832 | tf_op jit(solution)/shard_map/ppermute | solution.py:291
  162.6 0.7 copy-start.4

commit v3 on v2

v3 whole, which is shorter than its diff:
```python
import jax
import jax.numpy as jnp
import numpy as np
from jax import lax
from jax.experimental import pallas as pl
from jax.experimental.pallas import tpu as pltpu
from jax.sharding import Mesh, PartitionSpec as P

HEAD = 128
KL = 0.1
DECAY = 0.95
EPS = 1e-05
MASKED = -1e30
SMALL = 2.0 ** -20
F32 = jnp.float32
BF16 = jnp.bfloat16
NT = (((1,), (1,)), ((), ()))
NN = (((1,), (0,)), ((), ()))
TN = (((0,), (0,)), ((), ()))


def dot(a, b, dims):
    return lax.dot_general(a, b, dims, preferred_element_type=F32)


def halves(x):
    high = x.astype(BF16)
    return high, (x - high.astype(F32)).astype(BF16)


def as_column(row):
    n = row.shape[1]
    return jnp.broadcast_to(row, (n, n)).T


def square(row):
    n = row.shape[1]
    return jnp.broadcast_to(row, (n, n))


def kept_of(doc_row, groups):
    n = doc_row.shape[1]
    doc = doc_row.astype(F32)
    rows = lax.broadcasted_iota(jnp.int32, (n, n), 0)
    lanes = lax.broadcasted_iota(jnp.int32, (n, n), 1)
    kept = jnp.where((as_column(doc) == square(doc)) & (rows <= lanes), 1.0, 0.0)
    return jnp.concatenate([kept] * groups, axis=1) > 0.5


def stacked(ref, group, groups):
    first = group * groups
    return jnp.concatenate([ref[:, (first + i) * HEAD:(first + i + 1) * HEAD] for i in range(groups)], axis=0)


def probs_of(query, keys, kept):
    scores = dot(keys, query, NT)
    scores = jnp.where(kept, scores, MASKED)
    top = jnp.max(scores, axis=0, keepdims=True)
    raised = jnp.exp((scores - top) * HEAD ** (-0.5))
    return raised * (1.0 / jnp.sum(raised, axis=0, keepdims=True))


def scorer_kernel(doc_ref, q_ref, k_ref, v_ref, after_ref, out_ref):
    del after_ref
    n = q_ref.shape[0]
    groups = q_ref.shape[1] // k_ref.shape[1]
    kept = kept_of(doc_ref[...], groups)
    for group in range(k_ref.shape[1] // HEAD):
        kv = slice(group * HEAD, (group + 1) * HEAD)
        probs = probs_of(stacked(q_ref, group, groups), k_ref[:, kv], kept).astype(BF16)
        attended = dot(probs, v_ref[:, kv], TN)
        for i in range(groups):
            at = (group * groups + i) * HEAD
            out_ref[:, at:at + HEAD] = attended[i * n:(i + 1) * n]


def score_kernel(sec_ref, att_ref, own_ref, next_ref, after_ref, last_ref, heads_ref, out_ref):
    sec = sec_ref[0]
    n_sec = att_ref.shape[0]
    copies = out_ref.shape[0] // n_sec
    n_heads = att_ref.shape[2] // HEAD
    held = (own_ref, next_ref, after_ref, last_ref)

    def put(weight):
        for step in range(n_sec):
            row = lax.rem(sec + step, n_sec)
            total = None
            for head in range(n_heads):
                at = slice(head * HEAD, (head + 1) * HEAD)
                term = att_ref[row, :, at] * weight(step, at)
                total = term if total is None else total + term
            score = jnp.sum(total.T, axis=0, keepdims=True)
            for copy in range(copies):
                out_ref[row * copies + copy] = score

    @pl.when(sec < 2)
    def _():
        put(lambda step, at: held[step][:, at].astype(F32))

    @pl.when(sec >= 2)
    def _():
        put(lambda step, at: jnp.where(sec == 2, heads_ref[0:1, at], heads_ref[1:2, at]))


def policy_kernel(sec_ref, doc_ref, q_ref, memory_ref, rows_ref, adapter_ref, down_ref, up_ref,
                  att_ref, probs_ref, part_ref):
    k_ref, v_ref = memory_ref.at[0, 0], memory_ref.at[1, 0]
    n = q_ref.shape[0]
    groups = q_ref.shape[1] // k_ref.shape[1]
    kept = kept_of(doc_ref[sec_ref[0]], groups)
    base = None
    low_in = None
    for group in range(k_ref.shape[1] // HEAD):
        kv = slice(group * HEAD, (group + 1) * HEAD)
        probs = probs_of(stacked(q_ref, group, groups), k_ref[:, kv], kept)
        probs_ref[group] = probs
        attended = dot(probs.astype(BF16), v_ref[:, kv], TN)
        for i in range(groups):
            at = slice((group * groups + i) * HEAD, (group * groups + i + 1) * HEAD)
            own = attended[i * n:(i + 1) * n]
            att_ref[:, at] = own
            term = own * rows_ref[:, at].astype(F32)
            base = term if base is None else base + term
            high, low = halves(own)
            down = down_ref[:, at]
            term = dot(down, high, NT) + dot(down, low, NT)
            low_in = term if low_in is None else low_in + term
    rank = down_ref.shape[0]
    part_ref[0:rank, :] = low_in
    part_ref[rank:2 * rank, :] = dot(up_ref[...], adapter_ref[...], NT)
    base_row = jnp.sum(base.T, axis=0, keepdims=True)
    part_ref[2 * rank:, :] = jnp.broadcast_to(base_row, (8, base_row.shape[1]))


def pick(row, index):
    lane = lax.broadcasted_iota(jnp.int32, row.shape, 1)
    return jnp.sum(jnp.where(lane == index, row, 0.0), axis=1, keepdims=True)


def weights_kernel(sec_ref, core_ref, prompt_ref, doc_ref, got_ref, att_ref, adapter_ref,
                   part0, part1, part2, part3,
                   keep_ref, low_ref, own_ref, send_ref, both_ref):
    sec = sec_ref[0]
    doc = doc_ref[sec].astype(F32)
    n = doc.shape[1]
    doc_col, doc_row = as_column(doc), square(doc)
    rows = lax.broadcasted_iota(jnp.int32, (n, n), 0)
    lanes = lax.broadcasted_iota(jnp.int32, (n, n), 1)
    position = lax.broadcasted_iota(jnp.int32, (1, n), 1).astype(F32)
    start = jnp.sum(jnp.where(doc_col < doc_row, 1.0, 0.0), axis=0, keepdims=True)
    ending = jnp.sum(jnp.where(doc_col <= doc_row, 1.0, 0.0), axis=0, keepdims=True) - 1.0
    prompt = jnp.zeros((1, n), F32)
    for label in range(prompt_ref.shape[1]):
        length = prompt_ref[sec, label].astype(F32)
        prompt = jnp.where(doc == float(label), length, prompt)
    respond = jnp.where(position - start >= prompt, 1.0, 0.0)
    closing = jnp.where(position == ending, 1.0, 0.0)

    def section(index):
        return jnp.sum(got_ref[index], axis=0, keepdims=True)

    old, ref, reward, value = section(0), section(1), section(2), section(3)
    next_value = jnp.where(position < n - 1.0, pltpu.roll(value, n - 1, 1), 0.0) * (1.0 - closing)
    delta = -KL * (old - ref) + closing * reward + next_value - value
    later = rows - lanes
    linked = (doc_col == doc_row) & (later >= 0)
    powers = jnp.exp(jnp.maximum(later, 0).astype(F32) * float(np.log(DECAY)))
    terms = jnp.where(linked, powers, 0.0) * as_column(delta)
    advantage = jnp.sum(terms, axis=0, keepdims=True)
    lane = lax.broadcasted_iota(jnp.int32, (1, n), 1)
    count = jnp.sum(respond, axis=1, keepdims=True)
    total = jnp.sum(respond * advantage, axis=1, keepdims=True)
    squares = jnp.sum(respond * advantage * advantage, axis=1, keepdims=True)
    moments = jnp.where(lane == 0, count, jnp.where(lane == 1, total, jnp.where(lane == 2, squares, 0.0)))

    rank = (part0.shape[0] - 8) // 2
    part = (part0[...] + part1[...]) + (part2[...] + part3[...])
    low_in, low_out, base = part[0:rank], part[rank:2 * rank], part[2 * rank:2 * rank + 1]
    policy_new = base + jnp.sum(low_in * low_out, axis=0, keepdims=True)
    weight = -respond * jnp.exp(policy_new - old)
    keep_ref[0:1, :] = respond
    keep_ref[1:2, :] = advantage
    keep_ref[2:3, :] = weight
    keep_ref[3:8, :] = jnp.zeros((5, n), F32)
    low_ref[...] = low_out
    plain = weight * SMALL
    lifted = plain * advantage
    out_high, out_low = halves(jnp.concatenate([plain * low_out, lifted * low_out], axis=0))
    in_high, in_low = halves(jnp.concatenate([plain * low_in, lifted * low_in], axis=0))
    n_down = att_ref.shape[1] // HEAD
    cores = both_ref.shape[0]
    slots = (n_down + adapter_ref.shape[1] // HEAD) // cores
    half = slots * rank
    for block in range(cores * slots):
        if block < n_down:
            high, low = halves(att_ref[:, block * HEAD:(block + 1) * HEAD])
            term = dot(out_high, high, NN) + (dot(out_low, high, NN) + dot(out_high, low, NN))
        else:
            at = (block - n_down) * HEAD
            columns = adapter_ref[:, at:at + HEAD]
            term = dot(in_high, columns, NN) + dot(in_low, columns, NN)
        owner, at = block // slots, block % slots * rank
        both_ref[owner, at:at + rank] = term[0:rank]
        both_ref[owner, half + at:half + at + rank] = term[rank:]
    for owner in range(cores):
        both_ref[owner, 2 * half:] = jnp.broadcast_to(moments, (8, n))
    core = core_ref[0]
    own_ref[...] = both_ref[core]
    send_ref[...] = both_ref[cores - 1 - core]


def middle(moments):
    near = pick(moments, 1) / jnp.maximum(pick(moments, 0), 1.0)
    return near.astype(BF16).astype(F32)


def note(moments, centre):
    n = moments.shape[1]
    first = moments.astype(BF16).astype(F32)
    rest = moments - first
    second = rest.astype(BF16).astype(F32)
    third = rest - second
    lane = lax.broadcasted_iota(jnp.int32, moments.shape, 1)
    first = jnp.where(lane == 3, centre, first)
    row = lax.broadcasted_iota(jnp.int32, (16, n), 0)
    return jnp.where(row == 0, first, jnp.where(row == 1, second, jnp.where(row == 2, third, 0.0))).astype(BF16)


def pair_kernel(own_ref, got_ref, out_ref):
    n_z, per = out_ref.shape[0], (out_ref.shape[1] - 16) // 2
    half = n_z * per
    moments = own_ref[2 * half:2 * half + 1] + got_ref[2 * half:2 * half + 1]
    centre = middle(moments)
    tile = note(moments, centre)
    for slot in range(n_z):
        at = slice(slot * per, (slot + 1) * per)
        to = slice(half + slot * per, half + (slot + 1) * per)
        plain = own_ref[at] + got_ref[at]
        lifted = own_ref[to] + got_ref[to]
        out_ref[slot, 0:per] = plain.astype(BF16)
        out_ref[slot, per:2 * per] = (lifted - centre * plain).astype(BF16)
        out_ref[slot, 2 * per:] = tile


def gathered(got_ref, per):
    notes = [jnp.sum(got_ref[i, 2 * per:].astype(F32), axis=0, keepdims=True) for i in range(got_ref.shape[0])]
    lane = lax.broadcasted_iota(jnp.int32, notes[0].shape, 1)
    moments = notes[0]
    for other in notes[1:]:
        moments = moments + other
    return jnp.where(lane < 3, moments, 0.0), [pick(x, 3) for x in notes]


def added(got_ref, per, centres, centre):
    plain, lifted = None, None
    for index in range(got_ref.shape[0]):
        mine = got_ref[index, 0:per].astype(F32)
        high = got_ref[index, per:2 * per].astype(F32) + (centres[index] - centre) * mine
        plain = mine if plain is None else plain + mine
        lifted = high if lifted is None else lifted + high
    return plain, lifted


def column_kernel(got_ref, out_ref):
    per = (got_ref.shape[1] - 16) // 2
    moments, centres = gathered(got_ref, per)
    centre = middle(moments)
    plain, lifted = added(got_ref, per, centres, centre)
    plain, lifted = plain.astype(BF16), lifted.astype(BF16)
    tile = note(moments, centre)
    for index in range(out_ref.shape[0]):
        out_ref[index, 0:per] = plain
        out_ref[index, per:2 * per] = lifted
        out_ref[index, 2 * per:] = tile


def scale_of(moments):
    count = pick(moments, 0)
    mean = pick(moments, 1) / count
    spread = pick(moments, 2) / count - mean * mean
    return count, mean, lax.rsqrt(spread + EPS)


def final_kernel(got_ref, out_ref, moments_ref):
    per = (got_ref.shape[1] - 16) // 2
    moments, centres = gathered(got_ref, per)
    count, mean, scale = scale_of(moments)
    _, lifted = added(got_ref, per, centres, mean)
    total = (lifted * (scale / count * (1.0 / SMALL))).astype(BF16)
    for index in range(out_ref.shape[0]):
        out_ref[index] = total
    moments_ref[...] = jnp.broadcast_to(moments, moments_ref.shape)


def place_kernel(core_ref, own_ref, other_ref, down_ref, up_ref, both_ref):
    core = core_ref[0]
    slots = own_ref.shape[0]
    cores = both_ref.shape[0] // slots
    for slot in range(slots):
        both_ref[(cores - 1 - core) * slots + slot] = other_ref[slot]
        both_ref[core * slots + slot] = own_ref[slot]
    n_down = down_ref.shape[1] // HEAD
    for block in range(both_ref.shape[0]):
        value = both_ref[block].astype(F32)
        if block < n_down:
            down_ref[:, block * HEAD:(block + 1) * HEAD] = value
        else:
            at = (block - n_down) * HEAD
            up_ref[:, at:at + HEAD] = value


def backward_kernel(moments_ref, keep_ref, low_ref, down_ref, rows_ref, probs_ref, q_ref, memory_ref,
                    white_ref, query_ref, memory_grad_ref):
    k_ref, v_ref = memory_ref.at[0, 0], memory_ref.at[1, 0]
    n = q_ref.shape[0]
    count, mean, inverse = scale_of(moments_ref[0:1, :])
    whitened = keep_ref[0:1, :] * (keep_ref[1:2, :] - mean) * inverse
    white_ref[...] = whitened
    grad_score = keep_ref[2:3, :] * whitened / count
    grad_col = as_column(grad_score)
    high, low = halves(grad_score * low_ref[...])
    groups = q_ref.shape[1] // k_ref.shape[1]
    scale = HEAD ** (-0.5)
    for group in range(k_ref.shape[1] // HEAD):
        kv = slice(group * HEAD, (group + 1) * HEAD)
        keys, values = k_ref[:, kv], v_ref[:, kv]
        grads = []
        for head in range(group * groups, (group + 1) * groups):
            at = slice(head * HEAD, (head + 1) * HEAD)
            down = down_ref[:, at]
            grad = grad_col * rows_ref[:, at].astype(F32) + (dot(high, down, TN) + dot(low, down, TN))
            grads.append(grad.astype(BF16))
        grad = jnp.concatenate(grads, axis=0)
        probs = probs_ref[group]
        dprobs = dot(values, grad, NT)
        inner = jnp.sum(probs * dprobs, axis=0, keepdims=True)
        dscores = (probs * (dprobs - inner)).astype(BF16)
        query_grad = (dot(dscores, keys, TN) * scale).astype(BF16)
        for i in range(groups):
            at = (group * groups + i) * HEAD
            query_ref[:, at:at + HEAD] = query_grad[i * n:(i + 1) * n]
        memory_grad_ref[0, 0, :, kv] = (dot(dscores, stacked(q_ref, group, groups), NN) * scale).astype(BF16)
        memory_grad_ref[1, 0, :, kv] = dot(probs.astype(BF16), grad, NN).astype(BF16)


def call(kernel, outs, args, smem=(), scratch=(), **params):
    specs = [pl.BlockSpec(memory_space=pltpu.SMEM if i in smem else pltpu.VMEM) for i in range(len(args))]
    return pl.pallas_call(
        kernel,
        out_shape=outs,
        in_specs=specs,
        out_specs=jax.tree.map(lambda _: pl.BlockSpec(memory_space=pltpu.VMEM), outs),
        scratch_shapes=scratch,
        compiler_params=pltpu.CompilerParams(vmem_limit_bytes=16 * 2**20),
        interpret=INTERPRET,
        **params,
    )(*args)


def sds(shape, dtype=F32):
    return jax.ShapeDtypeStruct(shape, dtype)


INTERPRET = False
SPLIT = (2, 12, 2)
AXES = ("sec", "yh", "z", "core", "mp")
DP = ("yh", "z", "core")
Y = ("sec", "yh")


def exchange(x, axes):
    return lax.all_to_all(x, axes, 0, 0, tiled=True)


def swap(x, n):
    return lax.ppermute(x, "core", [(i, n - 1 - i) for i in range(n)])


def on_device(policy_query, policy_memory, chosen, adapter_rows, adapter_down, adapter_up,
              scorer_query, scorer_key_values, score_heads, document_ids, prompt_lengths):
    sec = lax.axis_index("sec").astype(jnp.int32).reshape(1)
    core = lax.axis_index("core").astype(jnp.int32).reshape(1)
    n_sec, n_mp = lax.axis_size("sec"), lax.axis_size("mp")
    n_yh, n_z, n_core = (lax.axis_size(a) for a in DP)
    n_y = n_sec * n_yh
    query = policy_query[0]
    rows = chosen[0]
    tokens, features = query.shape
    kv_features = policy_memory.shape[3]
    adapter = adapter_rows[0]
    down = adapter_down.T
    rank = down.shape[0]
    width = adapter.shape[1]
    heads = features // HEAD
    prompts = prompt_lengths[:, 0]
    blocks = (features + width) // HEAD
    half = blocks // n_core * rank
    per = half // n_z

    held = (
        rows,
        lax.ppermute(rows, "sec", [(1, 0), (2, 1)]),
        lax.ppermute(rows, "sec", [(2, 0), (3, 1)]),
        lax.ppermute(rows, "sec", [(3, 0), (0, 1)]),
    )
    attended, probs, part = call(
        policy_kernel,
        (sds((tokens, features)), sds((kv_features // HEAD, tokens, heads * HEAD * tokens // kv_features)), sds((2 * rank + 8, tokens))),
        (sec, document_ids, query, policy_memory, rows, adapter, down, adapter_up),
        smem=(0,),
        cost_estimate=pl.CostEstimate(flops=150_000_000, bytes_accessed=3_000_000, transcendentals=150_000),
    )
    parts = (part,) + tuple(
        lax.ppermute(part, "mp", [(i, (i + k) % n_mp) for i in range(n_mp)]) for k in range(1, n_mp)
    )
    scorer = pl.pallas_call(
        scorer_kernel,
        grid=(n_sec,),
        out_shape=sds((n_sec, tokens, features)),
        in_specs=[
            pl.BlockSpec((None, 1, tokens), lambda j: (j, 0, 0)),
            pl.BlockSpec((None, None, None, tokens, features), lambda j: (0, j, 0, 0, 0)),
            pl.BlockSpec((None, None, None, None, tokens, kv_features), lambda j: (0, 0, j, 0, 0, 0)),
            pl.BlockSpec((None, None, None, None, tokens, kv_features), lambda j: (0, 1, j, 0, 0, 0)),
            pl.BlockSpec(memory_space=pl.ANY),
        ],
        out_specs=pl.BlockSpec((None, tokens, features), lambda j: (j, 0, 0)),
        compiler_params=pltpu.CompilerParams(vmem_limit_bytes=16 * 2**20),
        interpret=INTERPRET,
        cost_estimate=pl.CostEstimate(flops=300_000_000, bytes_accessed=30_000_000, transcendentals=600_000),
    )
    scorer_att = scorer(document_ids, scorer_query, scorer_key_values, scorer_key_values, part)
    partials = call(score_kernel, sds((n_sec * n_mp, 1, tokens)), (sec, scorer_att) + held + (score_heads,),
                    smem=(0,),
                    cost_estimate=pl.CostEstimate(flops=2_000_000, bytes_accessed=3_000_000, transcendentals=0))
    got = exchange(partials, ("sec", "mp")).reshape(n_sec, n_mp, tokens)
    keep, low_out, own, send = call(
        weights_kernel,
        (sds((8, tokens)), sds((rank, tokens)), sds((2 * half + 8, HEAD)), sds((2 * half + 8, HEAD))),
        (sec, core, prompts, document_ids, got, attended, adapter) + parts,
        smem=(0, 1, 2),
        scratch=(pltpu.VMEM((n_core, 2 * half + 8, HEAD), F32),),
    )
    got = call(pair_kernel, sds((n_z, 2 * per + 16, HEAD), BF16), (own, swap(send, n_core)))
    got = exchange(got, "z")
    got = exchange(call(column_kernel, sds((n_y, 2 * per + 16, HEAD), BF16), (got,)), Y)
    got, moments = call(final_kernel, (sds((n_z, per, HEAD), BF16), sds((8, HEAD))), (got,))
    got = exchange(got, "z")
    got = got.reshape(blocks // n_core, rank, HEAD)
    down_grad, up_grad = call(place_kernel, (sds((rank, features)), sds((rank, width))),
                              (core, got, swap(got, n_core)), smem=(0,),
                              scratch=(pltpu.VMEM((blocks, rank, HEAD), BF16),))
    white, query_grad, memory_grad = call(
        backward_kernel,
        (sds((1, tokens)), sds((tokens, features), BF16), sds(policy_memory.shape, BF16)),
        (moments, keep, low_out, down, rows, probs, query, policy_memory),
        cost_estimate=pl.CostEstimate(flops=300_000_000, bytes_accessed=20_000_000, transcendentals=0),
    )
    return white, query_grad[None], memory_grad, down_grad.T, up_grad


def solution(mesh):
    devices = mesh.devices
    split = SPLIT if int(np.prod(SPLIT)) == devices.shape[1] else (1, devices.shape[1], 1)
    inner = Mesh(devices.reshape((devices.shape[0],) + split + (devices.shape[2],)), AXES)
    both = ("sec",) + DP

    return jax.shard_map(
        on_device,
        mesh=inner,
        in_specs=(
            P(both, None, "mp"),
            P(None, both, None, "mp"),
            P(both, None, "mp"),
            P(both, None, "mp"),
            P("mp", None),
            P(None, "mp"),
            P("sec", None, DP, None, "mp"),
            P("sec", None, None, DP, None, "mp"),
            P(None, "mp"),
            P(None, DP, None),
            P(None, DP, None),
        ),
        out_specs=(
            P(both, None),
            P(both, None, "mp"),
            P(None, both, None, "mp"),
            P("mp", None),
            P(None, "mp"),
        ),
        check_vma=False,
    )
```

time: 166 us -> 128 us (0.77)
  blocking collectives: 83.9 us -> 58.6 us
  Pallas kernels: 34.1 us -> 9.3 us
  starting transfers between devices: 34.2 us -> 42.1 us
  local copies, waits for them, and re-layouts: 3.26 us -> 7.45 us
    all_to_all x5 -> x3, blocking collectives: 83.9 us -> 58.6 us  [exchange(): return lax.all_to_all(x, axes, 0, 0, tiled=True)]
    pallas_call x8, Pallas kernels: 21.5 us -> 6.97 us  [call(): pl.pallas_call(kernel, out_shape=outs, in_specs=specs, out_specs=jax.tree...]
    pallas_call x1, Pallas kernels: 12.6 us -> 2.33 us  [on_device(): scorer(document_ids, scorer_query, scorer_key_values, scorer_key_values,...]
    ppermute x2, starting transfers between devices: 10.3 us -> 20.5 us  [swap(): return lax.ppermute(x, 'core', [(i, n - 1 - i) for i in range(n)])]
    unnamed x18 -> x34, local copies, waits for them, and re-layouts: 2.66 us -> 7.45 us
    all_to_all x1, starting transfers between devices: 5.92 us -> 3.49 us  [exchange(): return lax.all_to_all(x, axes, 0, 0, tiled=True)]
  transfers between devices with their start and end apart: 9 -> 9, of which waited for: 2 -> 2; matrix products, arithmetic and copies ran while one was open for 0% -> 0% of each run, Pallas kernels for 16% -> 5%
where the time goes in v3:
time: 128 us; the launch traced here: 127 us
  blocking collectives  58.6 us (46%)
  starting transfers between devices  42.1 us (33%)
  Pallas kernels  9.3 us (7%)
  waiting for transfers between devices  8.59 us (7%)
  local copies, waits for them, and re-layouts  7.45 us (6%)
    all_to_all x3, blocking collectives, exchange(): return lax.all_to_all(x, axes, 0, 0, tiled=True)  58.6 us
    ppermute x2, starting transfers between devices, swap(): return lax.ppermute(x, 'core', [(i, n - 1 - i) for i in range(n)])  20.5 us
    ppermute x3, starting transfers between devices, on_device(): lax.ppermute(part, 'mp', [(i, (i + k) % n_mp) for i in range(n_mp)])  10.8 us
    unnamed x34, local copies, waits for them, and re-layouts  7.45 us
    pallas_call x8, Pallas kernels, call(): pl.pallas_call(kernel, out_shape=outs, in_specs=specs, out_specs=jax.tree...  6.97 us
    all_to_all x1, waiting for transfers between devices, exchange(): return lax.all_to_all(x, axes, 0, 0, tiled=True)  6.67 us
    ppermute x1, starting transfers between devices, on_device(): lax.ppermute(rows, 'sec', [(3, 0), (0, 1)])  4.66 us
    all_to_all x1, starting transfers between devices, exchange(): return lax.all_to_all(x, axes, 0, 0, tiled=True)  3.49 us
  transfers between devices with their start and end apart: 9, of which 2 were waited for; matrix products, arithmetic and copies ran while one was open for 0% of the time, Pallas kernels for 5%

profile of v3, /device:TPU:1, one launch (start us, length us, event | category | flops | bytes accessed | tf_op | source)
XLA Modules:
  0.0 126.9 jit_solution(10409573150989671547)
XLA Ops:
  0.6 1.3 %collective-permute-start = (bf16[128,1024]{1,0:T(8,128)(2,1)}, bf16[128,1024]{1,0:T(8,128)(2,1)S(1)}, u32[]{:S(2)}, u32[]{:S(2)}) collective-permute-start(bf16[128,1024]{1,0:T(8,128)(2,1)} %bitcast.10), channel_id=1, source_target_pairs={{192,0},{384,192},{193,1},{385,193},{194,2},{386,194},{195,3},{387... | collective-permute-start | bytes 786440 | tf_op jit(solution)/shard_map/ppermute | solution.py:402
  1.9 1.3 %collective-permute-start.1 = (bf16[128,1024]{1,0:T(8,128)(2,1)}, bf16[128,1024]{1,0:T(8,128)(2,1)S(1)}, u32[]{:S(2)}, u32[]{:S(2)}) collective-permute-start(bf16[128,1024]{1,0:T(8,128)(2,1)} %bitcast.11), channel_id=1, source_target_pairs={{384,0},{576,192},{385,1},{577,193},{386,2},{578,194},{387,3},{579... | collective-permute-start | bytes 786440 | tf_op jit(solution)/shard_map/ppermute | solution.py:403
  3.2 4.7 %collective-permute-start.2 = (bf16[128,1024]{1,0:T(8,128)(2,1)}, bf16[128,1024]{1,0:T(8,128)(2,1)S(1)}, u32[]{:S(2)}, u32[]{:S(2)}) collective-permute-start(bf16[128,1024]{1,0:T(8,128)(2,1)} %bitcast.12), channel_id=1, source_target_pairs={{576,0},{0,192},{577,1},{1,193},{578,2},{2,194},{579,3},{3,195},{5... | collective-permute-start | bytes 786440 | tf_op jit(solution)/shard_map/ppermute | solution.py:404
  7.9 0.0 copy-start
  7.9 0.9 copy-done
  8.9 0.0 copy-start.3
  8.9 1.0 copy-done.3
  9.9 0.0 copy-start.6
  9.9 0.9 copy-done.6
  10.8 0.0 copy-start.8
  10.9 0.9 copy-done.8
  11.8 0.0 copy-start.10
  11.8 0.9 copy-done.10
  12.7 0.0 copy-start.12
  12.7 0.9 copy-done.12
  13.6 0.0 copy-start.13
  13.6 0.7 copy-done.13
  14.3 0.0 copy-start.5
  14.3 0.0 copy-start.15
  14.3 1.2 shard_map.146
  15.5 0.0 copy-start.1
  15.5 3.4 %collective-permute-start.3 = (f32[136,128]{1,0:T(8,128)S(1)}, f32[136,128]{1,0:T(8,128)S(1)}, u32[]{:S(2)}, u32[]{:S(2)}) collective-permute-start(f32[136,128]{1,0:T(8,128)S(1)} %get-tuple-element.19.after_ref.part0), channel_id=1, source_target_pairs={{0,1},{1,2},{2,3},{3,0},{4,5},{5,6},{6,7},{7,4},{8,9},{9,10},{10,1... | collective-permute-start | bytes 208904 | tf_op jit(solution)/shard_map/ppermute | solution.py:414
  18.9 4.4 %collective-permute-start.4 = (f32[136,128]{1,0:T(8,128)S(1)}, f32[136,128]{1,0:T(8,128)S(1)}, u32[]{:S(2)}, u32[]{:S(2)}) collective-permute-start(f32[136,128]{1,0:T(8,128)S(1)} %get-tuple-element.19.after_ref.part0), channel_id=1, source_target_pairs={{0,2},{1,3},{2,0},{3,1},{4,6},{5,7},{6,4},{7,5},{8,10},{9,11},{10,... | collective-permute-start | bytes 208904 | tf_op jit(solution)/shard_map/ppermute | solution.py:414
  23.3 0.0 collective-permute-done.next_ref
  23.3 3.1 %collective-permute-start.5 = (f32[136,128]{1,0:T(8,128)S(1)}, f32[136,128]{1,0:T(8,128)S(1)}, u32[]{:S(2)}, u32[]{:S(2)}) collective-permute-start(f32[136,128]{1,0:T(8,128)S(1)} %get-tuple-element.19.after_ref.part0), channel_id=1, source_target_pairs={{0,3},{1,0},{2,1},{3,2},{4,7},{5,4},{6,5},{7,6},{8,11},{9,8},{10,9... | collective-permute-start | bytes 208904 | tf_op jit(solution)/shard_map/ppermute | solution.py:414
  26.3 0.0 copy-done.5
  26.3 0.0 copy-start.2
  26.4 1.0 copy-done.2
  27.4 2.3 %shard_map.147.att_ref = f32[4,128,1024]{2,1,0:T(8,128)S(1)} custom-call(s32[4,1,128]{2,1,0:T(1,128)S(1)} %copy-done.13, bf16[1,4,1,128,1024]{4,3,2,1,0:T(8,128)(2,1)S(1)} %copy-done.5, bf16[1,2,4,1,128,256]{5,4,3,2,1,0:T(8,128)(2,1)S(1)} %copy-done.2, bf16[1,2,4,1,128,256]{5,4,3,2,1,0:T(8,128)(2,1)S(1)} %copy-done.2, ...), custom_call_target="tpu_custom_call" | custom-call | flops 300000000 | bytes 30000000 | tf_op jit(solution)/shard_map/pallas_call | solution.py:432
  29.7 0.0 copy-start.4
  29.7 0.0 copy-start.14
  29.8 0.0 copy-start.16
  29.8 0.0 collective-permute-done.1.after_ref
  29.8 0.0 collective-permute-done.2.last_ref
  29.8 0.0 copy-done.15
  29.8 0.0 copy-done.1
  29.8 0.9 shard_map.148
  30.7 3.5 %all-to-all-start = ((f32[16,1,128]{2,1,0:T(1,128)}), f32[16,1,128]{2,1,0:T(1,128)S(1)}, u32[]{:S(2)}, u32[]{:S(2)}) async-start(f32[16,1,128]{2,1,0:T(1,128)} %shard_map.148), calls=%async_computation | async-start | bytes 16384 | tf_op jit(solution)/shard_map/all_to_all | solution.py:372
  34.2 0.0 collective-permute-done.3.part1
  34.2 0.0 collective-permute-done.4.part2
  34.2 0.0 collective-permute-done.5.part3
  34.2 6.7 %all-to-all-done = f32[16,1,128]{2,1,0:T(1,128)S(1)} async-done(((f32[16,1,128]{2,1,0:T(1,128)}), f32[16,1,128]{2,1,0:T(1,128)S(1)}, u32[]{:S(2)}, u32[]{:S(2)}) %all-to-all-start) | async-done | bytes 8224 | tf_op jit(solution)/shard_map/all_to_all | solution.py:372
  40.9 0.0 copy-done.4
  40.9 0.0 copy-done.14
  40.9 0.0 copy-done.16
  40.9 1.5 %shard_map.149 = (f32[8,128]{1,0:T(8,128)S(1)}, f32[64,128]{1,0:T(8,128)S(1)}, f32[1544,128]{1,0:T(8,128)S(1)}, f32[1544,128]{1,0:T(8,128)S(1)}) custom-call(s32[1]{0:T(128)} %bitcast.sec_ref, s32[1]{0:T(128)} %bitcast.1.core_ref, s32[4,4]{1,0:T(4,128)S(1)} %bitcast.23, s32[4,1,128]{2,1,0:T(1,128)S(1)} %copy-done.14, f32[4,4,128]{2,1,0:T(4,128)S(1)} %bitcast.22, ...), custom_call_target="tpu_custom_call" | custom-call | tf_op jit(solution)/shard_map/pallas_call | solution.py:348
  42.5 14.3 %collective-permute-start.6 = (f32[1544,128]{1,0:T(8,128)S(1)}, f32[1544,128]{1,0:T(8,128)S(1)}, u32[]{:S(2)}, u32[]{:S(2)}) collective-permute-start(f32[1544,128]{1,0:T(8,128)S(1)} %get-tuple-element.22), channel_id=1, source_target_pairs={{0,4},{4,0},{1,5},{5,1},{2,6},{6,2},{3,7},{7,3},{8,12},{12,8},{9,1... | collective-permute-start | bytes 2371592 | tf_op jit(solution)/shard_map/ppermute | solution.py:376
  56.8 1.9 %collective-permute-done.6.got_ref = f32[1544,128]{1,0:T(8,128)S(1)} collective-permute-done((f32[1544,128]{1,0:T(8,128)S(1)}, f32[1544,128]{1,0:T(8,128)S(1)}, u32[]{:S(2)}, u32[]{:S(2)}) %collective-permute-start.6) | collective-permute-done | bytes 790560 | tf_op jit(solution)/shard_map/ppermute | solution.py:376
  58.7 0.0 copy-start.7
  58.7 0.0 copy-start.9
  58.7 0.0 copy-start.11
  58.7 0.1 shard_map.150
  58.8 26.0 %all_to_all.20.got_ref = bf16[12,144,128]{2,1,0:T(8,128)(2,1)S(1)} all-to-all(bf16[12,144,128]{2,1,0:T(8,128)(2,1)S(1)} %shard_map.150), channel_id=1, replica_groups=mesh['sec'=4,'yh'=2,'z'=12,'core'=2,'mp'=4] {'z'}, dimensions={0} | all-to-all | bytes 884736 | tf_op jit(solution)/shard_map/all_to_all | solution.py:372
  84.8 0.2 shard_map.151
  85.0 15.1 %all_to_all.21.got_ref = bf16[8,144,128]{2,1,0:T(8,128)(2,1)S(1)} all-to-all(bf16[8,144,128]{2,1,0:T(8,128)(2,1)S(1)} %shard_map.151), channel_id=1, replica_groups=mesh['sec'=4,'yh'=2,'z'=12,'core'=2,'mp'=4] {'sec','yh'}, dimensions={0} | all-to-all | bytes 589824 | tf_op jit(solution)/shard_map/all_to_all | solution.py:372
  100.1 0.2 shard_map.152
  100.3 17.5 %all_to_all.22.own_ref = bf16[12,64,128]{2,1,0:T(8,128)(2,1)S(1)} all-to-all(bf16[12,64,128]{2,1,0:T(8,128)(2,1)S(1)} %get-tuple-element.30), channel_id=1, replica_groups=mesh['sec'=4,'yh'=2,'z'=12,'core'=2,'mp'=4] {'z'}, dimensions={0} | all-to-all | bytes 393216 | tf_op jit(solution)/shard_map/all_to_all | solution.py:372
  117.8 6.2 %collective-permute-start.7 = (bf16[12,64,128]{2,1,0:T(8,128)(2,1)S(1)}, bf16[12,64,128]{2,1,0:T(8,128)(2,1)S(1)}, u32[]{:S(2)}, u32[]{:S(2)}) collective-permute-start(bf16[12,64,128]{2,1,0:T(8,128)(2,1)S(1)} %all_to_all.22.own_ref), channel_id=1, source_target_pairs={{0,4},{4,0},{1,5},{5,1},{2,6},{6,2},{3,7},{7,3},{8,12},{12,8},{9,1... | collective-permute-start | bytes 589832 | tf_op jit(solution)/shard_map/ppermute | solution.py:376
  124.0 0.0 copy-done.7
  124.0 0.0 copy-done.9
  124.0 0.0 copy-done.11
  124.0 2.0 %shard_map.153 = (f32[1,128]{1,0:T(1,128)}, bf16[128,1024]{1,0:T(8,128)(2,1)}, bf16[2,1,128,256]{3,2,1,0:T(8,128)(2,1)}) custom-call(f32[8,128]{1,0:T(8,128)S(1)} %get-tuple-element.23.moments_ref, f32[8,128]{1,0:T(8,128)S(1)} %get-tuple-element.24.keep_ref, f32[64,128]{1,0:T(8,128)S(1)} %get-tuple-element.25.low_ref, bf16[64,1024]{1,0:T(8,128)(2,1)S(1)} %bitcast.21, ...), custom_call_target="tpu_custom_call" | custom-call | flops 300000000 | bytes 20000000 | tf_op jit(solution)/shard_map/pallas_call | solution.py:348
  126.0 0.0 collective-permute-done.7.other_ref
  126.0 0.9 shard_map.154
Async XLA Ops:
  0.6 22.6 %collective-permute-start = (bf16[128,1024]{1,0:T(8,128)(2,1)}, bf16[128,1024]{1,0:T(8,128)(2,1)S(1)}, u32[]{:S(2)}, u32[]{:S(2)}) collective-permute-start(bf16[128,1024]{1,0:T(8,128)(2,1)} %bitcast.10), channel_id=1, source_target_pairs={{192,0},{384,192},{193,1},{385,193},{194,2},{386,194},{195,3},{387... | collective-permute-start | bytes 786440 | tf_op jit(solution)/shard_map/ppermute | solution.py:402
  1.9 27.8 %collective-permute-start.1 = (bf16[128,1024]{1,0:T(8,128)(2,1)}, bf16[128,1024]{1,0:T(8,128)(2,1)S(1)}, u32[]{:S(2)}, u32[]{:S(2)}) collective-permute-start(bf16[128,1024]{1,0:T(8,128)(2,1)} %bitcast.11), channel_id=1, source_target_pairs={{384,0},{576,192},{385,1},{577,193},{386,2},{578,194},{387,3},{579... | collective-permute-start | bytes 786440 | tf_op jit(solution)/shard_map/ppermute | solution.py:403
  3.2 26.6 %collective-permute-start.2 = (bf16[128,1024]{1,0:T(8,128)(2,1)}, bf16[128,1024]{1,0:T(8,128)(2,1)S(1)}, u32[]{:S(2)}, u32[]{:S(2)}) collective-permute-start(bf16[128,1024]{1,0:T(8,128)(2,1)} %bitcast.12), channel_id=1, source_target_pairs={{576,0},{0,192},{577,1},{1,193},{578,2},{2,194},{579,3},{3,195},{5... | collective-permute-start | bytes 786440 | tf_op jit(solution)/shard_map/ppermute | solution.py:404
  7.9 1.0 copy-start
  8.9 1.0 copy-start.3
  9.9 0.9 copy-start.6
  10.8 0.9 copy-start.8
  11.8 0.9 copy-start.10
  12.7 0.9 copy-start.12
  13.6 0.7 copy-start.13
  14.3 12.0 %copy-start.5 = (bf16[1,4,1,128,1024]{4,3,2,1,0:T(8,128)(2,1)S(1)}, bf16[1,4,1,128,1024]{4,3,2,1,0:T(8,128)(2,1)}, u32[]{:S(2)}) copy-start(bf16[1,4,1,128,1024]{4,3,2,1,0:T(8,128)(2,1)} %q_ref.1) | copy-start | bytes 3145732
  14.3 15.5 %copy-start.15 = (f32[2,1024]{1,0:T(2,128)S(1)}, f32[2,1024]{1,0:T(2,128)}, u32[]{:S(2)}) copy-start(f32[2,1024]{1,0:T(2,128)} %heads_ref.1) | copy-start | bytes 24580
  15.5 14.3 %copy-start.1 = (bf16[1,128,1024]{2,1,0:T(8,128)(2,1)S(1)}, bf16[1,128,1024]{2,1,0:T(8,128)(2,1)}, u32[]{:S(2)}) copy-start(bf16[1,128,1024]{2,1,0:T(8,128)(2,1)} %param.13) | copy-start | bytes 786436
  15.5 18.7 %collective-permute-start.3 = (f32[136,128]{1,0:T(8,128)S(1)}, f32[136,128]{1,0:T(8,128)S(1)}, u32[]{:S(2)}, u32[]{:S(2)}) collective-permute-start(f32[136,128]{1,0:T(8,128)S(1)} %get-tuple-element.19.after_ref.part0), channel_id=1, source_target_pairs={{0,1},{1,2},{2,3},{3,0},{4,5},{5,6},{6,7},{7,4},{8,9},{9,10},{10,1... | collective-permute-start | bytes 208904 | tf_op jit(solution)/shard_map/ppermute | solution.py:414
  18.9 15.3 %collective-permute-start.4 = (f32[136,128]{1,0:T(8,128)S(1)}, f32[136,128]{1,0:T(8,128)S(1)}, u32[]{:S(2)}, u32[]{:S(2)}) collective-permute-start(f32[136,128]{1,0:T(8,128)S(1)} %get-tuple-element.19.after_ref.part0), channel_id=1, source_target_pairs={{0,2},{1,3},{2,0},{3,1},{4,6},{5,7},{6,4},{7,5},{8,10},{9,11},{10,... | collective-permute-start | bytes 208904 | tf_op jit(solution)/shard_map/ppermute | solution.py:414
  23.3 11.0 %collective-permute-start.5 = (f32[136,128]{1,0:T(8,128)S(1)}, f32[136,128]{1,0:T(8,128)S(1)}, u32[]{:S(2)}, u32[]{:S(2)}) collective-permute-start(f32[136,128]{1,0:T(8,128)S(1)} %get-tuple-element.19.after_ref.part0), channel_id=1, source_target_pairs={{0,3},{1,0},{2,1},{3,2},{4,7},{5,4},{6,5},{7,6},{8,11},{9,8},{10,9... | collective-permute-start | bytes 208904 | tf_op jit(solution)/shard_map/ppermute | solution.py:414
  26.3 1.0 copy-start.2
  29.7 11.2 %copy-start.4 = (bf16[1,128,2048]{2,1,0:T(8,128)(2,1)S(1)}, bf16[1,128,2048]{2,1,0:T(8,128)(2,1)}, u32[]{:S(2)}) copy-start(bf16[1,128,2048]{2,1,0:T(8,128)(2,1)} %param.14) | copy-start | bytes 1572868
  29.7 11.2 %copy-start.14 = (s32[4,1,128]{2,1,0:T(1,128)S(1)}, s32[4,1,128]{2,1,0:T(1,128)}, u32[]{:S(2)}) copy-start(s32[4,1,128]{2,1,0:T(1,128)} %doc_ref.5) | copy-start | bytes 6148
  29.8 11.2 %copy-start.16 = (s32[4,1,4]{2,1,0:T(1,128)S(1)}, s32[4,1,4]{2,1,0:T(1,128)}, u32[]{:S(2)}) copy-start(s32[4,1,4]{2,1,0:T(1,128)} %param.21) | copy-start | bytes 196
  30.7 10.2 %all-to-all-start = ((f32[16,1,128]{2,1,0:T(1,128)}), f32[16,1,128]{2,1,0:T(1,128)S(1)}, u32[]{:S(2)}, u32[]{:S(2)}) async-start(f32[16,1,128]{2,1,0:T(1,128)} %shard_map.148), calls=%async_computation | async-start | bytes 16384 | tf_op jit(solution)/shard_map/all_to_all | solution.py:372
  42.5 16.2 %collective-permute-start.6 = (f32[1544,128]{1,0:T(8,128)S(1)}, f32[1544,128]{1,0:T(8,128)S(1)}, u32[]{:S(2)}, u32[]{:S(2)}) collective-permute-start(f32[1544,128]{1,0:T(8,128)S(1)} %get-tuple-element.22), channel_id=1, source_target_pairs={{0,4},{4,0},{1,5},{5,1},{2,6},{6,2},{3,7},{7,3},{8,12},{12,8},{9,1... | collective-permute-start | bytes 2371592 | tf_op jit(solution)/shard_map/ppermute | solution.py:376
  58.7 65.3 %copy-start.7 = (bf16[1,128,1024]{2,1,0:T(8,128)(2,1)S(1)}, bf16[1,128,1024]{2,1,0:T(8,128)(2,1)}, u32[]{:S(2)}) copy-start(bf16[1,128,1024]{2,1,0:T(8,128)(2,1)} %param.11) | copy-start | bytes 786436
  58.7 65.3 %copy-start.9 = (bf16[2,1,128,256]{3,2,1,0:T(8,128)(2,1)S(1)}, bf16[2,1,128,256]{3,2,1,0:T(8,128)(2,1)}, u32[]{:S(2)}) copy-start(bf16[2,1,128,256]{3,2,1,0:T(8,128)(2,1)} %memory_ref.3) | copy-start | bytes 393220
  58.7 65.3 %copy-start.11 = (bf16[1024,64]{0,1:T(8,128)(2,1)S(1)}, bf16[1024,64]{0,1:T(8,128)(2,1)}, u32[]{:S(2)}) copy-start(bf16[1024,64]{0,1:T(8,128)(2,1)} %param.15) | copy-start | bytes 393220
  117.8 8.2 %collective-permute-start.7 = (bf16[12,64,128]{2,1,0:T(8,128)(2,1)S(1)}, bf16[12,64,128]{2,1,0:T(8,128)(2,1)S(1)}, u32[]{:S(2)}, u32[]{:S(2)}) collective-permute-start(bf16[12,64,128]{2,1,0:T(8,128)(2,1)S(1)} %all_to_all.22.own_ref), channel_id=1, source_target_pairs={{0,4},{4,0},{1,5},{5,1},{2,6},{6,2},{3,7},{7,3},{8,12},{12,8},{9,1... | collective-permute-start | bytes 589832 | tf_op jit(solution)/shard_map/ppermute | solution.py:376

commit v4 on v3

--- a/solution.py
+++ b/solution.py
@@ -60,8 +60,7 @@
     return raised * (1.0 / jnp.sum(raised, axis=0, keepdims=True))
 
 
-def scorer_kernel(doc_ref, q_ref, k_ref, v_ref, after_ref, out_ref):
-    del after_ref
+def scorer_kernel(doc_ref, q_ref, k_ref, v_ref, out_ref, last_ref):
     n = q_ref.shape[0]
     groups = q_ref.shape[1] // k_ref.shape[1]
     kept = kept_of(doc_ref[...], groups)
@@ -73,37 +72,54 @@
             at = (group * groups + i) * HEAD
             out_ref[:, at:at + HEAD] = attended[i * n:(i + 1) * n]
 
-
-def score_kernel(sec_ref, att_ref, own_ref, next_ref, after_ref, last_ref, heads_ref, out_ref):
+    @pl.when(pl.program_id(0) == pl.num_programs(0) - 1)
+    def _():
+        last_ref[...] = out_ref[...].astype(BF16)
+
+
+def score_kernel(sec_ref, att_ref, own_ref, next_ref, other_ref, first_ref, second_ref, heads_ref, out_ref):
     sec = sec_ref[0]
     n_sec = att_ref.shape[0]
     copies = out_ref.shape[0] // n_sec
     n_heads = att_ref.shape[2] // HEAD
-    held = (own_ref, next_ref, after_ref, last_ref)
-
-    def put(weight):
-        for step in range(n_sec):
-            row = lax.rem(sec + step, n_sec)
-            total = None
-            for head in range(n_heads):
-                at = slice(head * HEAD, (head + 1) * HEAD)
-                term = att_ref[row, :, at] * weight(step, at)
-                total = term if total is None else total + term
-            score = jnp.sum(total.T, axis=0, keepdims=True)
-            for copy in range(copies):
-                out_ref[row * copies + copy] = score
+    late = n_sec - 1
+
+    def score(left, right):
+        total = None
+        for head in range(n_heads):
+            at = slice(head * HEAD, (head + 1) * HEAD)
+            term = left(at) * right(at)
+            total = term if total is None else total + term
+        return jnp.sum(total.T, axis=0, keepdims=True)
+
+    def put(row, index, value):
+        for copy in range(copies):
+            out_ref[row * copies + copy, index:index + 1] = value
+
+    out_ref[...] = jnp.zeros(out_ref.shape, F32)
 
     @pl.when(sec < 2)
     def _():
-        put(lambda step, at: held[step][:, at].astype(F32))
+        for held, row in ((own_ref, sec), (next_ref, sec + 1), (other_ref, 2 - 2 * sec)):
+            put(row, 0, score(lambda at: att_ref[row, :, at], lambda at: held[:, at].astype(F32)))
 
     @pl.when(sec >= 2)
     def _():
-        put(lambda step, at: jnp.where(sec == 2, heads_ref[0:1, at], heads_ref[1:2, at]))
-
-
-def policy_kernel(sec_ref, doc_ref, q_ref, memory_ref, rows_ref, adapter_ref, down_ref, up_ref,
+        def weight(at):
+            return jnp.where(sec == 2, heads_ref[0:1, at], heads_ref[1:2, at])
+
+        for row in range(n_sec):
+            put(row, 0, score(lambda at: att_ref[row, :, at], weight))
+
+    @pl.when(sec == late)
+    def _():
+        for index, held in ((1, first_ref), (2, second_ref)):
+            put(late, index, score(lambda at: held[:, at].astype(F32), lambda at: own_ref[:, at].astype(F32)))
+
+
+def policy_kernel(sec_ref, doc_ref, q_ref, memory_ref, rows_ref, adapter_ref, down_ref, up_ref, after_ref,
                   att_ref, probs_ref, part_ref):
+    del after_ref
     k_ref, v_ref = memory_ref.at[0, 0], memory_ref.at[1, 0]
     n = q_ref.shape[0]
     groups = q_ref.shape[1] // k_ref.shape[1]
@@ -157,7 +173,10 @@
     closing = jnp.where(position == ending, 1.0, 0.0)
 
     def section(index):
-        return jnp.sum(got_ref[index], axis=0, keepdims=True)
+        total = jnp.sum(got_ref[index, :, 0, :], axis=0, keepdims=True)
+        if index < 2:
+            total = total + jnp.sum(got_ref[3, :, index + 1, :], axis=0, keepdims=True)
+        return total
 
     old, ref, reward, value = section(0), section(1), section(2), section(3)
     next_value = jnp.where(position < n - 1.0, pltpu.roll(value, n - 1, 1), 0.0) * (1.0 - closing)
@@ -368,6 +387,15 @@
 Y = ("sec", "yh")
 
 
+def in_hbm(x):
+    return x if INTERPRET else pltpu.with_memory_space_constraint(x, pltpu.HBM)
+
+
+def full(x):
+    zeros = (0,) * len(x.shape)
+    return pl.BlockSpec(x.shape, lambda i: zeros)
+
+
 def exchange(x, axes):
     return lax.all_to_all(x, axes, 0, 0, tiled=True)
 
@@ -397,43 +425,51 @@
     half = blocks // n_core * rank
     per = half // n_z
 
-    held = (
-        rows,
-        lax.ppermute(rows, "sec", [(1, 0), (2, 1)]),
-        lax.ppermute(rows, "sec", [(2, 0), (3, 1)]),
-        lax.ppermute(rows, "sec", [(3, 0), (0, 1)]),
-    )
-    attended, probs, part = call(
-        policy_kernel,
-        (sds((tokens, features)), sds((kv_features // HEAD, tokens, heads * HEAD * tokens // kv_features)), sds((2 * rank + 8, tokens))),
-        (sec, document_ids, query, policy_memory, rows, adapter, down, adapter_up),
-        smem=(0,),
-        cost_estimate=pl.CostEstimate(flops=150_000_000, bytes_accessed=3_000_000, transcendentals=150_000),
-    )
-    parts = (part,) + tuple(
-        lax.ppermute(part, "mp", [(i, (i + k) % n_mp) for i in range(n_mp)]) for k in range(1, n_mp)
-    )
+    below = lax.ppermute(rows, "sec", [(1, 0), (2, 1)])
+    other = lax.ppermute(rows, "sec", [(2, 0), (0, 1)])
     scorer = pl.pallas_call(
         scorer_kernel,
         grid=(n_sec,),
-        out_shape=sds((n_sec, tokens, features)),
+        out_shape=(sds((n_sec, tokens, features)), sds((tokens, features), BF16)),
         in_specs=[
             pl.BlockSpec((None, 1, tokens), lambda j: (j, 0, 0)),
             pl.BlockSpec((None, None, None, tokens, features), lambda j: (0, j, 0, 0, 0)),
             pl.BlockSpec((None, None, None, None, tokens, kv_features), lambda j: (0, 0, j, 0, 0, 0)),
             pl.BlockSpec((None, None, None, None, tokens, kv_features), lambda j: (0, 1, j, 0, 0, 0)),
-            pl.BlockSpec(memory_space=pl.ANY),
         ],
-        out_specs=pl.BlockSpec((None, tokens, features), lambda j: (j, 0, 0)),
+        out_specs=(
+            pl.BlockSpec((None, tokens, features), lambda j: (j, 0, 0)),
+            pl.BlockSpec((tokens, features), lambda j: (0, 0)),
+        ),
         compiler_params=pltpu.CompilerParams(vmem_limit_bytes=16 * 2**20),
         interpret=INTERPRET,
-        cost_estimate=pl.CostEstimate(flops=300_000_000, bytes_accessed=30_000_000, transcendentals=600_000),
+        cost_estimate=pl.CostEstimate(flops=300_000_000, bytes_accessed=8_000_000, transcendentals=600_000),
     )
-    scorer_att = scorer(document_ids, scorer_query, scorer_key_values, scorer_key_values, part)
-    partials = call(score_kernel, sds((n_sec * n_mp, 1, tokens)), (sec, scorer_att) + held + (score_heads,),
-                    smem=(0,),
+    pairs = in_hbm(scorer_key_values)
+    scorer_att, last = scorer(in_hbm(document_ids), in_hbm(scorer_query), pairs, pairs)
+    first = lax.ppermute(last, "sec", [(0, 3)])
+    second = lax.ppermute(last, "sec", [(1, 3)])
+    held = (document_ids, query, policy_memory, rows, adapter, down, adapter_up)
+    groups = heads * HEAD // kv_features
+    results = (sds((tokens, features)), sds((heads // groups, tokens, groups * tokens)), sds((2 * rank + 8, tokens)))
+    policy = pl.pallas_call(
+        policy_kernel,
+        grid=(1,),
+        out_shape=results,
+        in_specs=[pl.BlockSpec(memory_space=pltpu.SMEM)] + [full(x) for x in held] + [pl.BlockSpec(memory_space=pl.ANY)],
+        out_specs=tuple(full(x) for x in results),
+        compiler_params=pltpu.CompilerParams(vmem_limit_bytes=16 * 2**20),
+        interpret=INTERPRET,
+        cost_estimate=pl.CostEstimate(flops=150_000_000, bytes_accessed=4_000_000, transcendentals=150_000),
+    )
+    attended, probs, part = policy(sec, *map(in_hbm, held), last)
+    parts = (part,) + tuple(
+        lax.ppermute(part, "mp", [(i, (i + k) % n_mp) for i in range(n_mp)]) for k in range(1, n_mp)
+    )
+    partials = call(score_kernel, sds((n_sec * n_mp, 4, tokens)),
+                    (sec, scorer_att, rows, below, other, first, second, score_heads), smem=(0,),
                     cost_estimate=pl.CostEstimate(flops=2_000_000, bytes_accessed=3_000_000, transcendentals=0))
-    got = exchange(partials, ("sec", "mp")).reshape(n_sec, n_mp, tokens)
+    got = exchange(partials, ("sec", "mp")).reshape(n_sec, n_mp, 4, tokens)
     keep, low_out, own, send = call(
         weights_kernel,
         (sds((8, tokens)), sds((rank, tokens)), sds((2 * half + 8, HEAD)), sds((2 * half + 8, HEAD))),

time: 128 us -> 128 us (level)
  local copies, waits for them, and re-layouts: 7.45 us -> 1.52 us
  Pallas kernels: 9.3 us -> 14.3 us
    unnamed x34 -> x20, local copies, waits for them, and re-layouts: 7.45 us -> 1.52 us
    pallas_call x1 -> x2, Pallas kernels: 2.33 us -> 7 us  [the longest x1 4.46 us: on_device(): scorer(in_hbm(document_ids), in_hbm(scorer_query), pairs, pairs)]
    ppermute x3 -> x4, starting transfers between devices: 7.24 us -> 10.9 us  [the longest x1 4.16 us: on_device(): other = lax.ppermute(rows, 'sec', [(2, 0), (0, 1)])]
    ppermute x2, starting transfers between devices: 20.5 us -> 19.1 us  [swap(): return lax.ppermute(x, 'core', [(i, n - 1 - i) for i in range(n)])]
    ppermute x3, starting transfers between devices: 10.8 us -> 9.45 us  [on_device(): lax.ppermute(part, 'mp', [(i, (i + k) % n_mp) for i in range(n_mp)])]
    pallas_call x8 -> x7, Pallas kernels: 6.97 us -> 7.3 us  [call(): pl.pallas_call(kernel, out_shape=outs, in_specs=specs, out_specs=jax.tree...]
  transfers between devices with their start and end apart: 9 -> 10, of which waited for: 2 -> 2; matrix products, arithmetic and copies ran while one was open for 0% -> 0% of each run, Pallas kernels for 5% -> 9%
where the time goes in v4:
time: 128 us
  blocking collectives  59.2 us (46%)
  starting transfers between devices  42.9 us (34%)
  Pallas kernels  14.3 us (11%)
  waiting for transfers between devices  8.87 us (7%)
  local copies, waits for them, and re-layouts  1.52 us (1%)
    all_to_all x3, blocking collectives, exchange(): return lax.all_to_all(x, axes, 0, 0, tiled=True)  59.2 us
    ppermute x2, starting transfers between devices, swap(): return lax.ppermute(x, 'core', [(i, n - 1 - i) for i in range(n)])  19.1 us
    ppermute x3, starting transfers between devices, on_device(): lax.ppermute(part, 'mp', [(i, (i + k) % n_mp) for i in range(n_mp)])  9.45 us
    pallas_call x7, Pallas kernels, call(): pl.pallas_call(kernel, out_shape=outs, in_specs=specs, out_specs=jax.tree...  7.3 us
    all_to_all x1, waiting for transfers between devices, exchange(): return lax.all_to_all(x, axes, 0, 0, tiled=True)  6.95 us
    pallas_call x1, Pallas kernels, on_device(): scorer(in_hbm(document_ids), in_hbm(scorer_query), pairs, pairs)  4.46 us
    ppermute x1, starting transfers between devices, on_device(): other = lax.ppermute(rows, 'sec', [(2, 0), (0, 1)])  4.16 us
    ppermute x1, starting transfers between devices, on_device(): first = lax.ppermute(last, 'sec', [(0, 3)])  4.05 us
  transfers between devices with their start and end apart: 10, of which 2 were waited for; matrix products, arithmetic and copies ran while one was open for 0% of the time, Pallas kernels for 9%

profile of v4, /device:TPU:1, one launch (start us, length us, event | category | flops | bytes accessed | tf_op | source)
XLA Modules:
  0.0 127.6 jit_solution(15015385529552651453)
XLA Ops:
  0.6 0.0 copy-start
  0.6 4.2 %collective-permute-start.1 = (bf16[128,1024]{1,0:T(8,128)(2,1)}, bf16[128,1024]{1,0:T(8,128)(2,1)}, u32[]{:S(2)}, u32[]{:S(2)}) collective-permute-start(bf16[128,1024]{1,0:T(8,128)(2,1)} %bitcast.10), channel_id=1, source_target_pairs={{384,0},{0,192},{385,1},{1,193},{386,2},{2,194},{387,3},{3,195},{3... | collective-permute-start | bytes 786440 | tf_op jit(solution)/shard_map/ppermute | solution.py:429
  4.8 1.3 %collective-permute-start = (bf16[128,1024]{1,0:T(8,128)(2,1)}, bf16[128,1024]{1,0:T(8,128)(2,1)}, u32[]{:S(2)}, u32[]{:S(2)}) collective-permute-start(bf16[128,1024]{1,0:T(8,128)(2,1)} %bitcast.11), channel_id=1, source_target_pairs={{192,0},{384,192},{193,1},{385,193},{194,2},{386,194},{195,3},{387... | collective-permute-start | bytes 786440 | tf_op jit(solution)/shard_map/ppermute | solution.py:428
  6.1 4.5 %shard_map.146 = (f32[4,128,1024]{2,1,0:T(8,128)S(1)}, bf16[128,1024]{1,0:T(8,128)(2,1)}) custom-call(s32[4,1,128]{2,1,0:T(1,128)} %doc_ref.5, bf16[1,4,1,128,1024]{4,3,2,1,0:T(8,128)(2,1)} %q_ref.1, bf16[1,2,4,1,128,256]{5,4,3,2,1,0:T(8,128)(2,1)} %v_ref.1, bf16[1,2,4,1,128,256]{5,4,3,2,1,0:T(8,128)(2,1)} %v_ref.1), custom_call_target="tpu_custom_call" | custom-call | flops 300000000 | bytes 8000000 | tf_op jit(solution)/shard_map/pallas_call | solution.py:449
  10.6 1.4 %collective-permute-start.3 = (bf16[128,1024]{1,0:T(8,128)(2,1)}, bf16[128,1024]{1,0:T(8,128)(2,1)}, u32[]{:S(2)}, u32[]{:S(2)}) collective-permute-start(bf16[128,1024]{1,0:T(8,128)(2,1)} %get-tuple-element.22.after_ref), channel_id=1, source_target_pairs={{192,576},{193,577},{194,578},{195,579},{196,580},{197,581},{198,5... | collective-permute-start | bytes 786440 | tf_op jit(solution)/shard_map/ppermute | solution.py:451
  11.9 4.0 %collective-permute-start.2 = (bf16[128,1024]{1,0:T(8,128)(2,1)}, bf16[128,1024]{1,0:T(8,128)(2,1)}, u32[]{:S(2)}, u32[]{:S(2)}) collective-permute-start(bf16[128,1024]{1,0:T(8,128)(2,1)} %get-tuple-element.22.after_ref), channel_id=1, source_target_pairs={{0,576},{1,577},{2,578},{3,579},{4,580},{5,581},{6,582},{7,583},{8... | collective-permute-start | bytes 786440 | tf_op jit(solution)/shard_map/ppermute | solution.py:450
  16.0 0.0 copy-start.9
  16.0 2.5 %shard_map.148 = (f32[128,1024]{1,0:T(8,128)S(1)}, f32[2,128,512]{2,1,0:T(8,128)S(1)}, f32[136,128]{1,0:T(8,128)S(1)}) custom-call(s32[1]{0:T(128)} %bitcast.sec_ref, s32[4,1,128]{2,1,0:T(1,128)} %doc_ref.5, bf16[128,1024]{1,0:T(8,128)(2,1)} %bitcast.17, bf16[2,1,128,256]{3,2,1,0:T(8,128)(2,1)} %memory_ref.3, bf16[128,1024]{1,0:T(8,128)(2,1)} %bitcast.12, ...), custom_call_target="tpu_custom_call" | custom-call | flops 150000000 | bytes 4000000 | tf_op jit(solution)/shard_map/pallas_call | solution.py:465
  18.5 0.0 copy-start.3
  18.5 0.8 copy-done.3
  19.3 0.0 copy-start.1
  19.3 0.0 copy-start.7
  19.3 4.5 %collective-permute-start.6 = (f32[136,128]{1,0:T(8,128)S(1)}, f32[136,128]{1,0:T(8,128)S(1)}, u32[]{:S(2)}, u32[]{:S(2)}) collective-permute-start(f32[136,128]{1,0:T(8,128)S(1)} %get-tuple-element.24.part0), channel_id=1, source_target_pairs={{0,3},{1,0},{2,1},{3,2},{4,7},{5,4},{6,5},{7,6},{8,11},{9,8},{10,9... | collective-permute-start | bytes 208904 | tf_op jit(solution)/shard_map/ppermute | solution.py:467
  23.8 0.0 collective-permute-done.1.other_ref
  23.9 2.4 %collective-permute-start.5 = (f32[136,128]{1,0:T(8,128)S(1)}, f32[136,128]{1,0:T(8,128)}, u32[]{:S(2)}, u32[]{:S(2)}) collective-permute-start(f32[136,128]{1,0:T(8,128)S(1)} %get-tuple-element.24.part0), channel_id=1, source_target_pairs={{0,2},{1,3},{2,0},{3,1},{4,6},{5,7},{6,4},{7,5},{8,10},{9,11},{10,... | collective-permute-start | bytes 208904 | tf_op jit(solution)/shard_map/ppermute | solution.py:467
  26.3 0.0 collective-permute-done.next_ref
  26.3 2.5 %collective-permute-start.4 = (f32[136,128]{1,0:T(8,128)S(1)}, f32[136,128]{1,0:T(8,128)}, u32[]{:S(2)}, u32[]{:S(2)}) collective-permute-start(f32[136,128]{1,0:T(8,128)S(1)} %get-tuple-element.24.part0), channel_id=1, source_target_pairs={{0,1},{1,2},{2,3},{3,0},{4,5},{5,6},{6,7},{7,4},{8,9},{9,10},{10,1... | collective-permute-start | bytes 208904 | tf_op jit(solution)/shard_map/ppermute | solution.py:467
  28.8 0.0 collective-permute-done.3.second_ref
  28.8 0.0 collective-permute-done.2.first_ref
  28.9 0.0 copy-done
  28.9 0.0 copy-start.8
  28.9 0.7 copy-done.8
  29.6 2.0 %shard_map.147 = f32[16,4,128]{2,1,0:T(4,128)} custom-call(s32[1]{0:T(128)} %bitcast.sec_ref, f32[4,128,1024]{2,1,0:T(8,128)S(1)} %get-tuple-element.21.att_ref, bf16[128,1024]{1,0:T(8,128)(2,1)S(1)} %bitcast.13, bf16[128,1024]{1,0:T(8,128)(2,1)} %collective-permute-done.next_ref, bf16[128,1024]{1,0:T(8,128)(2,1)} %collective-permute-done.1.other_ref, ...), custom_call_target="tpu_custom_call" | custom-call | flops 2000000 | bytes 3000000 | tf_op jit(solution)/shard_map/pallas_call | solution.py:367
  31.6 3.5 %all-to-all-start = ((f32[16,4,128]{2,1,0:T(4,128)}), f32[16,4,128]{2,1,0:T(4,128)S(1)}, u32[]{:S(2)}, u32[]{:S(2)}) async-start(f32[16,4,128]{2,1,0:T(4,128)} %shard_map.147), calls=%async_computation | async-start | bytes 65536 | tf_op jit(solution)/shard_map/all_to_all | solution.py:400
  35.1 0.0 collective-permute-done.6.part3
  35.1 0.0 collective-permute-done.5.part2
  35.1 0.0 collective-permute-done.4.part1
  35.2 6.9 %all-to-all-done = f32[16,4,128]{2,1,0:T(4,128)S(1)} async-done(((f32[16,4,128]{2,1,0:T(4,128)}), f32[16,4,128]{2,1,0:T(4,128)S(1)}, u32[]{:S(2)}, u32[]{:S(2)}) %all-to-all-start) | async-done | bytes 32800 | tf_op jit(solution)/shard_map/all_to_all | solution.py:400
  42.1 0.0 copy-done.9
  42.1 0.0 copy-done.1
  42.1 0.0 copy-done.7
  42.1 1.9 %shard_map.149 = (f32[8,128]{1,0:T(8,128)S(1)}, f32[64,128]{1,0:T(8,128)S(1)}, f32[1544,128]{1,0:T(8,128)S(1)}, f32[1544,128]{1,0:T(8,128)S(1)}) custom-call(s32[1]{0:T(128)} %bitcast.sec_ref, s32[1]{0:T(128)} %bitcast.1.core_ref, s32[4,4]{1,0:T(4,128)S(1)} %bitcast.22, s32[4,1,128]{2,1,0:T(1,128)S(1)} %copy-done.7, f32[4,4,4,128]{3,2,1,0:T(4,128)S(1)} %bitcast.21, ...), custom_call_target="tpu_custom_call" | custom-call | tf_op jit(solution)/shard_map/pallas_call | solution.py:367
  44.0 12.9 %collective-permute-start.7 = (f32[1544,128]{1,0:T(8,128)S(1)}, f32[1544,128]{1,0:T(8,128)S(1)}, u32[]{:S(2)}, u32[]{:S(2)}) collective-permute-start(f32[1544,128]{1,0:T(8,128)S(1)} %get-tuple-element.26), channel_id=1, source_target_pairs={{0,4},{4,0},{1,5},{5,1},{2,6},{6,2},{3,7},{7,3},{8,12},{12,8},{9,1... | collective-permute-start | bytes 2371592 | tf_op jit(solution)/shard_map/ppermute | solution.py:404
  56.9 1.9 %collective-permute-done.7.got_ref = f32[1544,128]{1,0:T(8,128)S(1)} collective-permute-done((f32[1544,128]{1,0:T(8,128)S(1)}, f32[1544,128]{1,0:T(8,128)S(1)}, u32[]{:S(2)}, u32[]{:S(2)}) %collective-permute-start.7) | collective-permute-done | bytes 790560 | tf_op jit(solution)/shard_map/ppermute | solution.py:404
  58.8 0.0 copy-start.2
  58.8 0.0 copy-start.4
  58.8 0.0 copy-start.5
  58.8 0.0 copy-start.6
  58.8 0.1 shard_map.150
  58.9 26.8 %all_to_all.20.got_ref = bf16[12,144,128]{2,1,0:T(8,128)(2,1)S(1)} all-to-all(bf16[12,144,128]{2,1,0:T(8,128)(2,1)S(1)} %shard_map.150), channel_id=1, replica_groups=mesh['sec'=4,'yh'=2,'z'=12,'core'=2,'mp'=4] {'z'}, dimensions={0} | all-to-all | bytes 884736 | tf_op jit(solution)/shard_map/all_to_all | solution.py:400
  85.7 0.2 shard_map.151
  85.9 14.9 %all_to_all.21.got_ref = bf16[8,144,128]{2,1,0:T(8,128)(2,1)S(1)} all-to-all(bf16[8,144,128]{2,1,0:T(8,128)(2,1)S(1)} %shard_map.151), channel_id=1, replica_groups=mesh['sec'=4,'yh'=2,'z'=12,'core'=2,'mp'=4] {'sec','yh'}, dimensions={0} | all-to-all | bytes 589824 | tf_op jit(solution)/shard_map/all_to_all | solution.py:400
  100.8 0.2 shard_map.152
  100.9 17.5 %all_to_all.22.own_ref = bf16[12,64,128]{2,1,0:T(8,128)(2,1)S(1)} all-to-all(bf16[12,64,128]{2,1,0:T(8,128)(2,1)S(1)} %get-tuple-element.34), channel_id=1, replica_groups=mesh['sec'=4,'yh'=2,'z'=12,'core'=2,'mp'=4] {'z'}, dimensions={0} | all-to-all | bytes 393216 | tf_op jit(solution)/shard_map/all_to_all | solution.py:400
  118.4 6.2 %collective-permute-start.8 = (bf16[12,64,128]{2,1,0:T(8,128)(2,1)S(1)}, bf16[12,64,128]{2,1,0:T(8,128)(2,1)S(1)}, u32[]{:S(2)}, u32[]{:S(2)}) collective-permute-start(bf16[12,64,128]{2,1,0:T(8,128)(2,1)S(1)} %all_to_all.22.own_ref), channel_id=1, source_target_pairs={{0,4},{4,0},{1,5},{5,1},{2,6},{6,2},{3,7},{7,3},{8,12},{12,8},{9,1... | collective-permute-start | bytes 589832 | tf_op jit(solution)/shard_map/ppermute | solution.py:404
  124.7 0.0 copy-done.2
  124.7 0.0 copy-done.4
  124.7 0.0 copy-done.5
  124.7 0.0 copy-done.6
  124.7 2.0 %shard_map.153 = (f32[1,128]{1,0:T(1,128)}, bf16[128,1024]{1,0:T(8,128)(2,1)}, bf16[2,1,128,256]{3,2,1,0:T(8,128)(2,1)}) custom-call(f32[8,128]{1,0:T(8,128)S(1)} %get-tuple-element.27.moments_ref, f32[8,128]{1,0:T(8,128)S(1)} %get-tuple-element.28.keep_ref, f32[64,128]{1,0:T(8,128)S(1)} %get-tuple-element.29.low_ref, bf16[64,1024]{1,0:T(8,128)(2,1)S(1)} %bitcast.20, ...), custom_call_target="tpu_custom_call" | custom-call | flops 300000000 | bytes 20000000 | tf_op jit(solution)/shard_map/pallas_call | solution.py:367
  126.7 0.0 collective-permute-done.8.other_ref
  126.7 0.9 shard_map.154
Async XLA Ops:
  0.6 28.2 %copy-start = (bf16[1,128,1024]{2,1,0:T(8,128)(2,1)S(1)}, bf16[1,128,1024]{2,1,0:T(8,128)(2,1)}, u32[]{:S(2)}) copy-start(bf16[1,128,1024]{2,1,0:T(8,128)(2,1)} %param.13) | copy-start | bytes 786436
  0.6 23.2 %collective-permute-start.1 = (bf16[128,1024]{1,0:T(8,128)(2,1)}, bf16[128,1024]{1,0:T(8,128)(2,1)}, u32[]{:S(2)}, u32[]{:S(2)}) collective-permute-start(bf16[128,1024]{1,0:T(8,128)(2,1)} %bitcast.10), channel_id=1, source_target_pairs={{384,0},{0,192},{385,1},{1,193},{386,2},{2,194},{387,3},{3,195},{3... | collective-permute-start | bytes 786440 | tf_op jit(solution)/shard_map/ppermute | solution.py:429
  4.8 21.5 %collective-permute-start = (bf16[128,1024]{1,0:T(8,128)(2,1)}, bf16[128,1024]{1,0:T(8,128)(2,1)}, u32[]{:S(2)}, u32[]{:S(2)}) collective-permute-start(bf16[128,1024]{1,0:T(8,128)(2,1)} %bitcast.11), channel_id=1, source_target_pairs={{192,0},{384,192},{193,1},{385,193},{194,2},{386,194},{195,3},{387... | collective-permute-start | bytes 786440 | tf_op jit(solution)/shard_map/ppermute | solution.py:428
  10.6 18.3 %collective-permute-start.3 = (bf16[128,1024]{1,0:T(8,128)(2,1)}, bf16[128,1024]{1,0:T(8,128)(2,1)}, u32[]{:S(2)}, u32[]{:S(2)}) collective-permute-start(bf16[128,1024]{1,0:T(8,128)(2,1)} %get-tuple-element.22.after_ref), channel_id=1, source_target_pairs={{192,576},{193,577},{194,578},{195,579},{196,580},{197,581},{198,5... | collective-permute-start | bytes 786440 | tf_op jit(solution)/shard_map/ppermute | solution.py:451
  11.9 16.9 %collective-permute-start.2 = (bf16[128,1024]{1,0:T(8,128)(2,1)}, bf16[128,1024]{1,0:T(8,128)(2,1)}, u32[]{:S(2)}, u32[]{:S(2)}) collective-permute-start(bf16[128,1024]{1,0:T(8,128)(2,1)} %get-tuple-element.22.after_ref), channel_id=1, source_target_pairs={{0,576},{1,577},{2,578},{3,579},{4,580},{5,581},{6,582},{7,583},{8... | collective-permute-start | bytes 786440 | tf_op jit(solution)/shard_map/ppermute | solution.py:450
  16.0 26.1 %copy-start.9 = (s32[4,1,4]{2,1,0:T(1,128)S(1)}, s32[4,1,4]{2,1,0:T(1,128)}, u32[]{:S(2)}) copy-start(s32[4,1,4]{2,1,0:T(1,128)} %param.21) | copy-start | bytes 196
  18.5 0.8 copy-start.3
  19.3 22.8 %copy-start.1 = (bf16[1,128,2048]{2,1,0:T(8,128)(2,1)S(1)}, bf16[1,128,2048]{2,1,0:T(8,128)(2,1)}, u32[]{:S(2)}) copy-start(bf16[1,128,2048]{2,1,0:T(8,128)(2,1)} %param.14) | copy-start | bytes 1572868
  19.3 22.8 %copy-start.7 = (s32[4,1,128]{2,1,0:T(1,128)S(1)}, s32[4,1,128]{2,1,0:T(1,128)}, u32[]{:S(2)}) copy-start(s32[4,1,128]{2,1,0:T(1,128)} %doc_ref.5) | copy-start | bytes 6148
  19.3 15.8 %collective-permute-start.6 = (f32[136,128]{1,0:T(8,128)S(1)}, f32[136,128]{1,0:T(8,128)S(1)}, u32[]{:S(2)}, u32[]{:S(2)}) collective-permute-start(f32[136,128]{1,0:T(8,128)S(1)} %get-tuple-element.24.part0), channel_id=1, source_target_pairs={{0,3},{1,0},{2,1},{3,2},{4,7},{5,4},{6,5},{7,6},{8,11},{9,8},{10,9... | collective-permute-start | bytes 208904 | tf_op jit(solution)/shard_map/ppermute | solution.py:467
  23.9 11.3 %collective-permute-start.5 = (f32[136,128]{1,0:T(8,128)S(1)}, f32[136,128]{1,0:T(8,128)}, u32[]{:S(2)}, u32[]{:S(2)}) collective-permute-start(f32[136,128]{1,0:T(8,128)S(1)} %get-tuple-element.24.part0), channel_id=1, source_target_pairs={{0,2},{1,3},{2,0},{3,1},{4,6},{5,7},{6,4},{7,5},{8,10},{9,11},{10,... | collective-permute-start | bytes 208904 | tf_op jit(solution)/shard_map/ppermute | solution.py:467
  26.3 8.8 %collective-permute-start.4 = (f32[136,128]{1,0:T(8,128)S(1)}, f32[136,128]{1,0:T(8,128)}, u32[]{:S(2)}, u32[]{:S(2)}) collective-permute-start(f32[136,128]{1,0:T(8,128)S(1)} %get-tuple-element.24.part0), channel_id=1, source_target_pairs={{0,1},{1,2},{2,3},{3,0},{4,5},{5,6},{6,7},{7,4},{8,9},{9,10},{10,1... | collective-permute-start | bytes 208904 | tf_op jit(solution)/shard_map/ppermute | solution.py:467
  28.9 0.7 copy-start.8
  31.6 10.5 %all-to-all-start = ((f32[16,4,128]{2,1,0:T(4,128)}), f32[16,4,128]{2,1,0:T(4,128)S(1)}, u32[]{:S(2)}, u32[]{:S(2)}) async-start(f32[16,4,128]{2,1,0:T(4,128)} %shard_map.147), calls=%async_computation | async-start | bytes 65536 | tf_op jit(solution)/shard_map/all_to_all | solution.py:400
  44.0 14.8 %collective-permute-start.7 = (f32[1544,128]{1,0:T(8,128)S(1)}, f32[1544,128]{1,0:T(8,128)S(1)}, u32[]{:S(2)}, u32[]{:S(2)}) collective-permute-start(f32[1544,128]{1,0:T(8,128)S(1)} %get-tuple-element.26), channel_id=1, source_target_pairs={{0,4},{4,0},{1,5},{5,1},{2,6},{6,2},{3,7},{7,3},{8,12},{12,8},{9,1... | collective-permute-start | bytes 2371592 | tf_op jit(solution)/shard_map/ppermute | solution.py:404
  58.8 65.9 %copy-start.2 = (bf16[1,128,1024]{2,1,0:T(8,128)(2,1)S(1)}, bf16[1,128,1024]{2,1,0:T(8,128)(2,1)}, u32[]{:S(2)}) copy-start(bf16[1,128,1024]{2,1,0:T(8,128)(2,1)} %param.11) | copy-start | bytes 786436
  58.8 65.9 %copy-start.4 = (f32[2,128,512]{2,1,0:T(8,128)S(1)}, f32[2,128,512]{2,1,0:T(8,128)}, u32[]{:S(2)}) copy-start(f32[2,128,512]{2,1,0:T(8,128)} %copy-done.3) | copy-start | bytes 1572868
  58.8 65.9 %copy-start.5 = (bf16[2,1,128,256]{3,2,1,0:T(8,128)(2,1)S(1)}, bf16[2,1,128,256]{3,2,1,0:T(8,128)(2,1)}, u32[]{:S(2)}) copy-start(bf16[2,1,128,256]{3,2,1,0:T(8,128)(2,1)} %memory_ref.3) | copy-start | bytes 393220
  58.8 65.9 %copy-start.6 = (bf16[1024,64]{0,1:T(8,128)(2,1)S(1)}, bf16[1024,64]{0,1:T(8,128)(2,1)}, u32[]{:S(2)}) copy-start(bf16[1024,64]{0,1:T(8,128)(2,1)} %param.15) | copy-start | bytes 393220
  118.4 8.3 %collective-permute-start.8 = (bf16[12,64,128]{2,1,0:T(8,128)(2,1)S(1)}, bf16[12,64,128]{2,1,0:T(8,128)(2,1)S(1)}, u32[]{:S(2)}, u32[]{:S(2)}) collective-permute-start(bf16[12,64,128]{2,1,0:T(8,128)(2,1)S(1)} %all_to_all.22.own_ref), channel_id=1, source_target_pairs={{0,4},{4,0},{1,5},{5,1},{2,6},{6,2},{3,7},{7,3},{8,12},{12,8},{9,1... | collective-permute-start | bytes 589832 | tf_op jit(solution)/shard_map/ppermute | solution.py:404

commit v5 on v4

--- a/solution.py
+++ b/solution.py
@@ -60,7 +60,7 @@
     return raised * (1.0 / jnp.sum(raised, axis=0, keepdims=True))
 
 
-def scorer_kernel(doc_ref, q_ref, k_ref, v_ref, out_ref, last_ref):
+def scorer_kernel(doc_ref, q_ref, k_ref, v_ref, heads_ref, out_ref, last_ref, held_ref):
     n = q_ref.shape[0]
     groups = q_ref.shape[1] // k_ref.shape[1]
     kept = kept_of(doc_ref[...], groups)
@@ -75,9 +75,10 @@
     @pl.when(pl.program_id(0) == pl.num_programs(0) - 1)
     def _():
         last_ref[...] = out_ref[...].astype(BF16)
-
-
-def score_kernel(sec_ref, att_ref, own_ref, next_ref, other_ref, first_ref, second_ref, heads_ref, out_ref):
+        held_ref[...] = heads_ref[...]
+
+
+def score_kernel(sec_ref, att_ref, own_ref, next_ref, other_ref, up_ref, first_ref, heads_ref, out_ref):
     sec = sec_ref[0]
     n_sec = att_ref.shape[0]
     copies = out_ref.shape[0] // n_sec
@@ -100,8 +101,12 @@
 
     @pl.when(sec < 2)
     def _():
-        for held, row in ((own_ref, sec), (next_ref, sec + 1), (other_ref, 2 - 2 * sec)):
+        for held, row in ((own_ref, sec), (next_ref, sec + 1), (other_ref, sec + 2)):
             put(row, 0, score(lambda at: att_ref[row, :, at], lambda at: held[:, at].astype(F32)))
+
+    @pl.when(sec == 1)
+    def _():
+        put(0, 0, score(lambda at: att_ref[0, :, at], lambda at: up_ref[:, at].astype(F32)))
 
     @pl.when(sec >= 2)
     def _():
@@ -113,8 +118,7 @@
 
     @pl.when(sec == late)
     def _():
-        for index, held in ((1, first_ref), (2, second_ref)):
-            put(late, index, score(lambda at: held[:, at].astype(F32), lambda at: own_ref[:, at].astype(F32)))
+        put(late, 1, score(lambda at: first_ref[:, at].astype(F32), lambda at: own_ref[:, at].astype(F32)))
 
 
 def policy_kernel(sec_ref, doc_ref, q_ref, memory_ref, rows_ref, adapter_ref, down_ref, up_ref, after_ref,
@@ -174,8 +178,8 @@
 
     def section(index):
         total = jnp.sum(got_ref[index, :, 0, :], axis=0, keepdims=True)
-        if index < 2:
-            total = total + jnp.sum(got_ref[3, :, index + 1, :], axis=0, keepdims=True)
+        if index == 0:
+            total = total + jnp.sum(got_ref[3, :, 1, :], axis=0, keepdims=True)
         return total
 
     old, ref, reward, value = section(0), section(1), section(2), section(3)
@@ -426,29 +430,32 @@
     per = half // n_z
 
     below = lax.ppermute(rows, "sec", [(1, 0), (2, 1)])
-    other = lax.ppermute(rows, "sec", [(2, 0), (0, 1)])
+    other = lax.ppermute(rows, "sec", [(2, 0), (3, 1)])
+    up = lax.ppermute(rows, "sec", [(0, 1)])
     scorer = pl.pallas_call(
         scorer_kernel,
         grid=(n_sec,),
-        out_shape=(sds((n_sec, tokens, features)), sds((tokens, features), BF16)),
+        out_shape=(sds((n_sec, tokens, features)), sds((tokens, features), BF16), sds(score_heads.shape)),
         in_specs=[
             pl.BlockSpec((None, 1, tokens), lambda j: (j, 0, 0)),
             pl.BlockSpec((None, None, None, tokens, features), lambda j: (0, j, 0, 0, 0)),
             pl.BlockSpec((None, None, None, None, tokens, kv_features), lambda j: (0, 0, j, 0, 0, 0)),
             pl.BlockSpec((None, None, None, None, tokens, kv_features), lambda j: (0, 1, j, 0, 0, 0)),
+            full(score_heads),
         ],
         out_specs=(
             pl.BlockSpec((None, tokens, features), lambda j: (j, 0, 0)),
             pl.BlockSpec((tokens, features), lambda j: (0, 0)),
+            full(score_heads),
         ),
         compiler_params=pltpu.CompilerParams(vmem_limit_bytes=16 * 2**20),
         interpret=INTERPRET,
         cost_estimate=pl.CostEstimate(flops=300_000_000, bytes_accessed=8_000_000, transcendentals=600_000),
     )
     pairs = in_hbm(scorer_key_values)
-    scorer_att, last = scorer(in_hbm(document_ids), in_hbm(scorer_query), pairs, pairs)
+    scorer_att, last, weights = scorer(
+        in_hbm(document_ids), in_hbm(scorer_query), pairs, pairs, in_hbm(score_heads))
     first = lax.ppermute(last, "sec", [(0, 3)])
-    second = lax.ppermute(last, "sec", [(1, 3)])
     held = (document_ids, query, policy_memory, rows, adapter, down, adapter_up)
     groups = heads * HEAD // kv_features
     results = (sds((tokens, features)), sds((heads // groups, tokens, groups * tokens)), sds((2 * rank + 8, tokens)))
@@ -463,13 +470,17 @@
         cost_estimate=pl.CostEstimate(flops=150_000_000, bytes_accessed=4_000_000, transcendentals=150_000),
     )
     attended, probs, part = policy(sec, *map(in_hbm, held), last)
-    parts = (part,) + tuple(
-        lax.ppermute(part, "mp", [(i, (i + k) % n_mp) for i in range(n_mp)]) for k in range(1, n_mp)
-    )
+
+    def from_mp(k):
+        return lax.ppermute(part, "mp", [(i, (i + k) % n_mp) for i in range(n_mp)])
+
+    parts = (part, from_mp(2), from_mp(1))
+    parts += (from_mp(3),)
     partials = call(score_kernel, sds((n_sec * n_mp, 4, tokens)),
-                    (sec, scorer_att, rows, below, other, first, second, score_heads), smem=(0,),
+                    (sec, scorer_att, rows, below, other, up, first, weights), smem=(0,),
                     cost_estimate=pl.CostEstimate(flops=2_000_000, bytes_accessed=3_000_000, transcendentals=0))
-    got = exchange(partials, ("sec", "mp")).reshape(n_sec, n_mp, 4, tokens)
+    got = exchange(partials, ("sec", "mp"))
+    got = got.reshape(n_sec, n_mp, 4, tokens)
     keep, low_out, own, send = call(
         weights_kernel,
         (sds((8, tokens)), sds((rank, tokens)), sds((2 * half + 8, HEAD)), sds((2 * half + 8, HEAD))),

time: 128 us -> 130 us (1.016)
  blocking collectives: 59.2 us -> 61.1 us
    ppermute x2, starting transfers between devices: 19.1 us -> 17.1 us  [swap(): return lax.ppermute(x, 'core', [(i, n - 1 - i) for i in range(n)])]
    all_to_all x3, blocking collectives: 59.2 us -> 61.1 us  [exchange(): return lax.all_to_all(x, axes, 0, 0, tiled=True)]
where the time goes in v5:
time: 130 us
  blocking collectives  61.1 us (47%)
  starting transfers between devices  42.9 us (33%)
  Pallas kernels  14.3 us (11%)
  waiting for transfers between devices  8.87 us (7%)
  local copies, waits for them, and re-layouts  1.53 us (1%)
    all_to_all x3, blocking collectives, exchange(): return lax.all_to_all(x, axes, 0, 0, tiled=True)  61.1 us
    ppermute x2, starting transfers between devices, swap(): return lax.ppermute(x, 'core', [(i, n - 1 - i) for i in range(n)])  17.1 us
    ppermute x3, starting transfers between devices, from_mp(): return lax.ppermute(part, 'mp', [(i, (i + k) % n_mp) for i in range(n_mp)])  10.1 us
    pallas_call x7, Pallas kernels, call(): pl.pallas_call(kernel, out_shape=outs, in_specs=specs, out_specs=jax.tree...  7.31 us
    all_to_all x1, waiting for transfers between devices, exchange(): return lax.all_to_all(x, axes, 0, 0, tiled=True)  6.95 us
    ppermute x1, starting transfers between devices, on_device(): up = lax.ppermute(rows, 'sec', [(0, 1)])  4.86 us
    ppermute x1, starting transfers between devices, on_device(): first = lax.ppermute(last, 'sec', [(0, 3)])  4.74 us
    pallas_call x1, Pallas kernels, on_device(): scorer(in_hbm(document_ids), in_hbm(scorer_query), pairs, pairs, in_hbm(s...  4.46 us
  transfers between devices with their start and end apart: 10, of which 2 were waited for; matrix products, arithmetic and copies ran while one was open for 0% of the time, Pallas kernels for 9%

profile of v5, /device:TPU:1, one launch (start us, length us, event | category | flops | bytes accessed | tf_op | source)
XLA Modules:
  0.0 129.6 jit_solution(3197052623008564948)
XLA Ops:
  0.6 0.0 copy-start
  0.6 4.9 %collective-permute-start.2 = (bf16[128,1024]{1,0:T(8,128)(2,1)}, bf16[128,1024]{1,0:T(8,128)(2,1)}, u32[]{:S(2)}, u32[]{:S(2)}) collective-permute-start(bf16[128,1024]{1,0:T(8,128)(2,1)} %bitcast.10), channel_id=1, source_target_pairs={{0,192},{1,193},{2,194},{3,195},{4,196},{5,197},{6,198},{7,199},{8... | collective-permute-start | bytes 786440 | tf_op jit(solution)/shard_map/ppermute | solution.py:434
  5.5 1.3 collective-permute-start.1
  6.8 1.3 collective-permute-start
  8.1 4.5 %shard_map.146 = (f32[4,128,1024]{2,1,0:T(8,128)S(1)}, bf16[128,1024]{1,0:T(8,128)(2,1)}, f32[2,1024]{1,0:T(2,128)S(1)}) custom-call(s32[4,1,128]{2,1,0:T(1,128)} %doc_ref.5, bf16[1,4,1,128,1024]{4,3,2,1,0:T(8,128)(2,1)} %q_ref.1, bf16[1,2,4,1,128,256]{5,4,3,2,1,0:T(8,128)(2,1)} %v_ref.1, bf16[1,2,4,1,128,256]{5,4,3,2,1,0:T(8,128)(2,1)} %v_ref.1, ...), custom_call_target="tpu_custom_call" | custom-call | flops 300000000 | bytes 8000000 | tf_op jit(solution)/shard_map/pallas_call | solution.py:456
  12.6 0.0 copy-start.8
  12.6 4.7 %collective-permute-start.3 = (bf16[128,1024]{1,0:T(8,128)(2,1)}, bf16[128,1024]{1,0:T(8,128)(2,1)}, u32[]{:S(2)}, u32[]{:S(2)}) collective-permute-start(bf16[128,1024]{1,0:T(8,128)(2,1)} %get-tuple-element.23.after_ref), channel_id=1, source_target_pairs={{0,576},{1,577},{2,578},{3,579},{4,580},{5,581},{6,582},{7,583},{8... | collective-permute-start | bytes 786440 | tf_op jit(solution)/shard_map/ppermute | solution.py:458
  17.3 0.0 copy-done.8
  17.3 0.0 copy-start.10
  17.3 2.5 %shard_map.148 = (f32[128,1024]{1,0:T(8,128)S(1)}, f32[2,128,512]{2,1,0:T(8,128)S(1)}, f32[136,128]{1,0:T(8,128)S(1)}) custom-call(s32[1]{0:T(128)} %bitcast.sec_ref, s32[4,1,128]{2,1,0:T(1,128)} %doc_ref.5, bf16[128,1024]{1,0:T(8,128)(2,1)} %bitcast.18, bf16[2,1,128,256]{3,2,1,0:T(8,128)(2,1)} %memory_ref.3, bf16[128,1024]{1,0:T(8,128)(2,1)} %bitcast.13, ...), custom_call_target="tpu_custom_call" | custom-call | flops 150000000 | bytes 4000000 | tf_op jit(solution)/shard_map/pallas_call | solution.py:472
  19.8 0.0 copy-start.3
  19.9 0.8 copy-done.3
  20.7 0.0 copy-start.1
  20.7 0.0 copy-start.7
  20.7 4.5 %collective-permute-start.6 = (f32[136,128]{1,0:T(8,128)S(1)}, f32[136,128]{1,0:T(8,128)S(1)}, u32[]{:S(2)}, u32[]{:S(2)}) collective-permute-start(f32[136,128]{1,0:T(8,128)S(1)} %get-tuple-element.26.part0), channel_id=1, source_target_pairs={{0,3},{1,0},{2,1},{3,2},{4,7},{5,4},{6,5},{7,6},{8,11},{9,8},{10,9... | collective-permute-start | bytes 208904 | tf_op jit(solution)/shard_map/ppermute | solution.py:475
  25.2 0.0 collective-permute-done.2.up_ref
  25.2 1.9 %collective-permute-start.5 = (f32[136,128]{1,0:T(8,128)S(1)}, f32[136,128]{1,0:T(8,128)}, u32[]{:S(2)}, u32[]{:S(2)}) collective-permute-start(f32[136,128]{1,0:T(8,128)S(1)} %get-tuple-element.26.part0), channel_id=1, source_target_pairs={{0,1},{1,2},{2,3},{3,0},{4,5},{5,6},{6,7},{7,4},{8,9},{9,10},{10,1... | collective-permute-start | bytes 208904 | tf_op jit(solution)/shard_map/ppermute | solution.py:475
  27.1 0.0 collective-permute-done.1.other_ref
  27.1 3.6 %collective-permute-start.4 = (f32[136,128]{1,0:T(8,128)S(1)}, f32[136,128]{1,0:T(8,128)}, u32[]{:S(2)}, u32[]{:S(2)}) collective-permute-start(f32[136,128]{1,0:T(8,128)S(1)} %get-tuple-element.26.part0), channel_id=1, source_target_pairs={{0,2},{1,3},{2,0},{3,1},{4,6},{5,7},{6,4},{7,5},{8,10},{9,11},{10,... | collective-permute-start | bytes 208904 | tf_op jit(solution)/shard_map/ppermute | solution.py:475
  30.8 0.0 collective-permute-done.next_ref
  30.8 0.0 collective-permute-done.3.first_ref
  30.8 0.0 copy-done
  30.8 0.0 copy-start.9
  30.8 0.7 copy-done.9
  31.5 2.0 %shard_map.147 = f32[16,4,128]{2,1,0:T(4,128)} custom-call(s32[1]{0:T(128)} %bitcast.sec_ref, f32[4,128,1024]{2,1,0:T(8,128)S(1)} %get-tuple-element.22.att_ref, bf16[128,1024]{1,0:T(8,128)(2,1)S(1)} %bitcast.14, bf16[128,1024]{1,0:T(8,128)(2,1)} %collective-permute-done.next_ref, bf16[128,1024]{1,0:T(8,128)(2,1)} %collective-permute-done.1.other_ref, ...), custom_call_target="tpu_custom_call" | custom-call | flops 2000000 | bytes 3000000 | tf_op jit(solution)/shard_map/pallas_call | solution.py:371
  33.5 3.6 %all-to-all-start = ((f32[16,4,128]{2,1,0:T(4,128)}), f32[16,4,128]{2,1,0:T(4,128)S(1)}, u32[]{:S(2)}, u32[]{:S(2)}) async-start(f32[16,4,128]{2,1,0:T(4,128)} %shard_map.147), calls=%async_computation | async-start | bytes 65536 | tf_op jit(solution)/shard_map/all_to_all | solution.py:404
  37.1 0.0 collective-permute-done.6.part3
  37.1 0.0 collective-permute-done.5.part2
  37.1 0.0 collective-permute-done.4.part1
  37.2 7.0 %all-to-all-done = f32[16,4,128]{2,1,0:T(4,128)S(1)} async-done(((f32[16,4,128]{2,1,0:T(4,128)}), f32[16,4,128]{2,1,0:T(4,128)S(1)}, u32[]{:S(2)}, u32[]{:S(2)}) %all-to-all-start) | async-done | bytes 32800 | tf_op jit(solution)/shard_map/all_to_all | solution.py:404
  44.1 0.0 copy-done.10
  44.1 0.0 copy-done.1
  44.1 0.0 copy-done.7
  44.1 1.9 %shard_map.149 = (f32[8,128]{1,0:T(8,128)S(1)}, f32[64,128]{1,0:T(8,128)S(1)}, f32[1544,128]{1,0:T(8,128)S(1)}, f32[1544,128]{1,0:T(8,128)S(1)}) custom-call(s32[1]{0:T(128)} %bitcast.sec_ref, s32[1]{0:T(128)} %bitcast.1.core_ref, s32[4,4]{1,0:T(4,128)S(1)} %bitcast.23, s32[4,1,128]{2,1,0:T(1,128)S(1)} %copy-done.7, f32[4,4,4,128]{3,2,1,0:T(4,128)S(1)} %bitcast.22, ...), custom_call_target="tpu_custom_call" | custom-call | tf_op jit(solution)/shard_map/pallas_call | solution.py:371
  46.0 10.9 %collective-permute-start.7 = (f32[1544,128]{1,0:T(8,128)S(1)}, f32[1544,128]{1,0:T(8,128)S(1)}, u32[]{:S(2)}, u32[]{:S(2)}) collective-permute-start(f32[1544,128]{1,0:T(8,128)S(1)} %get-tuple-element.28), channel_id=1, source_target_pairs={{0,4},{4,0},{1,5},{5,1},{2,6},{6,2},{3,7},{7,3},{8,12},{12,8},{9,1... | collective-permute-start | bytes 2371592 | tf_op jit(solution)/shard_map/ppermute | solution.py:408
  56.9 1.9 %collective-permute-done.7.got_ref = f32[1544,128]{1,0:T(8,128)S(1)} collective-permute-done((f32[1544,128]{1,0:T(8,128)S(1)}, f32[1544,128]{1,0:T(8,128)S(1)}, u32[]{:S(2)}, u32[]{:S(2)}) %collective-permute-start.7) | collective-permute-done | bytes 790560 | tf_op jit(solution)/shard_map/ppermute | solution.py:408
  58.8 0.0 copy-start.2
  58.8 0.0 copy-start.4
  58.8 0.0 copy-start.5
  58.8 0.0 copy-start.6
  58.8 0.1 shard_map.150
  59.0 29.0 %all_to_all.20.got_ref = bf16[12,144,128]{2,1,0:T(8,128)(2,1)S(1)} all-to-all(bf16[12,144,128]{2,1,0:T(8,128)(2,1)S(1)} %shard_map.150), channel_id=1, replica_groups=mesh['sec'=4,'yh'=2,'z'=12,'core'=2,'mp'=4] {'z'}, dimensions={0} | all-to-all | bytes 884736 | tf_op jit(solution)/shard_map/all_to_all | solution.py:404
  88.0 0.2 shard_map.151
  88.2 14.6 %all_to_all.21.got_ref = bf16[8,144,128]{2,1,0:T(8,128)(2,1)S(1)} all-to-all(bf16[8,144,128]{2,1,0:T(8,128)(2,1)S(1)} %shard_map.151), channel_id=1, replica_groups=mesh['sec'=4,'yh'=2,'z'=12,'core'=2,'mp'=4] {'sec','yh'}, dimensions={0} | all-to-all | bytes 589824 | tf_op jit(solution)/shard_map/all_to_all | solution.py:404
  102.8 0.2 shard_map.152
  102.9 17.5 %all_to_all.22.own_ref = bf16[12,64,128]{2,1,0:T(8,128)(2,1)S(1)} all-to-all(bf16[12,64,128]{2,1,0:T(8,128)(2,1)S(1)} %get-tuple-element.36), channel_id=1, replica_groups=mesh['sec'=4,'yh'=2,'z'=12,'core'=2,'mp'=4] {'z'}, dimensions={0} | all-to-all | bytes 393216 | tf_op jit(solution)/shard_map/all_to_all | solution.py:404
  120.4 6.2 %collective-permute-start.8 = (bf16[12,64,128]{2,1,0:T(8,128)(2,1)S(1)}, bf16[12,64,128]{2,1,0:T(8,128)(2,1)S(1)}, u32[]{:S(2)}, u32[]{:S(2)}) collective-permute-start(bf16[12,64,128]{2,1,0:T(8,128)(2,1)S(1)} %all_to_all.22.own_ref), channel_id=1, source_target_pairs={{0,4},{4,0},{1,5},{5,1},{2,6},{6,2},{3,7},{7,3},{8,12},{12,8},{9,1... | collective-permute-start | bytes 589832 | tf_op jit(solution)/shard_map/ppermute | solution.py:408
  126.7 0.0 copy-done.2
  126.7 0.0 copy-done.4
  126.7 0.0 copy-done.5
  126.7 0.0 copy-done.6
  126.7 2.0 %shard_map.153 = (f32[1,128]{1,0:T(1,128)}, bf16[128,1024]{1,0:T(8,128)(2,1)}, bf16[2,1,128,256]{3,2,1,0:T(8,128)(2,1)}) custom-call(f32[8,128]{1,0:T(8,128)S(1)} %get-tuple-element.29.moments_ref, f32[8,128]{1,0:T(8,128)S(1)} %get-tuple-element.30.keep_ref, f32[64,128]{1,0:T(8,128)S(1)} %get-tuple-element.31.low_ref, bf16[64,1024]{1,0:T(8,128)(2,1)S(1)} %bitcast.21, ...), custom_call_target="tpu_custom_call" | custom-call | flops 300000000 | bytes 20000000 | tf_op jit(solution)/shard_map/pallas_call | solution.py:371
  128.7 0.0 collective-permute-done.8.other_ref
  128.7 0.9 shard_map.154
Async XLA Ops:
  0.6 30.2 %copy-start = (bf16[1,128,1024]{2,1,0:T(8,128)(2,1)S(1)}, bf16[1,128,1024]{2,1,0:T(8,128)(2,1)}, u32[]{:S(2)}) copy-start(bf16[1,128,1024]{2,1,0:T(8,128)(2,1)} %param.13) | copy-start | bytes 786436
  0.6 24.5 %collective-permute-start.2 = (bf16[128,1024]{1,0:T(8,128)(2,1)}, bf16[128,1024]{1,0:T(8,128)(2,1)}, u32[]{:S(2)}, u32[]{:S(2)}) collective-permute-start(bf16[128,1024]{1,0:T(8,128)(2,1)} %bitcast.10), channel_id=1, source_target_pairs={{0,192},{1,193},{2,194},{3,195},{4,196},{5,197},{6,198},{7,199},{8... | collective-permute-start | bytes 786440 | tf_op jit(solution)/shard_map/ppermute | solution.py:434
  5.5 21.6 %collective-permute-start.1 = (bf16[128,1024]{1,0:T(8,128)(2,1)}, bf16[128,1024]{1,0:T(8,128)(2,1)}, u32[]{:S(2)}, u32[]{:S(2)}) collective-permute-start(bf16[128,1024]{1,0:T(8,128)(2,1)} %bitcast.11), channel_id=1, source_target_pairs={{384,0},{576,192},{385,1},{577,193},{386,2},{578,194},{387,3},{579... | collective-permute-start | bytes 786440 | tf_op jit(solution)/shard_map/ppermute | solution.py:433
  6.8 24.0 %collective-permute-start = (bf16[128,1024]{1,0:T(8,128)(2,1)}, bf16[128,1024]{1,0:T(8,128)(2,1)}, u32[]{:S(2)}, u32[]{:S(2)}) collective-permute-start(bf16[128,1024]{1,0:T(8,128)(2,1)} %bitcast.12), channel_id=1, source_target_pairs={{192,0},{384,192},{193,1},{385,193},{194,2},{386,194},{195,3},{387... | collective-permute-start | bytes 786440 | tf_op jit(solution)/shard_map/ppermute | solution.py:432
  12.6 4.7 %copy-start.8 = (f32[2,1024]{1,0:T(2,128)}, f32[2,1024]{1,0:T(2,128)S(1)}, u32[]{:S(2)}) copy-start(f32[2,1024]{1,0:T(2,128)S(1)} %get-tuple-element.24.heads_ref) | copy-start | bytes 24580
  12.6 18.2 %collective-permute-start.3 = (bf16[128,1024]{1,0:T(8,128)(2,1)}, bf16[128,1024]{1,0:T(8,128)(2,1)}, u32[]{:S(2)}, u32[]{:S(2)}) collective-permute-start(bf16[128,1024]{1,0:T(8,128)(2,1)} %get-tuple-element.23.after_ref), channel_id=1, source_target_pairs={{0,576},{1,577},{2,578},{3,579},{4,580},{5,581},{6,582},{7,583},{8... | collective-permute-start | bytes 786440 | tf_op jit(solution)/shard_map/ppermute | solution.py:458
  17.3 26.8 %copy-start.10 = (s32[4,1,4]{2,1,0:T(1,128)S(1)}, s32[4,1,4]{2,1,0:T(1,128)}, u32[]{:S(2)}) copy-start(s32[4,1,4]{2,1,0:T(1,128)} %param.21) | copy-start | bytes 196
  19.8 0.8 copy-start.3
  20.7 23.5 %copy-start.1 = (bf16[1,128,2048]{2,1,0:T(8,128)(2,1)S(1)}, bf16[1,128,2048]{2,1,0:T(8,128)(2,1)}, u32[]{:S(2)}) copy-start(bf16[1,128,2048]{2,1,0:T(8,128)(2,1)} %param.14) | copy-start | bytes 1572868
  20.7 23.5 %copy-start.7 = (s32[4,1,128]{2,1,0:T(1,128)S(1)}, s32[4,1,128]{2,1,0:T(1,128)}, u32[]{:S(2)}) copy-start(s32[4,1,128]{2,1,0:T(1,128)} %doc_ref.5) | copy-start | bytes 6148
  20.7 16.5 %collective-permute-start.6 = (f32[136,128]{1,0:T(8,128)S(1)}, f32[136,128]{1,0:T(8,128)S(1)}, u32[]{:S(2)}, u32[]{:S(2)}) collective-permute-start(f32[136,128]{1,0:T(8,128)S(1)} %get-tuple-element.26.part0), channel_id=1, source_target_pairs={{0,3},{1,0},{2,1},{3,2},{4,7},{5,4},{6,5},{7,6},{8,11},{9,8},{10,9... | collective-permute-start | bytes 208904 | tf_op jit(solution)/shard_map/ppermute | solution.py:475
  25.2 12.0 %collective-permute-start.5 = (f32[136,128]{1,0:T(8,128)S(1)}, f32[136,128]{1,0:T(8,128)}, u32[]{:S(2)}, u32[]{:S(2)}) collective-permute-start(f32[136,128]{1,0:T(8,128)S(1)} %get-tuple-element.26.part0), channel_id=1, source_target_pairs={{0,1},{1,2},{2,3},{3,0},{4,5},{5,6},{6,7},{7,4},{8,9},{9,10},{10,1... | collective-permute-start | bytes 208904 | tf_op jit(solution)/shard_map/ppermute | solution.py:475
  27.1 10.0 %collective-permute-start.4 = (f32[136,128]{1,0:T(8,128)S(1)}, f32[136,128]{1,0:T(8,128)}, u32[]{:S(2)}, u32[]{:S(2)}) collective-permute-start(f32[136,128]{1,0:T(8,128)S(1)} %get-tuple-element.26.part0), channel_id=1, source_target_pairs={{0,2},{1,3},{2,0},{3,1},{4,6},{5,7},{6,4},{7,5},{8,10},{9,11},{10,... | collective-permute-start | bytes 208904 | tf_op jit(solution)/shard_map/ppermute | solution.py:475
  30.8 0.7 copy-start.9
  33.5 10.6 %all-to-all-start = ((f32[16,4,128]{2,1,0:T(4,128)}), f32[16,4,128]{2,1,0:T(4,128)S(1)}, u32[]{:S(2)}, u32[]{:S(2)}) async-start(f32[16,4,128]{2,1,0:T(4,128)} %shard_map.147), calls=%async_computation | async-start | bytes 65536 | tf_op jit(solution)/shard_map/all_to_all | solution.py:404
  46.0 12.8 %collective-permute-start.7 = (f32[1544,128]{1,0:T(8,128)S(1)}, f32[1544,128]{1,0:T(8,128)S(1)}, u32[]{:S(2)}, u32[]{:S(2)}) collective-permute-start(f32[1544,128]{1,0:T(8,128)S(1)} %get-tuple-element.28), channel_id=1, source_target_pairs={{0,4},{4,0},{1,5},{5,1},{2,6},{6,2},{3,7},{7,3},{8,12},{12,8},{9,1... | collective-permute-start | bytes 2371592 | tf_op jit(solution)/shard_map/ppermute | solution.py:408
  58.8 67.8 %copy-start.2 = (bf16[1,128,1024]{2,1,0:T(8,128)(2,1)S(1)}, bf16[1,128,1024]{2,1,0:T(8,128)(2,1)}, u32[]{:S(2)}) copy-start(bf16[1,128,1024]{2,1,0:T(8,128)(2,1)} %param.11) | copy-start | bytes 786436
  58.8 67.8 %copy-start.4 = (f32[2,128,512]{2,1,0:T(8,128)S(1)}, f32[2,128,512]{2,1,0:T(8,128)}, u32[]{:S(2)}) copy-start(f32[2,128,512]{2,1,0:T(8,128)} %copy-done.3) | copy-start | bytes 1572868
  58.8 67.8 %copy-start.5 = (bf16[2,1,128,256]{3,2,1,0:T(8,128)(2,1)S(1)}, bf16[2,1,128,256]{3,2,1,0:T(8,128)(2,1)}, u32[]{:S(2)}) copy-start(bf16[2,1,128,256]{3,2,1,0:T(8,128)(2,1)} %memory_ref.3) | copy-start | bytes 393220
  58.8 67.9 %copy-start.6 = (bf16[1024,64]{0,1:T(8,128)(2,1)S(1)}, bf16[1024,64]{0,1:T(8,128)(2,1)}, u32[]{:S(2)}) copy-start(bf16[1024,64]{0,1:T(8,128)(2,1)} %param.15) | copy-start | bytes 393220
  120.4 8.3 %collective-permute-start.8 = (bf16[12,64,128]{2,1,0:T(8,128)(2,1)S(1)}, bf16[12,64,128]{2,1,0:T(8,128)(2,1)S(1)}, u32[]{:S(2)}, u32[]{:S(2)}) collective-permute-start(bf16[12,64,128]{2,1,0:T(8,128)(2,1)S(1)} %all_to_all.22.own_ref), channel_id=1, source_target_pairs={{0,4},{4,0},{1,5},{5,1},{2,6},{6,2},{3,7},{7,3},{8,12},{12,8},{9,1... | collective-permute-start | bytes 589832 | tf_op jit(solution)/shard_map/ppermute | solution.py:408

commit v6 on v5

--- a/solution.py
+++ b/solution.py
@@ -60,7 +60,7 @@
     return raised * (1.0 / jnp.sum(raised, axis=0, keepdims=True))
 
 
-def scorer_kernel(doc_ref, q_ref, k_ref, v_ref, heads_ref, out_ref, last_ref, held_ref):
+def scorer_kernel(sec_ref, doc_ref, q_ref, k_ref, v_ref, heads_ref, out_ref, last_ref, held_ref):
     n = q_ref.shape[0]
     groups = q_ref.shape[1] // k_ref.shape[1]
     kept = kept_of(doc_ref[...], groups)
@@ -72,13 +72,20 @@
             at = (group * groups + i) * HEAD
             out_ref[:, at:at + HEAD] = attended[i * n:(i + 1) * n]
 
-    @pl.when(pl.program_id(0) == pl.num_programs(0) - 1)
+    n_sec = pl.num_programs(0)
+
+    @pl.when(pl.program_id(0) == lax.rem(sec_ref[0] + n_sec - 1, n_sec))
     def _():
         last_ref[...] = out_ref[...].astype(BF16)
+
+    @pl.when(pl.program_id(0) == 0)
+    def _():
         held_ref[...] = heads_ref[...]
 
 
-def score_kernel(sec_ref, att_ref, own_ref, next_ref, other_ref, up_ref, first_ref, heads_ref, out_ref):
+def score_kernel(sec_ref, att_ref, own_ref, next_ref, other_ref, first_ref, heads_ref,
+                 part_ref, near_ref, out_ref, sum_ref):
+    sum_ref[...] = part_ref[...] + near_ref[...]
     sec = sec_ref[0]
     n_sec = att_ref.shape[0]
     copies = out_ref.shape[0] // n_sec
@@ -104,10 +111,6 @@
         for held, row in ((own_ref, sec), (next_ref, sec + 1), (other_ref, sec + 2)):
             put(row, 0, score(lambda at: att_ref[row, :, at], lambda at: held[:, at].astype(F32)))
 
-    @pl.when(sec == 1)
-    def _():
-        put(0, 0, score(lambda at: att_ref[0, :, at], lambda at: up_ref[:, at].astype(F32)))
-
     @pl.when(sec >= 2)
     def _():
         def weight(at):
@@ -116,13 +119,15 @@
         for row in range(n_sec):
             put(row, 0, score(lambda at: att_ref[row, :, at], weight))
 
-    @pl.when(sec == late)
+    @pl.when((sec == late) | (sec == 0))
     def _():
-        put(late, 1, score(lambda at: first_ref[:, at].astype(F32), lambda at: own_ref[:, at].astype(F32)))
+        value = score(lambda at: first_ref[:, at].astype(F32), lambda at: own_ref[:, at].astype(F32))
+        put(sec, 1, value)
 
 
 def policy_kernel(sec_ref, doc_ref, q_ref, memory_ref, rows_ref, adapter_ref, down_ref, up_ref, after_ref,
-                  att_ref, probs_ref, part_ref):
+                  att_ref, held_ref, part_ref):
+    held_ref[...] = rows_ref[...]
     del after_ref
     k_ref, v_ref = memory_ref.at[0, 0], memory_ref.at[1, 0]
     n = q_ref.shape[0]
@@ -133,7 +138,6 @@
     for group in range(k_ref.shape[1] // HEAD):
         kv = slice(group * HEAD, (group + 1) * HEAD)
         probs = probs_of(stacked(q_ref, group, groups), k_ref[:, kv], kept)
-        probs_ref[group] = probs
         attended = dot(probs.astype(BF16), v_ref[:, kv], TN)
         for i in range(groups):
             at = slice((group * groups + i) * HEAD, (group * groups + i + 1) * HEAD)
@@ -158,7 +162,7 @@
 
 
 def weights_kernel(sec_ref, core_ref, prompt_ref, doc_ref, got_ref, att_ref, adapter_ref,
-                   part0, part1, part2, part3,
+                   near_ref, far_ref,
                    keep_ref, low_ref, own_ref, send_ref, both_ref):
     sec = sec_ref[0]
     doc = doc_ref[sec].astype(F32)
@@ -178,8 +182,8 @@
 
     def section(index):
         total = jnp.sum(got_ref[index, :, 0, :], axis=0, keepdims=True)
-        if index == 0:
-            total = total + jnp.sum(got_ref[3, :, 1, :], axis=0, keepdims=True)
+        if index < 2:
+            total = total + jnp.sum(got_ref[3 - 3 * index, :, 1, :], axis=0, keepdims=True)
         return total
 
     old, ref, reward, value = section(0), section(1), section(2), section(3)
@@ -196,8 +200,8 @@
     squares = jnp.sum(respond * advantage * advantage, axis=1, keepdims=True)
     moments = jnp.where(lane == 0, count, jnp.where(lane == 1, total, jnp.where(lane == 2, squares, 0.0)))
 
-    rank = (part0.shape[0] - 8) // 2
-    part = (part0[...] + part1[...]) + (part2[...] + part3[...])
+    rank = (near_ref.shape[0] - 8) // 2
+    part = near_ref[...] + far_ref[...]
     low_in, low_out, base = part[0:rank], part[rank:2 * rank], part[2 * rank:2 * rank + 1]
     policy_new = base + jnp.sum(low_in * low_out, axis=0, keepdims=True)
     weight = -respond * jnp.exp(policy_new - old)
@@ -277,8 +281,9 @@
 def added(got_ref, per, centres, centre):
     plain, lifted = None, None
     for index in range(got_ref.shape[0]):
-        mine = got_ref[index, 0:per].astype(F32)
-        high = got_ref[index, per:2 * per].astype(F32) + (centres[index] - centre) * mine
+        both = got_ref[index, 0:2 * per].astype(F32)
+        mine = both[0:per]
+        high = both[per:2 * per] + (centres[index] - centre) * mine
         plain = mine if plain is None else plain + mine
         lifted = high if lifted is None else lifted + high
     return plain, lifted
@@ -289,12 +294,12 @@
     moments, centres = gathered(got_ref, per)
     centre = middle(moments)
     plain, lifted = added(got_ref, per, centres, centre)
-    plain, lifted = plain.astype(BF16), lifted.astype(BF16)
     tile = note(moments, centre)
+    part = per // out_ref.shape[0]
     for index in range(out_ref.shape[0]):
-        out_ref[index, 0:per] = plain
-        out_ref[index, per:2 * per] = lifted
-        out_ref[index, 2 * per:] = tile
+        at = slice(index * part, (index + 1) * part)
+        out_ref[index, 0:2 * part] = jnp.concatenate([plain[at], lifted[at]], axis=0).astype(BF16)
+        out_ref[index, 2 * part:] = tile
 
 
 def scale_of(moments):
@@ -332,7 +337,7 @@
             up_ref[:, at:at + HEAD] = value
 
 
-def backward_kernel(moments_ref, keep_ref, low_ref, down_ref, rows_ref, probs_ref, q_ref, memory_ref,
+def backward_kernel(sec_ref, doc_ref, moments_ref, keep_ref, low_ref, down_ref, rows_ref, q_ref, memory_ref,
                     white_ref, query_ref, memory_grad_ref):
     k_ref, v_ref = memory_ref.at[0, 0], memory_ref.at[1, 0]
     n = q_ref.shape[0]
@@ -344,6 +349,7 @@
     high, low = halves(grad_score * low_ref[...])
     groups = q_ref.shape[1] // k_ref.shape[1]
     scale = HEAD ** (-0.5)
+    kept = kept_of(doc_ref[sec_ref[0]], groups)
     for group in range(k_ref.shape[1] // HEAD):
         kv = slice(group * HEAD, (group + 1) * HEAD)
         keys, values = k_ref[:, kv], v_ref[:, kv]
@@ -354,7 +360,8 @@
             grad = grad_col * rows_ref[:, at].astype(F32) + (dot(high, down, TN) + dot(low, down, TN))
             grads.append(grad.astype(BF16))
         grad = jnp.concatenate(grads, axis=0)
-        probs = probs_ref[group]
+        query = stacked(q_ref, group, groups)
+        probs = probs_of(query, keys, kept)
         dprobs = dot(values, grad, NT)
         inner = jnp.sum(probs * dprobs, axis=0, keepdims=True)
         dscores = (probs * (dprobs - inner)).astype(BF16)
@@ -362,7 +369,7 @@
         for i in range(groups):
             at = (group * groups + i) * HEAD
             query_ref[:, at:at + HEAD] = query_grad[i * n:(i + 1) * n]
-        memory_grad_ref[0, 0, :, kv] = (dot(dscores, stacked(q_ref, group, groups), NN) * scale).astype(BF16)
+        memory_grad_ref[0, 0, :, kv] = (dot(dscores, query, NN) * scale).astype(BF16)
         memory_grad_ref[1, 0, :, kv] = dot(probs.astype(BF16), grad, NN).astype(BF16)
 
 
@@ -423,20 +430,19 @@
     down = adapter_down.T
     rank = down.shape[0]
     width = adapter.shape[1]
-    heads = features // HEAD
     prompts = prompt_lengths[:, 0]
     blocks = (features + width) // HEAD
     half = blocks // n_core * rank
-    per = half // n_z
+    per = half // n_y
 
     below = lax.ppermute(rows, "sec", [(1, 0), (2, 1)])
     other = lax.ppermute(rows, "sec", [(2, 0), (3, 1)])
-    up = lax.ppermute(rows, "sec", [(0, 1)])
     scorer = pl.pallas_call(
         scorer_kernel,
         grid=(n_sec,),
         out_shape=(sds((n_sec, tokens, features)), sds((tokens, features), BF16), sds(score_heads.shape)),
         in_specs=[
+            pl.BlockSpec(memory_space=pltpu.SMEM),
             pl.BlockSpec((None, 1, tokens), lambda j: (j, 0, 0)),
             pl.BlockSpec((None, None, None, tokens, features), lambda j: (0, j, 0, 0, 0)),
             pl.BlockSpec((None, None, None, None, tokens, kv_features), lambda j: (0, 0, j, 0, 0, 0)),
@@ -454,11 +460,10 @@
     )
     pairs = in_hbm(scorer_key_values)
     scorer_att, last, weights = scorer(
-        in_hbm(document_ids), in_hbm(scorer_query), pairs, pairs, in_hbm(score_heads))
-    first = lax.ppermute(last, "sec", [(0, 3)])
+        sec, in_hbm(document_ids), in_hbm(scorer_query), pairs, pairs, in_hbm(score_heads))
+    first = lax.ppermute(last, "sec", [(0, 3), (1, 0)])
     held = (document_ids, query, policy_memory, rows, adapter, down, adapter_up)
-    groups = heads * HEAD // kv_features
-    results = (sds((tokens, features)), sds((heads // groups, tokens, groups * tokens)), sds((2 * rank + 8, tokens)))
+    results = (sds((tokens, features)), sds((tokens, features), BF16), sds((2 * rank + 8, tokens)))
     policy = pl.pallas_call(
         policy_kernel,
         grid=(1,),
@@ -469,30 +474,28 @@
         interpret=INTERPRET,
         cost_estimate=pl.CostEstimate(flops=150_000_000, bytes_accessed=4_000_000, transcendentals=150_000),
     )
-    attended, probs, part = policy(sec, *map(in_hbm, held), last)
-
-    def from_mp(k):
-        return lax.ppermute(part, "mp", [(i, (i + k) % n_mp) for i in range(n_mp)])
-
-    parts = (part, from_mp(2), from_mp(1))
-    parts += (from_mp(3),)
-    partials = call(score_kernel, sds((n_sec * n_mp, 4, tokens)),
-                    (sec, scorer_att, rows, below, other, up, first, weights), smem=(0,),
+    attended, rows_held, part = policy(sec, *map(in_hbm, held), last)
+    near = lax.ppermute(part, "mp", [(0, 1), (1, 0), (2, 3), (3, 2)])
+    partials, near = call(score_kernel, (sds((n_sec * n_mp, 4, tokens)), sds(part.shape)),
+                    (sec, scorer_att, rows_held, below, other, first, weights, part, near), smem=(0,),
                     cost_estimate=pl.CostEstimate(flops=2_000_000, bytes_accessed=3_000_000, transcendentals=0))
     got = exchange(partials, ("sec", "mp"))
     got = got.reshape(n_sec, n_mp, 4, tokens)
+    far = lax.ppermute(near, "mp", [(0, 3), (3, 0), (1, 2), (2, 1)])
     keep, low_out, own, send = call(
         weights_kernel,
         (sds((8, tokens)), sds((rank, tokens)), sds((2 * half + 8, HEAD)), sds((2 * half + 8, HEAD))),
-        (sec, core, prompts, document_ids, got, attended, adapter) + parts,
+        (sec, core, prompts, document_ids, got, attended, adapter, near, far),
         smem=(0, 1, 2),
         scratch=(pltpu.VMEM((n_core, 2 * half + 8, HEAD), F32),),
     )
-    got = call(pair_kernel, sds((n_z, 2 * per + 16, HEAD), BF16), (own, swap(send, n_core)))
+    got = call(pair_kernel, sds((n_y, 2 * per + 16, HEAD), BF16), (own, swap(send, n_core)))
+    got = exchange(got, Y)
+    part = per // n_z
+    got = exchange(call(column_kernel, sds((n_z, 2 * part + 16, HEAD), BF16), (got,)), "z")
+    got, moments = call(final_kernel, (sds((n_z, part, HEAD), BF16), sds((8, HEAD))), (got,))
     got = exchange(got, "z")
-    got = exchange(call(column_kernel, sds((n_y, 2 * per + 16, HEAD), BF16), (got,)), Y)
-    got, moments = call(final_kernel, (sds((n_z, per, HEAD), BF16), sds((8, HEAD))), (got,))
-    got = exchange(got, "z")
+    got = exchange(jnp.broadcast_to(got.reshape(1, per, HEAD), (n_y, per, HEAD)), Y)
     got = got.reshape(blocks // n_core, rank, HEAD)
     down_grad, up_grad = call(place_kernel, (sds((rank, features)), sds((rank, width))),
                               (core, got, swap(got, n_core)), smem=(0,),
@@ -500,7 +503,8 @@
     white, query_grad, memory_grad = call(
         backward_kernel,
         (sds((1, tokens)), sds((tokens, features), BF16), sds(policy_memory.shape, BF16)),
-        (moments, keep, low_out, down, rows, probs, query, policy_memory),
+        (sec, document_ids, moments, keep, low_out, down, rows, query, policy_memory),
+        smem=(0,),
         cost_estimate=pl.CostEstimate(flops=300_000_000, bytes_accessed=20_000_000, transcendentals=0),
     )
     return white, query_grad[None], memory_grad, down_grad.T, up_grad

time: 130 us -> 131 us (level)
  blocking collectives: 61.1 us -> 66.1 us
  starting transfers between devices: 42.9 us -> 38.8 us
  waiting for transfers between devices: 8.87 us -> 12.7 us
  Pallas kernels: 14.3 us -> 12.3 us
  local copies, waits for them, and re-layouts: 1.53 us -> 0.06 us
    all_to_all x3 -> x4, blocking collectives: 61.1 us -> 66.1 us  [exchange(): return lax.all_to_all(x, axes, 0, 0, tiled=True)]
    ppermute x2, starting transfers between devices: 17.1 us -> 13.3 us  [swap(): return lax.ppermute(x, 'core', [(i, n - 1 - i) for i in range(n)])]
    ppermute x5 -> x3, waiting for transfers between devices: 0.01 us -> 2.23 us  [the longest x1 2.22 us: on_device(): near = lax.ppermute(part, 'mp', [(0, 1), (1, 0), (2, 3), (3, 2)])]
    ppermute x1, waiting for transfers between devices: 0.01 us -> 1.61 us  [on_device(): other = lax.ppermute(rows, 'sec', [(2, 0), (3, 1)])]
    unnamed x22 -> x16, local copies, waits for them, and re-layouts: 1.53 us -> 0.04 us
    pallas_call x7, Pallas kernels: 7.31 us -> 5.9 us  [call(): pl.pallas_call(kernel, out_shape=outs, in_specs=specs, out_specs=jax.tree...]
    ppermute x5 -> x3, starting transfers between devices: 19.7 us -> 19.4 us  [the longest x1 10.1 us: on_device(): far = lax.ppermute(near, 'mp', [(0, 3), (3, 0), (1, 2), (2, 1)])]
  transfers between devices with their start and end apart: 10 -> 8, of which waited for: 2 -> 4; matrix products, arithmetic and copies ran while one was open for 0% -> 0% of each run, Pallas kernels for 9% -> 3%
where the time goes in v6:
time: 131 us
  blocking collectives  66.1 us (50%)
  starting transfers between devices  38.8 us (30%)
  waiting for transfers between devices  12.7 us (10%)
  Pallas kernels  12.3 us (9%)
    all_to_all x4, blocking collectives, exchange(): return lax.all_to_all(x, axes, 0, 0, tiled=True)  66.1 us
    ppermute x2, starting transfers between devices, swap(): return lax.ppermute(x, 'core', [(i, n - 1 - i) for i in range(n)])  13.3 us
    ppermute x1, starting transfers between devices, on_device(): far = lax.ppermute(near, 'mp', [(0, 3), (3, 0), (1, 2), (2, 1)])  10.1 us
    all_to_all x1, waiting for transfers between devices, exchange(): return lax.all_to_all(x, axes, 0, 0, tiled=True)  6.95 us
    ppermute x1, starting transfers between devices, on_device(): first = lax.ppermute(last, 'sec', [(0, 3), (1, 0)])  6.02 us
    pallas_call x7, Pallas kernels, call(): pl.pallas_call(kernel, out_shape=outs, in_specs=specs, out_specs=jax.tree...  5.9 us
    pallas_call x1, Pallas kernels, on_device(): scorer(sec, in_hbm(document_ids), in_hbm(scorer_query), pairs, pairs, in_...  3.84 us
    all_to_all x1, starting transfers between devices, exchange(): return lax.all_to_all(x, axes, 0, 0, tiled=True)  3.51 us
  transfers between devices with their start and end apart: 8, of which 4 were waited for; matrix products, arithmetic and copies ran while one was open for 0% of the time, Pallas kernels for 3%

profile of v6, /device:TPU:1, one launch (start us, length us, event | category | flops | bytes accessed | tf_op | source)
XLA Modules:
  0.0 130.8 jit_solution(13922304321839578780)
XLA Ops:
  0.6 0.0 copy-start.2
  0.7 3.8 %shard_map.146 = (f32[4,128,1024]{2,1,0:T(8,128)S(1)}, bf16[128,1024]{1,0:T(8,128)(2,1)S(1)}, f32[2,1024]{1,0:T(2,128)S(1)}) custom-call(s32[1]{0:T(128)} %bitcast.sec_ref, s32[4,1,128]{2,1,0:T(1,128)} %doc_ref.7, bf16[1,4,1,128,1024]{4,3,2,1,0:T(8,128)(2,1)} %q_ref.1, bf16[1,2,4,1,128,256]{5,4,3,2,1,0:T(8,128)(2,1)} %v_ref.1, ...), custom_call_target="tpu_custom_call" | custom-call | flops 300000000 | bytes 8000000 | tf_op jit(solution)/shard_map/pallas_call | solution.py:462
  4.5 6.0 %collective-permute-start.2 = (bf16[128,1024]{1,0:T(8,128)(2,1)S(1)}, bf16[128,1024]{1,0:T(8,128)(2,1)S(1)}, u32[]{:S(2)}, u32[]{:S(2)}) collective-permute-start(bf16[128,1024]{1,0:T(8,128)(2,1)S(1)} %get-tuple-element.25.after_ref), channel_id=1, source_target_pairs={{0,576},{192,0},{1,577},{193,1},{2,578},{194,2},{3,579},{195,3},{4... | collective-permute-start | bytes 786440 | tf_op jit(solution)/shard_map/ppermute | solution.py:464
  10.5 0.0 copy-done.2
  10.5 1.3 collective-permute-start
  11.8 1.3 collective-permute-start.1
  13.1 2.5 %shard_map.147 = (f32[128,1024]{1,0:T(8,128)S(1)}, bf16[128,1024]{1,0:T(8,128)(2,1)S(1)}, f32[136,128]{1,0:T(8,128)S(1)}) custom-call(s32[1]{0:T(128)} %bitcast.sec_ref, s32[4,1,128]{2,1,0:T(1,128)} %doc_ref.7, bf16[128,1024]{1,0:T(8,128)(2,1)} %bitcast.16, bf16[2,1,128,256]{3,2,1,0:T(8,128)(2,1)} %memory_ref.3, bf16[128,1024]{1,0:T(8,128)(2,1)} %bitcast.18, ...), custom_call_target="tpu_custom_call" | custom-call | flops 150000000 | bytes 4000000 | tf_op jit(solution)/shard_map/pallas_call | solution.py:477
  15.7 0.0 copy-start
  15.7 0.0 copy-start.6
  15.7 0.0 copy-start.7
  15.7 3.2 %collective-permute-start.3 = (f32[136,128]{1,0:T(8,128)S(1)}, f32[136,128]{1,0:T(8,128)S(1)}, u32[]{:S(2)}, u32[]{:S(2)}) collective-permute-start(f32[136,128]{1,0:T(8,128)S(1)} %get-tuple-element.28.part_ref), channel_id=1, source_target_pairs={{0,1},{1,0},{2,3},{3,2},{4,5},{5,4},{6,7},{7,6},{8,9},{9,8},{10,11... | collective-permute-start | bytes 208904 | tf_op jit(solution)/shard_map/ppermute | solution.py:478
  19.0 2.2 %collective-permute-done.3.near_ref = f32[136,128]{1,0:T(8,128)S(1)} collective-permute-done((f32[136,128]{1,0:T(8,128)S(1)}, f32[136,128]{1,0:T(8,128)S(1)}, u32[]{:S(2)}, u32[]{:S(2)}) %collective-permute-start.3) | collective-permute-done | bytes 69664 | tf_op jit(solution)/shard_map/ppermute | solution.py:478
  21.2 0.0 collective-permute-done.2.first_ref
  21.2 0.0 collective-permute-done.next_ref
  21.2 1.6 %collective-permute-done.1.other_ref = bf16[128,1024]{1,0:T(8,128)(2,1)S(1)} collective-permute-done((bf16[128,1024]{1,0:T(8,128)(2,1)S(1)}, bf16[128,1024]{1,0:T(8,128)(2,1)S(1)}, u32[]{:S(2)}, u32[]{:S(2)}) %collective-permute-start.1) | collective-permute-done | bytes 262176 | tf_op jit(solution)/shard_map/ppermute | solution.py:439
  22.8 1.0 shard_map.148
  23.8 10.1 %collective-permute-start.4 = (f32[136,128]{1,0:T(8,128)S(1)}, f32[136,128]{1,0:T(8,128)S(1)}, u32[]{:S(2)}, u32[]{:S(2)}) collective-permute-start(f32[136,128]{1,0:T(8,128)S(1)} %get-tuple-element.31.near_ref), channel_id=1, source_target_pairs={{0,3},{3,0},{1,2},{2,1},{4,7},{7,4},{5,6},{6,5},{8,11},{11,8},{9,1... | collective-permute-start | bytes 208904 | tf_op jit(solution)/shard_map/ppermute | solution.py:484
  34.0 3.5 %all-to-all-start = ((f32[16,4,128]{2,1,0:T(4,128)}), f32[16,4,128]{2,1,0:T(4,128)S(1)}, u32[]{:S(2)}, u32[]{:S(2)}) async-start(f32[16,4,128]{2,1,0:T(4,128)} %get-tuple-element.29), calls=%async_computation | async-start | bytes 65536 | tf_op jit(solution)/shard_map/all_to_all | solution.py:411
  37.5 6.9 %all-to-all-done = f32[16,4,128]{2,1,0:T(4,128)S(1)} async-done(((f32[16,4,128]{2,1,0:T(4,128)}), f32[16,4,128]{2,1,0:T(4,128)S(1)}, u32[]{:S(2)}, u32[]{:S(2)}) %all-to-all-start) | async-done | bytes 32800 | tf_op jit(solution)/shard_map/all_to_all | solution.py:411
  44.5 0.0 collective-permute-done.4.far_ref
  44.5 0.0 copy-done
  44.5 0.0 copy-done.6
  44.5 0.0 copy-done.7
  44.5 1.5 %shard_map.149 = (f32[8,128]{1,0:T(8,128)S(1)}, f32[64,128]{1,0:T(8,128)S(1)}, f32[1544,128]{1,0:T(8,128)S(1)}, f32[1544,128]{1,0:T(8,128)S(1)}) custom-call(s32[1]{0:T(128)} %bitcast.sec_ref, s32[1]{0:T(128)} %bitcast.1.core_ref, s32[4,4]{1,0:T(4,128)S(1)} %bitcast.25, s32[4,1,128]{2,1,0:T(1,128)S(1)} %copy-done.6, f32[4,4,4,128]{3,2,1,0:T(4,128)S(1)} %bitcast.24, ...), custom_call_target="tpu_custom_call" | custom-call | tf_op jit(solution)/shard_map/pallas_call | solution.py:378
  46.0 6.6 %collective-permute-start.5 = (f32[1544,128]{1,0:T(8,128)S(1)}, f32[1544,128]{1,0:T(8,128)S(1)}, u32[]{:S(2)}, u32[]{:S(2)}) collective-permute-start(f32[1544,128]{1,0:T(8,128)S(1)} %get-tuple-element.33), channel_id=1, source_target_pairs={{0,4},{4,0},{1,5},{5,1},{2,6},{6,2},{3,7},{7,3},{8,12},{12,8},{9,1... | collective-permute-start | bytes 2371592 | tf_op jit(solution)/shard_map/ppermute | solution.py:415
  52.7 1.9 %collective-permute-done.5.got_ref = f32[1544,128]{1,0:T(8,128)S(1)} collective-permute-done((f32[1544,128]{1,0:T(8,128)S(1)}, f32[1544,128]{1,0:T(8,128)S(1)}, u32[]{:S(2)}, u32[]{:S(2)}) %collective-permute-start.5) | collective-permute-done | bytes 790560 | tf_op jit(solution)/shard_map/ppermute | solution.py:415
  54.6 0.0 copy-start.1
  54.6 0.0 copy-start.3
  54.6 0.0 copy-start.4
  54.6 0.0 copy-start.5
  54.6 0.1 shard_map.150
  54.7 15.9 %all_to_all.25.got_ref = bf16[8,208,128]{2,1,0:T(8,128)(2,1)S(1)} all-to-all(bf16[8,208,128]{2,1,0:T(8,128)(2,1)S(1)} %shard_map.150), channel_id=1, replica_groups=mesh['sec'=4,'yh'=2,'z'=12,'core'=2,'mp'=4] {'sec','yh'}, dimensions={0} | all-to-all | bytes 851968 | tf_op jit(solution)/shard_map/all_to_all | solution.py:411
  70.6 0.2 shard_map.151
  70.8 24.8 %all_to_all.26.got_ref = bf16[12,32,128]{2,1,0:T(8,128)(2,1)S(1)} all-to-all(bf16[12,32,128]{2,1,0:T(8,128)(2,1)S(1)} %shard_map.151), channel_id=1, replica_groups=mesh['sec'=4,'yh'=2,'z'=12,'core'=2,'mp'=4] {'z'}, dimensions={0} | all-to-all | bytes 196608 | tf_op jit(solution)/shard_map/all_to_all | solution.py:411
  95.5 0.1 shard_map.152
  95.7 11.9 %all_to_all.27 = bf16[12,8,128]{2,1,0:T(8,128)(2,1)S(1)} all-to-all(bf16[12,8,128]{2,1,0:T(8,128)(2,1)S(1)} %get-tuple-element.40), channel_id=1, replica_groups=mesh['sec'=4,'yh'=2,'z'=12,'core'=2,'mp'=4] {'z'}, dimensions={0} | all-to-all | bytes 49152 | tf_op jit(solution)/shard_map/all_to_all | solution.py:411
  107.6 13.6 %all_to_all.28 = bf16[8,96,128]{2,1,0:T(8,128)(2,1)S(1)} all-to-all(bf16[8,96,128]{2,1,0:T(8,128)(2,1)S(1)} %broadcast_in_dim.12), channel_id=1, replica_groups=mesh['sec'=4,'yh'=2,'z'=12,'core'=2,'mp'=4] {'sec','yh'}, dimensions={0} | all-to-all | bytes 393216 | tf_op jit(solution)/shard_map/all_to_all | solution.py:411
  121.1 6.7 %collective-permute-start.6 = (bf16[12,64,128]{2,1,0:T(8,128)(2,1)S(1)}, bf16[12,64,128]{2,1,0:T(8,128)(2,1)S(1)}, u32[]{:S(2)}, u32[]{:S(2)}) collective-permute-start(bf16[12,64,128]{2,1,0:T(8,128)(2,1)S(1)} %bitcast.14), channel_id=1, source_target_pairs={{0,4},{4,0},{1,5},{5,1},{2,6},{6,2},{3,7},{7,3},{8,12},{12,8},{9,1... | collective-permute-start | bytes 589832 | tf_op jit(solution)/shard_map/ppermute | solution.py:415
  127.8 0.0 copy-done.1
  127.8 0.0 copy-done.3
  127.8 0.0 copy-done.4
  127.8 0.0 copy-done.5
  127.8 2.0 %shard_map.153 = (f32[1,128]{1,0:T(1,128)}, bf16[128,1024]{1,0:T(8,128)(2,1)}, bf16[2,1,128,256]{3,2,1,0:T(8,128)(2,1)}) custom-call(s32[1]{0:T(128)} %bitcast.sec_ref, s32[4,1,128]{2,1,0:T(1,128)S(1)} %copy-done.6, f32[8,128]{1,0:T(8,128)S(1)} %get-tuple-element.34.moments_ref, f32[8,128]{1,0:T(8,128)S(1)} %get-tuple-element.35.keep_ref, ...), custom_call_target="tpu_custom_call" | custom-call | flops 300000000 | bytes 20000000 | tf_op jit(solution)/shard_map/pallas_call | solution.py:378
  129.8 0.0 collective-permute-done.6.other_ref
  129.8 0.9 shard_map.154
  (1 shorter events, 0.0 us)
Async XLA Ops:
  0.6 9.9 %copy-start.2 = (bf16[1,128,1024]{2,1,0:T(8,128)(2,1)S(1)}, bf16[1,128,1024]{2,1,0:T(8,128)(2,1)}, u32[]{:S(2)}) copy-start(bf16[1,128,1024]{2,1,0:T(8,128)(2,1)} %param.13) | copy-start | bytes 786436
  4.5 16.7 %collective-permute-start.2 = (bf16[128,1024]{1,0:T(8,128)(2,1)S(1)}, bf16[128,1024]{1,0:T(8,128)(2,1)S(1)}, u32[]{:S(2)}, u32[]{:S(2)}) collective-permute-start(bf16[128,1024]{1,0:T(8,128)(2,1)S(1)} %get-tuple-element.25.after_ref), channel_id=1, source_target_pairs={{0,576},{192,0},{1,577},{193,1},{2,578},{194,2},{3,579},{195,3},{4... | collective-permute-start | bytes 786440 | tf_op jit(solution)/shard_map/ppermute | solution.py:464
  10.5 10.7 %collective-permute-start = (bf16[128,1024]{1,0:T(8,128)(2,1)S(1)}, bf16[128,1024]{1,0:T(8,128)(2,1)S(1)}, u32[]{:S(2)}, u32[]{:S(2)}) collective-permute-start(bf16[128,1024]{1,0:T(8,128)(2,1)S(1)} %bitcast.19), channel_id=1, source_target_pairs={{192,0},{384,192},{193,1},{385,193},{194,2},{386,194},{195,3},{387... | collective-permute-start | bytes 786440 | tf_op jit(solution)/shard_map/ppermute | solution.py:438
  11.8 11.0 %collective-permute-start.1 = (bf16[128,1024]{1,0:T(8,128)(2,1)S(1)}, bf16[128,1024]{1,0:T(8,128)(2,1)S(1)}, u32[]{:S(2)}, u32[]{:S(2)}) collective-permute-start(bf16[128,1024]{1,0:T(8,128)(2,1)S(1)} %bitcast.20), channel_id=1, source_target_pairs={{384,0},{576,192},{385,1},{577,193},{386,2},{578,194},{387,3},{579... | collective-permute-start | bytes 786440 | tf_op jit(solution)/shard_map/ppermute | solution.py:439
  15.7 28.8 %copy-start = (bf16[1,128,2048]{2,1,0:T(8,128)(2,1)S(1)}, bf16[1,128,2048]{2,1,0:T(8,128)(2,1)}, u32[]{:S(2)}) copy-start(bf16[1,128,2048]{2,1,0:T(8,128)(2,1)} %param.14) | copy-start | bytes 1572868
  15.7 28.8 %copy-start.6 = (s32[4,1,128]{2,1,0:T(1,128)S(1)}, s32[4,1,128]{2,1,0:T(1,128)}, u32[]{:S(2)}) copy-start(s32[4,1,128]{2,1,0:T(1,128)} %doc_ref.7) | copy-start | bytes 6148
  15.7 28.8 %copy-start.7 = (s32[4,1,4]{2,1,0:T(1,128)S(1)}, s32[4,1,4]{2,1,0:T(1,128)}, u32[]{:S(2)}) copy-start(s32[4,1,4]{2,1,0:T(1,128)} %param.21) | copy-start | bytes 196
  15.7 5.5 %collective-permute-start.3 = (f32[136,128]{1,0:T(8,128)S(1)}, f32[136,128]{1,0:T(8,128)S(1)}, u32[]{:S(2)}, u32[]{:S(2)}) collective-permute-start(f32[136,128]{1,0:T(8,128)S(1)} %get-tuple-element.28.part_ref), channel_id=1, source_target_pairs={{0,1},{1,0},{2,3},{3,2},{4,5},{5,4},{6,7},{7,6},{8,9},{9,8},{10,11... | collective-permute-start | bytes 208904 | tf_op jit(solution)/shard_map/ppermute | solution.py:478
  23.8 20.6 %collective-permute-start.4 = (f32[136,128]{1,0:T(8,128)S(1)}, f32[136,128]{1,0:T(8,128)S(1)}, u32[]{:S(2)}, u32[]{:S(2)}) collective-permute-start(f32[136,128]{1,0:T(8,128)S(1)} %get-tuple-element.31.near_ref), channel_id=1, source_target_pairs={{0,3},{3,0},{1,2},{2,1},{4,7},{7,4},{5,6},{6,5},{8,11},{11,8},{9,1... | collective-permute-start | bytes 208904 | tf_op jit(solution)/shard_map/ppermute | solution.py:484
  34.0 10.5 %all-to-all-start = ((f32[16,4,128]{2,1,0:T(4,128)}), f32[16,4,128]{2,1,0:T(4,128)S(1)}, u32[]{:S(2)}, u32[]{:S(2)}) async-start(f32[16,4,128]{2,1,0:T(4,128)} %get-tuple-element.29), calls=%async_computation | async-start | bytes 65536 | tf_op jit(solution)/shard_map/all_to_all | solution.py:411
  46.0 8.5 %collective-permute-start.5 = (f32[1544,128]{1,0:T(8,128)S(1)}, f32[1544,128]{1,0:T(8,128)S(1)}, u32[]{:S(2)}, u32[]{:S(2)}) collective-permute-start(f32[1544,128]{1,0:T(8,128)S(1)} %get-tuple-element.33), channel_id=1, source_target_pairs={{0,4},{4,0},{1,5},{5,1},{2,6},{6,2},{3,7},{7,3},{8,12},{12,8},{9,1... | collective-permute-start | bytes 2371592 | tf_op jit(solution)/shard_map/ppermute | solution.py:415
  54.6 73.3 %copy-start.1 = (bf16[1,128,1024]{2,1,0:T(8,128)(2,1)S(1)}, bf16[1,128,1024]{2,1,0:T(8,128)(2,1)}, u32[]{:S(2)}) copy-start(bf16[1,128,1024]{2,1,0:T(8,128)(2,1)} %param.11) | copy-start | bytes 786436
  54.6 73.3 %copy-start.3 = (bf16[1,128,1024]{2,1,0:T(8,128)(2,1)S(1)}, bf16[1,128,1024]{2,1,0:T(8,128)(2,1)}, u32[]{:S(2)}) copy-start(bf16[1,128,1024]{2,1,0:T(8,128)(2,1)} %param.13) | copy-start | bytes 786436
  54.6 73.3 %copy-start.4 = (bf16[2,1,128,256]{3,2,1,0:T(8,128)(2,1)S(1)}, bf16[2,1,128,256]{3,2,1,0:T(8,128)(2,1)}, u32[]{:S(2)}) copy-start(bf16[2,1,128,256]{3,2,1,0:T(8,128)(2,1)} %memory_ref.3) | copy-start | bytes 393220
  54.6 73.3 %copy-start.5 = (bf16[1024,64]{0,1:T(8,128)(2,1)S(1)}, bf16[1024,64]{0,1:T(8,128)(2,1)}, u32[]{:S(2)}) copy-start(bf16[1024,64]{0,1:T(8,128)(2,1)} %param.15) | copy-start | bytes 393220
  121.1 8.7 %collective-permute-start.6 = (bf16[12,64,128]{2,1,0:T(8,128)(2,1)S(1)}, bf16[12,64,128]{2,1,0:T(8,128)(2,1)S(1)}, u32[]{:S(2)}, u32[]{:S(2)}) collective-permute-start(bf16[12,64,128]{2,1,0:T(8,128)(2,1)S(1)} %bitcast.14), channel_id=1, source_target_pairs={{0,4},{4,0},{1,5},{5,1},{2,6},{6,2},{3,7},{7,3},{8,12},{12,8},{9,1... | collective-permute-start | bytes 589832 | tf_op jit(solution)/shard_map/ppermute | solution.py:415
